TPU v7x, 256 devices: a whole 4x4x8 slice. The times are simulated.
256 devices in a mesh: leaf: 16 (over y, x), sep: 8 (over z), mode: 2 (over core).
Axes of the slice: x: 4, y: 4, z: 8, core: 2. Of those that a mesh axis runs over, the one named last changes fastest.
Arguments:
- modes: bfloat16 [1024, 2048, 256], P(('leaf', 'sep'), 'mode'), may hold values from -0.125 to 0.125
- coupling: bfloat16 [1024, 2048, 256], P(('leaf', 'sep'), 'mode'), may hold values from -6 to 6
- eigenvalues: float32 [1024, 256], P(('leaf', 'sep'), 'mode'), may hold values from 200 to 4000
- separator_of: int32 [1024, 1], P(('leaf', 'sep')), may hold values from 0 to 7; in each aligned block of 8 rows (0 to 7, 8 to 15, ...) at most 2 rows name the same one
- row_offset: int32 [1024], P(('leaf', 'sep')), may hold values from 0 to 256
- stiffness: bfloat16 [8, 512, 512], P('sep', None, ('leaf', 'mode')), may hold values from -1 to 40
- start_block: bfloat16 [8, 512, 256], P('sep', ('leaf', 'mode')), may hold values from -40 to 40
- rotations: bfloat16 [8, 2, 256, 256], P('sep'), may hold values from -0.375 to 0.375
Outputs:
- subspace: bfloat16 [8, 512, 256], P('sep', ('leaf', 'mode'))
- column_norms: float32 [8, 2, 256], P('sep')
Inputs may be any that keep to these rules, and one draw needn't show every extreme that they name: `separator_of`: among the 8 leaves of one device at most 2 couple to one separator, and in every draw some separator gets exactly 2 of them.
All inputs are finite; a program needn't handle non-finite values.
Results may differ from a plain program's by a relative error of at most 0.0075.
Values may be sent and summed in bfloat16 or wider, within the bound.
No kernel may reach another device: no remote copies, remote signals or barrier semaphores. Data moves between devices by JAX's collectives and lax.ppermute only.
A program may use at most 64 MiB of HBM per device.

v0:
```python
import jax
import jax.numpy as jnp
from jax import lax
from jax.sharding import PartitionSpec as P

SEP_ROWS = 512
CAP = 2
ITERS = 2


epsilon = 1e-06


def leaf_projection(modes, coupling, eigenvalues):
    summed = lax.psum_scatter(
        jnp.einsum("ldm,ldw->mlw", modes, coupling, preferred_element_type=jnp.float32),
        "mode",
        scatter_dimension=0,
        tiled=True,
    )
    return (summed / jnp.sqrt(eigenvalues.T)[:, :, None]).astype(jnp.bfloat16)


def route_blocks(scaled, separator_of, row_offset):
    groups = lax.axis_size("sep")
    leaves = scaled.shape[1]
    target = separator_of[:, 0]
    leaf_order = jnp.arange(leaves)
    earlier = (target[:, None] == target[None, :]) & (leaf_order[None, :] < leaf_order[:, None])
    position = jnp.sum(earlier.astype(jnp.int32), 1)
    slot_of = target * CAP + position
    slot_table = slot_of[None, :] == jnp.arange(groups * CAP)[:, None]
    send_blocks = jnp.einsum(
        "sl,mlw->smw", slot_table.astype(jnp.bfloat16), scaled, preferred_element_type=jnp.float32
    ).astype(jnp.bfloat16)
    send_offsets = jnp.sum(jnp.where(slot_table, row_offset[None, :], 0), 1)
    block_shape = (groups, CAP, send_blocks.shape[1], send_blocks.shape[2])
    got_blocks, got_offsets = (
        lax.all_to_all(
            send_blocks.reshape(block_shape), "sep", split_axis=0, concat_axis=0, tiled=True
        ),
        lax.all_to_all(
            send_offsets.reshape(groups, CAP), "sep", split_axis=0, concat_axis=0, tiled=True
        ),
    )
    return (
        got_blocks.reshape(groups * CAP, block_shape[2], block_shape[3]),
        got_offsets.reshape(groups * CAP),
    )


def coupled_correction(full_block, blocks, offsets):
    width_rows = blocks.shape[2]

    def add_slot(slot_index, accumulated):
        offset = offsets[slot_index]
        weights = blocks[slot_index]
        window = lax.dynamic_slice_in_dim(full_block, offset, width_rows, 0)
        projected = jnp.dot(weights, window, preferred_element_type=jnp.float32).astype(
            jnp.bfloat16
        )
        update = jnp.einsum("mw,mc->wc", weights, projected, preferred_element_type=jnp.float32)
        current = lax.dynamic_slice_in_dim(accumulated, offset, width_rows, 0)
        return lax.dynamic_update_slice_in_dim(accumulated, current + update, offset, 0)

    initial = jnp.zeros(full_block.shape, jnp.float32)
    return lax.fori_loop(0, blocks.shape[0], add_slot, initial)


def gather_rows(own_block):
    return lax.all_gather(own_block, ("leaf", "mode"), axis=0, tiled=True)


def per_device(
    modes, coupling, eigenvalues, separator_of, row_offset, stiffness, start_block, rotations
):
    scaled = leaf_projection(modes, coupling, eigenvalues)
    blocks, offsets = route_blocks(scaled, separator_of, row_offset)
    stiff_columns = stiffness[0]
    own_block = start_block[0]
    ritz_turns = rotations[0]
    own_rows = own_block.shape[0]
    norm_list = []
    for iteration in range(ITERS):
        full_block = gather_rows(own_block)
        correction = coupled_correction(full_block, blocks, offsets)

        def assemble_rows(first_row, row_count, block_now=own_block, correction_now=correction):
            product = jnp.dot(stiff_columns, block_now, preferred_element_type=jnp.float32)
            return product - correction_now

        summed = lax.psum_scatter(
            assemble_rows(jnp.int32(0), lax.axis_size(("leaf", "mode")) * own_rows),
            ("leaf", "mode"),
            scatter_dimension=0,
            tiled=True,
        )
        squares = lax.psum(jnp.sum(summed * summed, 0), ("leaf", "mode"))
        column_scale = jnp.sqrt(squares / SEP_ROWS + epsilon)
        normed = (summed / column_scale).astype(jnp.bfloat16)
        own_block = jnp.dot(
            normed, ritz_turns[iteration], preferred_element_type=jnp.float32
        ).astype(jnp.bfloat16)
        norm_list.append(column_scale)
    return (own_block[None], jnp.stack(norm_list)[None])


def solution(mesh):
    in_specs = (
        P(("leaf", "sep"), "mode", None),
        P(("leaf", "sep"), "mode", None),
        P(("leaf", "sep"), "mode"),
        P(("leaf", "sep"), None),
        P(("leaf", "sep")),
        P("sep", None, ("leaf", "mode")),
        P("sep", ("leaf", "mode"), None),
        P("sep", None, None, None),
    )
    out_specs = (P("sep", ("leaf", "mode"), None), P("sep", None, None))
    return jax.shard_map(
        per_device, mesh=mesh, in_specs=in_specs, out_specs=out_specs, check_vma=False
    )
```

profile of v0, /device:TPU:1, one launch (start us, length us, event | category | flops | bytes accessed | tf_op | source)
XLA Modules:
  0.0 563.1 jit_solution(13401757239637969915)
XLA Ops:
  7.3 6.2 %convolution_bitcast_fusion = f32[256,8,256]{0,2,1:T(8,128)} fusion(bf16[8,1024,256]{2,1,0:T(8,128)(2,1)} %param.13, bf16[8,1024,256]{2,1,0:T(8,128)(2,1)} %param.12), kind=kOutput, calls=%fused_computation.13 | convolution fusion | flops 1073741824 | bytes 10485760 | tf_op jit(solution)/shard_map/ldm,ldw->mlw/dot_general | solution.py:16
  14.5 9.0 %all-to-all-start = ((s32[8,1,2]{2,1,0:T(1,128)}), s32[8,1,2]{2,1,0:T(1,128)S(1)}, u32[]{:S(2)}, u32[]{:S(2)}) async-start(s32[8,1,2]{2,1,0:T(1,128)} %bitcast.7), calls=%async_computation | async-start | bytes 8192 | tf_op jit(solution)/shard_map/all_to_all | solution.py:42
  23.5 9.3 %reduce-scatter.6.cloned.1.call-done = f32[128,8,256]{0,2,1:T(8,128)} async-done(((f32[256,8,256]{0,2,1:T(8,128)}), f32[128,8,256]{0,2,1:T(8,128)}) %reduce-scatter.6.cloned.1.call-update) | async-done | bytes 1048592 | tf_op jit(solution)/shard_map/reduce_scatter | solution.py:15
  37.3 6.8 %all-to-all-start.1 = ((bf16[8,2,128,256]{3,1,2,0:T(2,128)(2,1)}), bf16[8,2,128,256]{3,1,2,0:T(2,128)(2,1)S(1)}, u32[]{:S(2)}, u32[]{:S(2)}) async-start(bf16[8,2,128,256]{3,1,2,0:T(2,128)(2,1)} %copy.30), calls=%async_computation.2 | async-start | bytes 2097152 | tf_op jit(solution)/shard_map/all_to_all | solution.py:39
  44.2 25.3 %all-gather = bf16[1,512,256]{2,1,0:T(8,128)(2,1)S(1)} all-gather(bf16[1,16,256]{2,1,0:T(8,128)(2,1)S(1)} %copy-done.1), channel_id=2, replica_groups=mesh['leaf'=16,'sep'=8,'mode'=2] {'leaf','mode'}, dimensions={1}, use_global_device_ids=true | all-gather | bytes 270336 | tf_op jit(solution)/shard_map/all_gather | solution.py:71
  70.8 2.6 all-to-all-done.1
  73.6 75.1 %while.26 = (s32[]{:T(128)}, f32[512,256]{1,0:T(8,128)S(1)}, s32[16]{0:T(128)S(1)}, bf16[16,128,256]{2,1,0:T(8,128)(2,1)S(1)}, bf16[512,256]{1,0:T(8,128)(2,1)S(1)}, /*index=5*/s32[]{:T(128)}, s32[]{:T(128)}, s32[]{:T(128)}) while((s32[]{:T(128)}, f32[512,256]{1,0:T(8,128)S(1)}, s32[16]{0:T(128)S(1)}, bf16[16,128,256]{2,1,0:T(8,128)(2,1)S(1)}, ...), condition=%wide.region_4.5_spmd, body=%wide.region_3.4_spmd.sunk | while | flops 33652740 | bytes 1312903 | solution.py:67
  81.2 1.9 dynamic_update_slice.16
  90.2 1.9 dynamic_update_slice.16
  95.0 1.9 dynamic_update_slice.16
  99.9 1.9 dynamic_update_slice.16
  108.8 1.9 dynamic_update_slice.16
  149.8 79.8 %reduce-scatter.8.cloned.1.call-done = f32[16,256]{1,0:T(8,128)} async-done(((f32[512,256]{1,0:T(8,128)}), f32[16,256]{1,0:T(8,128)}) %reduce-scatter.8.cloned.1.call-update) | async-done | bytes 16400 | tf_op jit(solution)/shard_map/reduce_scatter | solution.py:92
  230.4 64.5 %psum.14 = f32[256]{0:T(256)S(1)} all-reduce(f32[256]{0:T(256)S(1)} %multiply_reduce_fusion.1), channel_id=1, replica_groups=mesh['leaf'=16,'sep'=8,'mode'=2] {'leaf','mode'}, use_global_device_ids=true, to_apply=%region_7.8 | all-reduce | flops 256 | bytes 2048 | tf_op jit(solution)/shard_map/psum | solution.py:98
  295.8 22.7 %all_gather.7 = bf16[512,256]{1,0:T(8,128)(2,1)S(1)} all-gather(bf16[16,256]{1,0:T(8,128)(2,1)S(1)} %convolution_convert_fusion.4), channel_id=1, replica_groups=mesh['leaf'=16,'sep'=8,'mode'=2] {'leaf','mode'}, dimensions={0}, use_global_device_ids=true | all-gather | bytes 270336 | tf_op jit(solution)/shard_map/all_gather | solution.py:71
  318.5 85.6 %while.27 = (s32[]{:T(128)}, f32[512,256]{0,1:T(8,128)S(1)}, s32[16]{0:T(128)S(1)}, bf16[16,128,256]{2,1,0:T(8,128)(2,1)S(1)}, bf16[512,256]{1,0:T(8,128)(2,1)S(1)}, /*index=5*/s32[]{:T(128)}, s32[]{:T(128)}, s32[]{:T(128)}) while((s32[]{:T(128)}, f32[512,256]{0,1:T(8,128)S(1)}, s32[16]{0:T(128)S(1)}, bf16[16,128,256]{2,1,0:T(8,128)(2,1)S(1)}, ...), condition=%wide.region_9.10_spmd, body=%wide.region_8.9_spmd.sunk | while | flops 33652740 | bytes 2884751 | solution.py:67
  321.8 2.2 dynamic_update_slice.17
  327.4 1.9 dynamic_update_slice.17
  337.9 1.9 dynamic_update_slice.17
  343.2 1.9 dynamic_update_slice.17
  348.5 1.9 dynamic_update_slice.17
  359.0 1.9 dynamic_update_slice.17
  364.2 1.9 dynamic_update_slice.17
  369.5 1.9 dynamic_update_slice.17
  374.8 2.2 dynamic_update_slice.17
  380.4 1.9 dynamic_update_slice.17
  385.7 2.2 dynamic_update_slice.17
  391.3 1.9 dynamic_update_slice.17
  396.6 2.2 dynamic_update_slice.17
  402.2 1.9 dynamic_update_slice.17
  405.4 84.3 %reduce-scatter.10.cloned.1.call-done = f32[16,256]{1,0:T(8,128)} async-done(((f32[512,256]{1,0:T(8,128)}), f32[16,256]{1,0:T(8,128)}) %reduce-scatter.10.cloned.1.call-update) | async-done | bytes 16400
  490.6 64.5 %psum.15 = f32[256]{0:T(256)S(1)} all-reduce(f32[256]{0:T(256)S(1)} %multiply_reduce_fusion), channel_id=1, replica_groups=mesh['leaf'=16,'sep'=8,'mode'=2] {'leaf','mode'}, use_global_device_ids=true, to_apply=%region_12.13 | all-reduce | flops 256 | bytes 2048 | tf_op jit(solution)/shard_map/psum | solution.py:98
  (171 shorter events, 72.9 us)
Async XLA Ops:
  7.2 141.5 %copy-start = (bf16[1,512,16]{1,2,0:T(8,128)(2,1)S(1)}, bf16[1,512,16]{1,2,0:T(8,128)(2,1)}, u32[]{:S(2)}) copy-start(bf16[1,512,16]{1,2,0:T(8,128)(2,1)} %param.17) | copy-start | bytes 49156
  7.2 6.3 %copy-start.4 = (s32[8,1]{0,1:T(1,128)S(1)}, s32[8,1]{0,1:T(1,128)}, u32[]{:S(2)}) copy-start(s32[8,1]{0,1:T(1,128)} %param.15) | copy-start | bytes 100
  7.2 6.5 %copy-start.5 = (s32[8]{0:T(128)S(1)}, s32[8]{0:T(128)}, u32[]{:S(2)}) copy-start(s32[8]{0:T(128)} %param.16) | copy-start | bytes 100
  7.2 16.3 %copy-start.2 = (f32[8,128]{1,0:T(8,128)S(1)}, f32[8,128]{1,0:T(8,128)}, u32[]{:S(2)}) copy-start(f32[8,128]{1,0:T(8,128)} %param.14) | copy-start | bytes 12292
  7.2 25.6 %reduce-scatter.6.cloned.1.call-start = ((), (), s32[]{:S(2)}) async-start(), calls=%async_computation.5 | async-start | bytes 3145728 | tf_op jit(solution)/shard_map/reduce_scatter | solution.py:15
  14.5 22.9 %all-to-all-start = ((s32[8,1,2]{2,1,0:T(1,128)}), s32[8,1,2]{2,1,0:T(1,128)S(1)}, u32[]{:S(2)}, u32[]{:S(2)}) async-start(s32[8,1,2]{2,1,0:T(1,128)} %bitcast.7), calls=%async_computation | async-start | bytes 8192 | tf_op jit(solution)/shard_map/all_to_all | solution.py:42
  34.5 9.6 %copy-start.1 = (bf16[1,16,256]{2,1,0:T(8,128)(2,1)S(1)}, bf16[1,16,256]{2,1,0:T(8,128)(2,1)}, u32[]{:S(2)}) copy-start(bf16[1,16,256]{2,1,0:T(8,128)(2,1)} %param.18) | copy-start | bytes 24580
  37.3 36.0 %all-to-all-start.1 = ((bf16[8,2,128,256]{3,1,2,0:T(2,128)(2,1)}), bf16[8,2,128,256]{3,1,2,0:T(2,128)(2,1)S(1)}, u32[]{:S(2)}, u32[]{:S(2)}) async-start(bf16[8,2,128,256]{3,1,2,0:T(2,128)(2,1)} %copy.30), calls=%async_computation.2 | async-start | bytes 2097152 | tf_op jit(solution)/shard_map/all_to_all | solution.py:39
  44.1 185.5 %reduce-scatter.8.cloned.1.call-start = ((), (), s32[]{:S(2)}) async-start(), calls=%async_computation.6 | async-start | bytes 540672 | tf_op jit(solution)/shard_map/reduce_scatter | solution.py:92
  73.6 221.3 %copy-start.3 = (bf16[1,2,256,256]{3,2,1,0:T(8,128)(2,1)S(1)}, bf16[1,2,256,256]{3,2,1,0:T(8,128)(2,1)}, u32[]{:S(2)}) copy-start(bf16[1,2,256,256]{3,2,1,0:T(8,128)(2,1)} %param.19) | copy-start | bytes 786436
  149.8 339.9 %reduce-scatter.10.cloned.1.call-start = ((), (), s32[]{:S(2)}) async-start(), calls=%async_computation.7 | async-start | bytes 540672
Sparse Core Ops, SparseCore 0:
  13.6 19.1 reduce-scatter.5
  149.9 79.6 reduce-scatter.7
  405.5 84.1 reduce-scatter.9
where the time goes:
time: 563 us
  blocking collectives  177 us (31%)
  waiting for transfers between devices  176 us (31%)
  local copies, waits for them, and re-layouts  91.2 us (16%)
  loops' own time  63.5 us (11%)
  matrix products  21.7 us (4%)
  starting transfers between devices  15.9 us (3%)
  between operations  13.9 us (2%)
    psum x2, blocking collectives, per_device(): squares = lax.psum(jnp.sum(summed * summed, 0), ('leaf', 'mode'))  129 us
    unnamed x4, waiting for transfers between devices  84.4 us
    reduce_scatter x1, waiting for transfers between devices, per_device(): lax.psum_scatter(assemble_rows(jnp.int32(0), lax.axis_size(('leaf', 'mode...  79.8 us
    another operation x2, loops' own time, coupled_correction(): return lax.fori_loop(0, blocks.shape[0], add_slot, initial)  63.5 us
    dynamic_update_slice x48, local copies, waits for them, and re-layouts, add_slot(): lax.dynamic_update_slice_in_dim(accumulated, current + update, offset, 0)  62.2 us
    all_gather x2, blocking collectives, gather_rows(): return lax.all_gather(own_block, ('leaf', 'mode'), axis=0, tiled=True)  48 us
    dynamic_slice x32, local copies, waits for them, and re-layouts, add_slot(): offset = offsets[slot_index]  18.8 us
    dot_general x32, matrix products, add_slot(): jnp.einsum('mw,mc->wc', weights, projected, preferred_element_type=jnp.fl...  11.9 us
  transfers between devices with their start and end apart: 5, of which 4 were waited for; matrix products, arithmetic and copies ran while one was open for 1% of the time, Pallas kernels for 0%

commit v1 on v0

v1 whole, which is shorter than its diff:
```python
import functools

import jax
import jax.numpy as jnp
from jax import lax
from jax.experimental import pallas as pl
from jax.experimental.pallas import tpu as pltpu
from jax.sharding import PartitionSpec as P

SEP_ROWS = 512
IFACE = 256
MODES = 256
COLS = 256
NSEP = 8
LEAF_DEV = 8
PLANE = 16
STRIP = 16
ITERS = 2
epsilon = 1e-06


def gram_kernel(target_ref, offset_ref, core_ref, own_ref, other_ref, eigen_ref, out_ref, acc_ref, pad_ref):
    leaf = pl.program_id(0)

    @pl.when(leaf == 0)
    def _():
        acc_ref[...] = jnp.zeros_like(acc_ref)

    inverse = 1.0 / jnp.sqrt(eigen_ref[0])
    scaled = ((own_ref[0] + other_ref[0]) * inverse).astype(jnp.bfloat16)
    row = lax.broadcasted_iota(jnp.int32, (SEP_ROWS, IFACE), 0)
    column = lax.broadcasted_iota(jnp.int32, (SEP_ROWS, IFACE), 1)
    placing = (row - column == offset_ref[leaf]).astype(jnp.bfloat16)
    full = jnp.dot(placing, scaled, preferred_element_type=jnp.float32).astype(jnp.bfloat16)
    pad_ref[...] = full
    core = core_ref[0]
    strips = [
        pad_ref[pl.ds(pl.multiple_of(32 * g + 16 * core, STRIP), STRIP), :] for g in range(PLANE)
    ]
    rows = jnp.concatenate(strips, axis=0)
    product = lax.dot_general(
        rows, full, (((1,), (1,)), ((), ())), preferred_element_type=jnp.float32
    )
    target = target_ref[leaf]
    acc_ref[target] = acc_ref[target] + product

    @pl.when(leaf == pl.num_programs(0) - 1)
    def _():
        for s in range(NSEP):
            for g in range(PLANE):
                out_ref[g, s] = acc_ref[s, g * STRIP : (g + 1) * STRIP, :].astype(jnp.bfloat16)


def gram(target, offset, core, own, other, eigen):
    grid_spec = pltpu.PrefetchScalarGridSpec(
        num_scalar_prefetch=3,
        grid=(LEAF_DEV,),
        in_specs=[
            pl.BlockSpec((1, IFACE, MODES), lambda l, *_: (l, 0, 0)),
            pl.BlockSpec((1, IFACE, MODES), lambda l, *_: (l, 0, 0)),
            pl.BlockSpec((1, 1, MODES), lambda l, *_: (l, 0, 0)),
        ],
        out_specs=pl.BlockSpec((PLANE, NSEP, STRIP, SEP_ROWS), lambda l, *_: (0, 0, 0, 0)),
        scratch_shapes=[
            pltpu.VMEM((NSEP, SEP_ROWS // 2, SEP_ROWS), jnp.float32),
            pltpu.VMEM((SEP_ROWS, MODES), jnp.bfloat16),
        ],
    )
    return pl.pallas_call(
        gram_kernel,
        grid_spec=grid_spec,
        out_shape=jax.ShapeDtypeStruct((PLANE, NSEP, STRIP, SEP_ROWS), jnp.bfloat16),
        name="gram",
    )(target, offset, core, own, other, eigen)


def iterate_kernel(place_ref, own_ref, other_ref, turns_ref, out_ref, norms_ref, at_ref, x_ref):
    core = place_ref[0]
    device = place_ref[1]
    for g in range(PLANE):
        first = pl.multiple_of(32 * g + 16 * core, STRIP)
        second = pl.multiple_of(32 * g + 16 * (1 - core), STRIP)
        at_ref[pl.ds(first, STRIP), :] = own_ref[g, :, :SEP_ROWS]
        at_ref[pl.ds(second, STRIP), :] = other_ref[g, :, :SEP_ROWS]
        x_ref[pl.ds(first, STRIP), :] = own_ref[g, :, SEP_ROWS:]
        x_ref[pl.ds(second, STRIP), :] = other_ref[g, :, SEP_ROWS:]
    for step in range(ITERS):
        summed = lax.dot_general(
            at_ref[...], x_ref[...], (((0,), (0,)), ((), ())), preferred_element_type=jnp.float32
        )
        scale = jnp.sqrt(jnp.sum(summed * summed, 0, keepdims=True) / SEP_ROWS + epsilon)
        norms_ref[0, pl.ds(step, 1), :] = scale
        normed = (summed / scale).astype(jnp.bfloat16)
        if step < ITERS - 1:
            x_ref[...] = jnp.dot(
                normed, turns_ref[step], preferred_element_type=jnp.float32
            ).astype(jnp.bfloat16)
        else:
            x_ref[...] = normed
            rows = x_ref[pl.ds(pl.multiple_of(16 * device, STRIP), STRIP), :]
            out_ref[0] = jnp.dot(
                rows, turns_ref[step], preferred_element_type=jnp.float32
            ).astype(jnp.bfloat16)


def iterate(place, own, other, turns):
    vmem = pl.BlockSpec(memory_space=pltpu.VMEM)
    return pl.pallas_call(
        iterate_kernel,
        in_specs=[pl.BlockSpec(memory_space=pltpu.SMEM), vmem, vmem, vmem],
        out_specs=[vmem, vmem],
        out_shape=[
            jax.ShapeDtypeStruct((1, STRIP, COLS), jnp.bfloat16),
            jax.ShapeDtypeStruct((1, ITERS, COLS), jnp.float32),
        ],
        scratch_shapes=[
            pltpu.VMEM((SEP_ROWS, SEP_ROWS), jnp.bfloat16),
            pltpu.VMEM((SEP_ROWS, COLS), jnp.bfloat16),
        ],
        name="iterate",
    )(place, own, other, turns)


SWAP = [(0, 1), (1, 0)]


def per_device(
    modes, coupling, eigenvalues, separator_of, row_offset, stiffness, start_block, rotations
):
    core = lax.axis_index("mode").astype(jnp.int32)
    device = lax.axis_index(("leaf", "mode")).astype(jnp.int32)
    other_eigen = lax.ppermute(eigenvalues, "mode", SWAP)
    eigen = jnp.where(
        core == 0,
        jnp.concatenate([eigenvalues, other_eigen], 1),
        jnp.concatenate([other_eigen, eigenvalues], 1),
    )
    own = jnp.einsum("ldw,ldm->lwm", coupling, modes, preferred_element_type=jnp.float32)
    other = lax.ppermute(own, "mode", SWAP)
    pieces = gram(
        separator_of[:, 0], row_offset, core[None], own, other, eigen[:, None, :]
    )
    got = lax.all_to_all(pieces, "leaf", split_axis=0, concat_axis=0, tiled=True)
    plane_sum = jnp.sum(got.astype(jnp.float32), 0).astype(jnp.bfloat16)
    got = lax.all_to_all(plane_sum, "sep", split_axis=0, concat_axis=0, tiled=True)
    correction = jnp.sum(got.astype(jnp.float32), 0)
    columns = (stiffness[0].T.astype(jnp.float32) - correction).astype(jnp.bfloat16)
    packed = jnp.concatenate([columns, start_block[0]], 1)
    mine = lax.all_to_all(
        jnp.broadcast_to(packed[None], (PLANE, *packed.shape)),
        "leaf",
        split_axis=0,
        concat_axis=0,
        tiled=True,
    )
    theirs = lax.ppermute(mine, "mode", SWAP)
    return tuple(iterate(jnp.stack([core, device]), mine, theirs, rotations[0]))


def solution(mesh):
    in_specs = (
        P(("leaf", "sep"), "mode", None),
        P(("leaf", "sep"), "mode", None),
        P(("leaf", "sep"), "mode"),
        P(("leaf", "sep"), None),
        P(("leaf", "sep")),
        P("sep", None, ("leaf", "mode")),
        P("sep", ("leaf", "mode"), None),
        P("sep", None, None, None),
    )
    out_specs = (P("sep", ("leaf", "mode"), None), P("sep", None, None))
    return jax.shard_map(
        per_device, mesh=mesh, in_specs=in_specs, out_specs=out_specs, check_vma=False
    )
```

time: 563 us -> 93.2 us (0.17)
  waiting for transfers between devices: 176 us -> 4.55 us
  blocking collectives: 177 us -> 60.3 us
  local copies, waits for them, and re-layouts: 91.2 us -> 0.79 us
  loops' own time: 63.5 us -> 0 us
  matrix products: 21.7 us -> 4.87 us
  between operations: 13.9 us -> 0.71 us
  Pallas kernels: 0 us -> 12.6 us
  starting transfers between devices: 15.9 us -> 7.32 us
    psum x2 -> x0, blocking collectives: 129 us -> none  [per_device(): squares = lax.psum(jnp.sum(summed * summed, 0), ('leaf', 'mode'))]
    reduce_scatter x2 -> x0, waiting for transfers between devices: 89.1 us -> none  [the longest x1 79.8 us: per_device(): lax.psum_scatter(assemble_rows(jnp.int32(0), lax.axis_size(('leaf', 'mode...]
    unnamed x4 -> x0, waiting for transfers between devices: 84.4 us -> none
    another operation x2 -> x0, loops' own time: 63.5 us -> none  [coupled_correction(): return lax.fori_loop(0, blocks.shape[0], add_slot, initial)]
    dynamic_update_slice x48 -> x0, local copies, waits for them, and re-layouts: 62.2 us -> none  [add_slot(): lax.dynamic_update_slice_in_dim(accumulated, current + update, offset, 0)]
    all_to_all x0 -> x3, blocking collectives: none -> 60.3 us  [the longest x1 32.8 us: per_device(): lax.all_to_all(pieces, 'leaf', split_axis=0, concat_axis=0, tiled=True)]
    all_gather x2 -> x0, blocking collectives: 48 us -> none  [gather_rows(): return lax.all_gather(own_block, ('leaf', 'mode'), axis=0, tiled=True)]
    dynamic_slice x64 -> x0, local copies, waits for them, and re-layouts: 23 us -> none  [the longest x32 18.8 us: add_slot(): offset = offsets[slot_index]]
  transfers between devices with their start and end apart: 5 -> 3, of which waited for: 4 -> 2; matrix products, arithmetic and copies ran while one was open for 1% -> 1% of each run, Pallas kernels for 0% -> 0%
where the time goes in v1:
time: 93.2 us; the launch traced here: 92.8 us
  blocking collectives  60.3 us (65%)
  Pallas kernels  12.6 us (14%)
  starting transfers between devices  7.32 us (8%)
  matrix products  4.87 us (5%)
  waiting for transfers between devices  4.55 us (5%)
  other arithmetic  1.65 us (2%)
    all_to_all x1, blocking collectives, per_device(): lax.all_to_all(pieces, 'leaf', split_axis=0, concat_axis=0, tiled=True)  32.8 us
    all_to_all x1, blocking collectives, per_device(): lax.all_to_all(plane_sum, 'sep', split_axis=0, concat_axis=0, tiled=True)  16 us
    all_to_all x1, blocking collectives, per_device(): lax.all_to_all(jnp.broadcast_to(packed[None], (PLANE, *packed.shape)), 'l...  11.5 us
    pallas_call x1, Pallas kernels, gram(): pl.pallas_call(gram_kernel, grid_spec=grid_spec, out_shape=jax.ShapeDtype...  9.5 us
    dot_general x1, matrix products, per_device(): jnp.einsum('ldw,ldm->lwm', coupling, modes, preferred_element_type=jnp.fl...  4.87 us
    ppermute x1, starting transfers between devices, per_device(): theirs = lax.ppermute(mine, 'mode', SWAP)  3.93 us
    ppermute x1, waiting for transfers between devices, per_device(): other_eigen = lax.ppermute(eigenvalues, 'mode', SWAP)  3.81 us
    ppermute x1, starting transfers between devices, per_device(): other = lax.ppermute(own, 'mode', SWAP)  3.29 us
  transfers between devices with their start and end apart: 3, of which 2 were waited for; matrix products, arithmetic and copies ran while one was open for 1% of the time, Pallas kernels for 0%

profile of v1, /device:TPU:1, one launch (start us, length us, event | category | flops | bytes accessed | tf_op | source)
XLA Modules:
  0.0 92.8 jit_solution(10214218351160043381)
XLA Ops:
  0.6 0.0 copy-start.5
  0.6 4.9 %fusion.2.own_ref = f32[8,256,256]{2,1,0:T(8,128)S(1)} fusion(bf16[8,1024,256]{2,1,0:T(8,128)(2,1)} %param.9, bf16[8,1024,256]{2,1,0:T(8,128)(2,1)} %param.8), kind=kOutput, calls=%fused_computation.7 | convolution fusion | flops 1073741824 | bytes 10485760 | tf_op jit(solution)/shard_map/ldw,ldm->lwm/dot_general | solution.py:138
  5.5 0.0 copy-start
  5.5 3.3 %collective-permute-start = (f32[8,256,256]{2,1,0:T(8,128)S(1)}, f32[8,256,256]{2,1,0:T(8,128)}, u32[]{:S(2)}, u32[]{:S(2)}) collective-permute-start(f32[8,256,256]{2,1,0:T(8,128)S(1)} %fusion.2.own_ref), channel_id=1, source_target_pairs={{0,1},{1,0},{2,3},{3,2},{4,5},{5,4},{6,7},{7,6},{8,9},{9,8},{10,11... | collective-permute-start | bytes 6291464 | tf_op jit(solution)/shard_map/ppermute | solution.py:139
  8.8 0.0 copy-done.5
  8.8 0.1 collective-permute-start.1
  8.9 3.8 %collective-permute-done.1 = f32[8,128]{1,0:T(8,128)S(1)} collective-permute-done((f32[8,128]{1,0:T(8,128)S(1)}, f32[8,128]{1,0:T(8,128)S(1)}, u32[]{:S(2)}, u32[]{:S(2)}) %collective-permute-start.1) | collective-permute-done | bytes 4128 | tf_op jit(solution)/shard_map/ppermute | solution.py:132
  12.7 0.6 broadcast_select_fusion.eigen_ref
  13.3 0.0 collective-permute-done.other_ref
  13.3 0.0 copy-done
  13.3 9.5 %gram.1 = bf16[16,8,16,512]{3,2,1,0:T(8,128)(2,1)} custom-call(s32[8]{0:T(128)} %bitcast.22, s32[8]{0:T(128)} %offset_ref.1, s32[1]{0:T(128)} %bitcast.core_ref, f32[8,256,256]{2,1,0:T(8,128)} %copy-done, f32[8,256,256]{2,1,0:T(8,128)} %collective-permute-done.other_ref, f32[8,1,256]{2,1,0:T(1,128)} %broadcast_select_fusion.eigen_ref), custom_call_target="tpu_custom_call" | custom-call | tf_op jit(solution)/shard_map/gram/pallas_call | solution.py:69
  22.8 0.0 copy-start.3
  22.8 0.0 copy-start.4
  22.9 32.8 %all_to_all.15 = bf16[16,8,16,512]{3,2,1,0:T(8,128)(2,1)S(1)} all-to-all(bf16[16,8,16,512]{3,2,1,0:T(8,128)(2,1)} %gram.1), channel_id=1, replica_groups=mesh['leaf'=16,'sep'=8,'mode'=2] {'leaf'}, dimensions={0} | all-to-all | bytes 4194304 | tf_op jit(solution)/shard_map/all_to_all | solution.py:143
  55.6 0.4 reduce_sum.21
  56.0 16.0 %all_to_all.16 = bf16[8,16,512]{2,1,0:T(8,128)(2,1)S(1)} all-to-all(bf16[8,16,512]{2,1,0:T(8,128)(2,1)S(1)} %reduce_sum.21), channel_id=1, replica_groups=mesh['leaf'=16,'sep'=8,'mode'=2] {'sep'}, dimensions={0} | all-to-all | bytes 262144 | tf_op jit(solution)/shard_map/all_to_all | solution.py:145
  72.0 0.0 copy-done.3
  72.1 0.0 copy-done.4
  72.1 11.5 %all_to_all.17.own_ref = bf16[16,16,768]{2,1,0:T(8,128)(2,1)S(1)} all-to-all(bf16[16,16,768]{2,1,0:T(8,128)(2,1)S(1)} %broadcast_in_dim.2), channel_id=1, replica_groups=mesh['leaf'=16,'sep'=8,'mode'=2] {'leaf'}, dimensions={0} | all-to-all | bytes 786432 | tf_op jit(solution)/shard_map/all_to_all | solution.py:149
  83.6 0.0 copy-start.1
  83.6 3.9 %collective-permute-start.2 = (bf16[16,16,768]{2,1,0:T(8,128)(2,1)S(1)}, bf16[16,16,768]{2,1,0:T(8,128)(2,1)S(1)}, u32[]{:S(2)}, u32[]{:S(2)}) collective-permute-start(bf16[16,16,768]{2,1,0:T(8,128)(2,1)S(1)} %all_to_all.17.own_ref), channel_id=1, source_target_pairs={{0,1},{1,0},{2,3},{3,2},{4,5},{5,4},{6,7},{7,6},{8,9},{9,8},{10,11... | collective-permute-start | bytes 1179656 | tf_op jit(solution)/shard_map/ppermute | solution.py:156
  87.6 0.6 pad_add_fusion.place_ref
  88.2 0.7 collective-permute-done.2.other_ref
  88.9 0.0 copy-start.2
  88.9 0.0 copy-done.1
  88.9 0.7 copy-done.2
  89.7 3.1 %iterate.1 = (bf16[1,16,256]{2,1,0:T(8,128)(2,1)}, f32[1,2,256]{2,1,0:T(2,128)}) custom-call(s32[2]{0:T(128)} %pad_add_fusion.place_ref, bf16[16,16,768]{2,1,0:T(8,128)(2,1)} %copy-done.1, bf16[16,16,768]{2,1,0:T(8,128)(2,1)} %copy-done.2, bf16[2,256,256]{2,1,0:T(8,128)(2,1)} %bitcast.18), custom_call_target="tpu_custom_call" | custom-call | tf_op jit(solution)/shard_map/iterate/pallas_call | solution.py:108
  (4 shorter events, 0.1 us)
Async XLA Ops:
  0.6 8.2 %copy-start.5 = (f32[8,128]{1,0:T(8,128)S(1)}, f32[8,128]{1,0:T(8,128)}, u32[]{:S(2)}) copy-start(f32[8,128]{1,0:T(8,128)} %param.10) | copy-start | bytes 12292
  5.5 7.8 %copy-start = (f32[8,256,256]{2,1,0:T(8,128)}, f32[8,256,256]{2,1,0:T(8,128)S(1)}, u32[]{:S(2)}) copy-start(f32[8,256,256]{2,1,0:T(8,128)S(1)} %fusion.2.own_ref) | copy-start | bytes 6291460
  5.5 7.8 %collective-permute-start = (f32[8,256,256]{2,1,0:T(8,128)S(1)}, f32[8,256,256]{2,1,0:T(8,128)}, u32[]{:S(2)}, u32[]{:S(2)}) collective-permute-start(f32[8,256,256]{2,1,0:T(8,128)S(1)} %fusion.2.own_ref), channel_id=1, source_target_pairs={{0,1},{1,0},{2,3},{3,2},{4,5},{5,4},{6,7},{7,6},{8,9},{9,8},{10,11... | collective-permute-start | bytes 6291464 | tf_op jit(solution)/shard_map/ppermute | solution.py:139
  8.8 3.9 %collective-permute-start.1 = (f32[8,128]{1,0:T(8,128)S(1)}, f32[8,128]{1,0:T(8,128)S(1)}, u32[]{:S(2)}, u32[]{:S(2)}) collective-permute-start(f32[8,128]{1,0:T(8,128)S(1)} %copy-done.5), channel_id=1, source_target_pairs={{0,1},{1,0},{2,3},{3,2},{4,5},{5,4},{6,7},{7,6},{8,9},{9,8},{10,11... | collective-permute-start | bytes 12296 | tf_op jit(solution)/shard_map/ppermute | solution.py:132
  22.8 49.2 %copy-start.3 = (bf16[1,512,16]{1,2,0:T(8,128)(2,1)S(1)}, bf16[1,512,16]{1,2,0:T(8,128)(2,1)}, u32[]{:S(2)}) copy-start(bf16[1,512,16]{1,2,0:T(8,128)(2,1)} %param.13) | copy-start | bytes 49156
  22.8 49.2 %copy-start.4 = (bf16[1,16,256]{2,1,0:T(8,128)(2,1)S(1)}, bf16[1,16,256]{2,1,0:T(8,128)(2,1)}, u32[]{:S(2)}) copy-start(bf16[1,16,256]{2,1,0:T(8,128)(2,1)} %param.14) | copy-start | bytes 24580
  83.6 5.3 %copy-start.1 = (bf16[16,16,768]{2,1,0:T(8,128)(2,1)}, bf16[16,16,768]{2,1,0:T(8,128)(2,1)S(1)}, u32[]{:S(2)}) copy-start(bf16[16,16,768]{2,1,0:T(8,128)(2,1)S(1)} %all_to_all.17.own_ref) | copy-start | bytes 1179652
  83.6 5.3 %collective-permute-start.2 = (bf16[16,16,768]{2,1,0:T(8,128)(2,1)S(1)}, bf16[16,16,768]{2,1,0:T(8,128)(2,1)S(1)}, u32[]{:S(2)}, u32[]{:S(2)}) collective-permute-start(bf16[16,16,768]{2,1,0:T(8,128)(2,1)S(1)} %all_to_all.17.own_ref), channel_id=1, source_target_pairs={{0,1},{1,0},{2,3},{3,2},{4,5},{5,4},{6,7},{7,6},{8,9},{9,8},{10,11... | collective-permute-start | bytes 1179656 | tf_op jit(solution)/shard_map/ppermute | solution.py:156
  88.9 0.7 copy-start.2

commit v2 on v1

--- a/solution.py
+++ b/solution.py
@@ -14,64 +14,92 @@
 NSEP = 8
 LEAF_DEV = 8
 PLANE = 16
+SIDE = 4
+GROUPS = 8
 STRIP = 16
 ITERS = 2
 epsilon = 1e-06
 
 
-def gram_kernel(target_ref, offset_ref, core_ref, own_ref, other_ref, eigen_ref, out_ref, acc_ref, pad_ref):
-    leaf = pl.program_id(0)
-
-    @pl.when(leaf == 0)
-    def _():
-        acc_ref[...] = jnp.zeros_like(acc_ref)
-
-    inverse = 1.0 / jnp.sqrt(eigen_ref[0])
-    scaled = ((own_ref[0] + other_ref[0]) * inverse).astype(jnp.bfloat16)
+def place_of(d, e, first, second, core):
+    one = (first + d) & (SIDE - 1)
+    two = (second + e) & (SIDE - 1)
+    return jnp.where(core == 0, two * SIDE + one, one * SIDE + two)
+
+
+def gram_kernel(target_ref, offset_ref, place_ref, own_ref, other_ref, eigen_ref, *refs):
+    out_refs, pad_ref = refs[:SIDE], refs[SIDE]
+    core, first, second = place_ref[0], place_ref[1], place_ref[2]
     row = lax.broadcasted_iota(jnp.int32, (SEP_ROWS, IFACE), 0)
     column = lax.broadcasted_iota(jnp.int32, (SEP_ROWS, IFACE), 1)
-    placing = (row - column == offset_ref[leaf]).astype(jnp.bfloat16)
-    full = jnp.dot(placing, scaled, preferred_element_type=jnp.float32).astype(jnp.bfloat16)
-    pad_ref[...] = full
-    core = core_ref[0]
-    strips = [
-        pad_ref[pl.ds(pl.multiple_of(32 * g + 16 * core, STRIP), STRIP), :] for g in range(PLANE)
+    distance = row - column
+    pad_ref[LEAF_DEV] = jnp.zeros((SEP_ROWS, MODES), jnp.bfloat16)
+    for leaf in range(LEAF_DEV):
+        inverse = 1.0 / jnp.sqrt(eigen_ref[leaf : leaf + 1, :])
+        scaled = ((own_ref[leaf] + other_ref[leaf]) * inverse).astype(jnp.bfloat16)
+        placing = (distance == offset_ref[leaf]).astype(jnp.bfloat16)
+        pad_ref[leaf] = jnp.dot(placing, scaled, preferred_element_type=jnp.float32).astype(
+            jnp.bfloat16
+        )
+    starts = [
+        pl.multiple_of(32 * place_of(d, e, first, second, core) + 16 * core, STRIP)
+        for d in range(SIDE)
+        for e in range(SIDE)
     ]
-    rows = jnp.concatenate(strips, axis=0)
-    product = lax.dot_general(
-        rows, full, (((1,), (1,)), ((), ())), preferred_element_type=jnp.float32
-    )
-    target = target_ref[leaf]
-    acc_ref[target] = acc_ref[target] + product
-
-    @pl.when(leaf == pl.num_programs(0) - 1)
-    def _():
-        for s in range(NSEP):
-            for g in range(PLANE):
-                out_ref[g, s] = acc_ref[s, g * STRIP : (g + 1) * STRIP, :].astype(jnp.bfloat16)
-
-
-def gram(target, offset, core, own, other, eigen):
-    grid_spec = pltpu.PrefetchScalarGridSpec(
-        num_scalar_prefetch=3,
-        grid=(LEAF_DEV,),
-        in_specs=[
-            pl.BlockSpec((1, IFACE, MODES), lambda l, *_: (l, 0, 0)),
-            pl.BlockSpec((1, IFACE, MODES), lambda l, *_: (l, 0, 0)),
-            pl.BlockSpec((1, 1, MODES), lambda l, *_: (l, 0, 0)),
-        ],
-        out_specs=pl.BlockSpec((PLANE, NSEP, STRIP, SEP_ROWS), lambda l, *_: (0, 0, 0, 0)),
-        scratch_shapes=[
-            pltpu.VMEM((NSEP, SEP_ROWS // 2, SEP_ROWS), jnp.float32),
-            pltpu.VMEM((SEP_ROWS, MODES), jnp.bfloat16),
-        ],
-    )
+    for s in range(NSEP):
+        slots = [jnp.int32(LEAF_DEV), jnp.int32(LEAF_DEV)]
+        for leaf in range(LEAF_DEV):
+            hit = target_ref[leaf] == s
+            later = hit & (slots[0] < LEAF_DEV)
+            slots[1] = jnp.where(later, leaf, slots[1])
+            slots[0] = jnp.where(hit & jnp.logical_not(later), leaf, slots[0])
+        total = None
+        for slot in slots:
+            rows = jnp.concatenate([pad_ref[slot, pl.ds(x, STRIP), :] for x in starts], axis=0)
+            product = lax.dot_general(
+                rows, pad_ref[slot], (((1,), (1,)), ((), ())), preferred_element_type=jnp.float32
+            )
+            total = product if total is None else total + product
+        total = total.astype(jnp.bfloat16)
+        for d in range(SIDE):
+            for e in range(SIDE):
+                k = (d * SIDE + e) * STRIP
+                out_refs[d][e, s] = total[k : k + STRIP, :]
+
+
+VMEM = pl.BlockSpec(memory_space=pltpu.VMEM)
+SMEM = pl.BlockSpec(memory_space=pltpu.SMEM)
+
+
+def gram(target, offset, place, own, other, eigen):
+    piece = jax.ShapeDtypeStruct((SIDE, NSEP, STRIP, SEP_ROWS), jnp.bfloat16)
     return pl.pallas_call(
         gram_kernel,
-        grid_spec=grid_spec,
-        out_shape=jax.ShapeDtypeStruct((PLANE, NSEP, STRIP, SEP_ROWS), jnp.bfloat16),
+        in_specs=[SMEM, SMEM, SMEM, VMEM, VMEM, VMEM],
+        out_specs=[VMEM] * SIDE,
+        out_shape=[piece] * SIDE,
+        scratch_shapes=[pltpu.VMEM((LEAF_DEV + 1, SEP_ROWS, MODES), jnp.bfloat16)],
         name="gram",
-    )(target, offset, core, own, other, eigen)
+    )(target, offset, place, own, other, eigen)
+
+
+def total_kernel(count, *refs):
+    sources, outs = refs[:count], refs[count:]
+    for k, out_ref in enumerate(outs):
+        for s in range(NSEP):
+            value = sum(ref[k, s].astype(jnp.float32) for ref in sources)
+            out_ref[s] = value.astype(jnp.bfloat16)
+
+
+def total(pieces):
+    lead = pieces[0].shape[0]
+    return pl.pallas_call(
+        functools.partial(total_kernel, len(pieces)),
+        in_specs=[VMEM] * len(pieces),
+        out_specs=[VMEM] * lead,
+        out_shape=[jax.ShapeDtypeStruct(pieces[0].shape[1:], jnp.bfloat16)] * lead,
+        name="total",
+    )(*pieces)
 
 
 def iterate_kernel(place_ref, own_ref, other_ref, turns_ref, out_ref, norms_ref, at_ref, x_ref):
@@ -122,6 +150,28 @@
 
 
 SWAP = [(0, 1), (1, 0)]
+AXES = ("leaf", "sep", "mode")
+
+
+def index_of(y, x, z, core):
+    return ((y * SIDE + x) * GROUPS + z) * 2 + core
+
+
+def plane_steps(step, stage):
+    pairs = []
+    for y in range(SIDE):
+        for x in range(SIDE):
+            for z in range(GROUPS):
+                for core in range(2):
+                    along_x = (core + stage) % 2 == 0
+                    to = (y, (x + step) % SIDE) if along_x else ((y + step) % SIDE, x)
+                    pairs.append((index_of(y, x, z, core), index_of(*to, z, core)))
+    return pairs
+
+
+def scatter_stage(pieces, stage):
+    got = [lax.ppermute(pieces[d], AXES, plane_steps(d, stage)) for d in range(1, SIDE)]
+    return [pieces[0], *got]
 
 
 def per_device(
@@ -137,11 +187,13 @@
     )
     own = jnp.einsum("ldw,ldm->lwm", coupling, modes, preferred_element_type=jnp.float32)
     other = lax.ppermute(own, "mode", SWAP)
-    pieces = gram(
-        separator_of[:, 0], row_offset, core[None], own, other, eigen[:, None, :]
-    )
-    got = lax.all_to_all(pieces, "leaf", split_axis=0, concat_axis=0, tiled=True)
-    plane_sum = jnp.sum(got.astype(jnp.float32), 0).astype(jnp.bfloat16)
+    leaf = lax.axis_index("leaf").astype(jnp.int32)
+    y, x = leaf >> 2, leaf & 3
+    place = jnp.stack([core, jnp.where(core == 0, x, y), jnp.where(core == 0, y, x)])
+    pieces = gram(separator_of[:, 0], row_offset, place, own, other, eigen)
+    pieces = total(scatter_stage(pieces, 0))
+    pieces = [piece[None] for piece in pieces]
+    (plane_sum,) = total(scatter_stage(pieces, 1))
     got = lax.all_to_all(plane_sum, "sep", split_axis=0, concat_axis=0, tiled=True)
     correction = jnp.sum(got.astype(jnp.float32), 0)
     columns = (stiffness[0].T.astype(jnp.float32) - correction).astype(jnp.bfloat16)

time: 93.2 us -> 88.9 us (0.954)
  blocking collectives: 60.3 us -> 29.2 us
  waiting for transfers between devices: 4.55 us -> 20.5 us
  starting transfers between devices: 7.32 us -> 16.2 us
  local copies, waits for them, and re-layouts: 0.79 us -> 2.26 us
    all_to_all x1 -> x0, blocking collectives: 32.8 us -> none  [per_device(): lax.all_to_all(pieces, 'leaf', split_axis=0, concat_axis=0, tiled=True)]
    ppermute x0 -> x6, waiting for transfers between devices: none -> 16.6 us  [scatter_stage(): lax.ppermute(pieces[d], AXES, plane_steps(d, stage))]
    ppermute x0 -> x6, starting transfers between devices: none -> 6.9 us  [scatter_stage(): lax.ppermute(pieces[d], AXES, plane_steps(d, stage))]
    all_to_all x1, blocking collectives: 11.5 us -> 14 us  [per_device(): lax.all_to_all(jnp.broadcast_to(packed[None], (PLANE, *packed.shape)), 'l...]
    ppermute x1, starting transfers between devices: 3.93 us -> 5.89 us  [per_device(): theirs = lax.ppermute(mine, 'mode', SWAP)]
    unnamed x12 -> x24, local copies, waits for them, and re-layouts: 0.76 us -> 2.23 us
    pallas_call x1 -> x3, Pallas kernels: 9.5 us -> 9.88 us  [the longest x1 5.63 us: gram(): pl.pallas_call(gram_kernel, in_specs=[SMEM, SMEM, SMEM, VMEM, VMEM, VMEM]...]
  transfers between devices with their start and end apart: 3 -> 9, of which waited for: 2 -> 6; matrix products, arithmetic and copies ran while one was open for 1% -> 2% of each run, Pallas kernels for 0% -> 0%
where the time goes in v2:
time: 88.9 us; the launch traced here: 88.6 us
  blocking collectives  29.2 us (33%)
  waiting for transfers between devices  20.5 us (23%)
  starting transfers between devices  16.2 us (18%)
  Pallas kernels  13 us (15%)
  matrix products  4.87 us (5%)
  local copies, waits for them, and re-layouts  2.26 us (3%)
  other arithmetic  1.91 us (2%)
    ppermute x6, waiting for transfers between devices, scatter_stage(): lax.ppermute(pieces[d], AXES, plane_steps(d, stage))  16.6 us
    all_to_all x1, blocking collectives, per_device(): lax.all_to_all(plane_sum, 'sep', split_axis=0, concat_axis=0, tiled=True)  15.1 us
    all_to_all x1, blocking collectives, per_device(): lax.all_to_all(jnp.broadcast_to(packed[None], (PLANE, *packed.shape)), 'l...  14 us
    ppermute x6, starting transfers between devices, scatter_stage(): lax.ppermute(pieces[d], AXES, plane_steps(d, stage))  6.9 us
    ppermute x1, starting transfers between devices, per_device(): theirs = lax.ppermute(mine, 'mode', SWAP)  5.89 us
    pallas_call x1, Pallas kernels, gram(): pl.pallas_call(gram_kernel, in_specs=[SMEM, SMEM, SMEM, VMEM, VMEM, VMEM]...  5.63 us
    dot_general x1, matrix products, per_device(): jnp.einsum('ldw,ldm->lwm', coupling, modes, preferred_element_type=jnp.fl...  4.87 us
    pallas_call x2, Pallas kernels, total(): pl.pallas_call(functools.partial(total_kernel, len(pieces)), in_specs=[VM...  4.25 us
  transfers between devices with their start and end apart: 9, of which 6 were waited for; matrix products, arithmetic and copies ran while one was open for 2% of the time, Pallas kernels for 0%

profile of v2, /device:TPU:1, one launch (start us, length us, event | category | flops | bytes accessed | tf_op | source)
XLA Modules:
  0.0 88.6 jit_solution(4413596178645736379)
XLA Ops:
  0.6 4.9 %fusion.2.own_ref = f32[8,256,256]{2,1,0:T(8,128)S(1)} fusion(bf16[8,1024,256]{2,1,0:T(8,128)(2,1)} %param.9, bf16[8,1024,256]{2,1,0:T(8,128)(2,1)} %param.8), kind=kOutput, calls=%fused_computation.8 | convolution fusion | flops 1073741824 | bytes 10485760 | tf_op jit(solution)/shard_map/ldw,ldm->lwm/dot_general | solution.py:188
  5.5 0.0 copy-start.10
  5.5 3.3 %collective-permute-start = (f32[8,256,256]{2,1,0:T(8,128)S(1)}, f32[8,256,256]{2,1,0:T(8,128)}, u32[]{:S(2)}, u32[]{:S(2)}) collective-permute-start(f32[8,256,256]{2,1,0:T(8,128)S(1)} %fusion.2.own_ref), channel_id=1, source_target_pairs={{0,1},{1,0},{2,3},{3,2},{4,5},{5,4},{6,7},{7,6},{8,9},{9,8},{10,11... | collective-permute-start | bytes 6291464 | tf_op jit(solution)/shard_map/ppermute | solution.py:189
  8.8 0.1 collective-permute-start.1
  8.9 0.6 pad_add_fusion.1.place_ref
  9.6 3.2 %collective-permute-done.1 = f32[8,128]{1,0:T(8,128)S(1)} collective-permute-done((f32[8,128]{1,0:T(8,128)S(1)}, f32[8,128]{1,0:T(8,128)S(1)}, u32[]{:S(2)}, u32[]{:S(2)}) %collective-permute-start.1) | collective-permute-done | bytes 4128 | tf_op jit(solution)/shard_map/ppermute | solution.py:182
  12.8 0.6 maximum_select_fusion.eigen_ref
  13.4 5.6 %gram.1 = (bf16[4,8,16,512]{3,2,1,0:T(8,128)(2,1)}, bf16[4,8,16,512]{3,2,1,0:T(8,128)(2,1)}, bf16[4,8,16,512]{3,2,1,0:T(8,128)(2,1)}, bf16[4,8,16,512]{3,2,1,0:T(8,128)(2,1)}) custom-call(s32[8]{0:T(128)} %bitcast.25, s32[8]{0:T(128)} %offset_ref.1, s32[3]{0:T(128)} %pad_add_fusion.1.place_ref, f32[8,256,256]{2,1,0:T(8,128)} %copy-done, ...), custom_call_target="tpu_custom_call" | custom-call | tf_op jit(solution)/shard_map/gram/pallas_call | solution.py:76
  19.0 2.2 %collective-permute-start.3 = (bf16[4,8,16,512]{3,2,1,0:T(8,128)(2,1)}, bf16[4,8,16,512]{3,2,1,0:T(8,128)(2,1)S(1)}, u32[]{:S(2)}, u32[]{:S(2)}) collective-permute-start(bf16[4,8,16,512]{3,2,1,0:T(8,128)(2,1)} %get-tuple-element.12), channel_id=1, source_target_pairs={{0,32},{1,129},{2,34},{3,131},{4,36},{5,133},{6,38},{7,135},{8,40}... | collective-permute-start | bytes 1572872 | tf_op jit(solution)/shard_map/ppermute | solution.py:173
  21.2 1.1 %collective-permute-start.4 = (bf16[4,8,16,512]{3,2,1,0:T(8,128)(2,1)}, bf16[4,8,16,512]{3,2,1,0:T(8,128)(2,1)S(1)}, u32[]{:S(2)}, u32[]{:S(2)}) collective-permute-start(bf16[4,8,16,512]{3,2,1,0:T(8,128)(2,1)} %get-tuple-element.13), channel_id=1, source_target_pairs={{0,48},{1,193},{2,50},{3,195},{4,52},{5,197},{6,54},{7,199},{8,56}... | collective-permute-start | bytes 1572872 | tf_op jit(solution)/shard_map/ppermute | solution.py:173
  22.3 12.1 %collective-permute-done.2.refs_1_ = bf16[4,8,16,512]{3,2,1,0:T(8,128)(2,1)S(1)} collective-permute-done((bf16[4,8,16,512]{3,2,1,0:T(8,128)(2,1)}, bf16[4,8,16,512]{3,2,1,0:T(8,128)(2,1)S(1)}, u32[]{:S(2)}, u32[]{:S(2)}) %collective-permute-start.2) | collective-permute-done | bytes 524320 | tf_op jit(solution)/shard_map/ppermute | solution.py:173
  34.4 0.6 collective-permute-done.4.refs_3_
  35.0 0.2 copy-done.2
  35.2 0.2 copy-done.3
  35.4 0.4 copy-done.4
  35.8 2.4 %total.2 = (bf16[8,16,512]{2,1,0:T(8,128)(2,1)}, bf16[8,16,512]{2,1,0:T(8,128)(2,1)}, bf16[8,16,512]{2,1,0:T(8,128)(2,1)}, bf16[8,16,512]{2,1,0:T(8,128)(2,1)}) custom-call(bf16[4,8,16,512]{3,2,1,0:T(8,128)(2,1)} %get-tuple-element.10.refs_0_, bf16[4,8,16,512]{3,2,1,0:T(8,128)(2,1)} %copy-done.2, bf16[4,8,16,512]{3,2,1,0:T(8,128)(2,1)} %copy-done.3, ...), custom_call_target="tpu_custom_call" | custom-call | tf_op jit(solution)/shard_map/total/pallas_call | solution.py:96
  38.2 0.0 collective-permute-start.5
  38.3 2.4 %collective-permute-start.6 = (bf16[1,8,16,512]{3,2,1,0:T(8,128)(2,1)}, bf16[1,8,16,512]{3,2,1,0:T(8,128)(2,1)S(1)}, u32[]{:S(2)}, u32[]{:S(2)}) collective-permute-start(bf16[1,8,16,512]{3,2,1,0:T(8,128)(2,1)} %bitcast.27), channel_id=1, source_target_pairs={{0,128},{1,33},{2,130},{3,35},{4,132},{5,37},{6,134},{7,39},{8,136... | collective-permute-start | bytes 393224 | tf_op jit(solution)/shard_map/ppermute | solution.py:173
  40.7 1.2 %collective-permute-start.7 = (bf16[1,8,16,512]{3,2,1,0:T(8,128)(2,1)}, bf16[1,8,16,512]{3,2,1,0:T(8,128)(2,1)S(1)}, u32[]{:S(2)}, u32[]{:S(2)}) collective-permute-start(bf16[1,8,16,512]{3,2,1,0:T(8,128)(2,1)} %bitcast.26), channel_id=1, source_target_pairs={{0,192},{1,49},{2,194},{3,51},{4,196},{5,53},{6,198},{7,55},{8,200... | collective-permute-start | bytes 393224 | tf_op jit(solution)/shard_map/ppermute | solution.py:173
  41.9 3.3 %collective-permute-done.5.refs_1_ = bf16[1,8,16,512]{3,2,1,0:T(8,128)(2,1)S(1)} collective-permute-done((bf16[1,8,16,512]{3,2,1,0:T(8,128)(2,1)}, bf16[1,8,16,512]{3,2,1,0:T(8,128)(2,1)S(1)}, u32[]{:S(2)}, u32[]{:S(2)}) %collective-permute-start.5) | collective-permute-done | bytes 131104 | tf_op jit(solution)/shard_map/ppermute | solution.py:173
  45.2 0.6 collective-permute-done.7.refs_3_
  45.8 0.1 copy-done.6
  45.8 0.1 copy-done.7
  45.9 0.5 copy-done.8
  46.4 1.8 %total.3 = bf16[8,16,512]{2,1,0:T(8,128)(2,1)} custom-call(bf16[1,8,16,512]{3,2,1,0:T(8,128)(2,1)} %bitcast.23, bf16[1,8,16,512]{3,2,1,0:T(8,128)(2,1)} %copy-done.6, bf16[1,8,16,512]{3,2,1,0:T(8,128)(2,1)} %copy-done.7, bf16[1,8,16,512]{3,2,1,0:T(8,128)(2,1)} %copy-done.8), custom_call_target="tpu_custom_call" | custom-call | tf_op jit(solution)/shard_map/total/pallas_call | solution.py:96
  48.2 15.1 %all_to_all.10 = bf16[8,16,512]{2,1,0:T(8,128)(2,1)S(1)} all-to-all(bf16[8,16,512]{2,1,0:T(8,128)(2,1)} %total.3), channel_id=1, replica_groups=mesh['leaf'=16,'sep'=8,'mode'=2] {'sep'}, dimensions={0} | all-to-all | bytes 262144 | tf_op jit(solution)/shard_map/all_to_all | solution.py:197
  63.4 14.0 %all_to_all.11.own_ref = bf16[16,16,768]{2,1,0:T(8,128)(2,1)S(1)} all-to-all(bf16[16,16,768]{2,1,0:T(8,128)(2,1)S(1)} %broadcast_in_dim.22), channel_id=1, replica_groups=mesh['leaf'=16,'sep'=8,'mode'=2] {'leaf'}, dimensions={0} | all-to-all | bytes 786432 | tf_op jit(solution)/shard_map/all_to_all | solution.py:201
  77.5 5.9 %collective-permute-start.8 = (bf16[16,16,768]{2,1,0:T(8,128)(2,1)S(1)}, bf16[16,16,768]{2,1,0:T(8,128)(2,1)S(1)}, u32[]{:S(2)}, u32[]{:S(2)}) collective-permute-start(bf16[16,16,768]{2,1,0:T(8,128)(2,1)S(1)} %all_to_all.11.own_ref), channel_id=1, source_target_pairs={{0,1},{1,0},{2,3},{3,2},{4,5},{5,4},{6,7},{7,6},{8,9},{9,8},{10,11... | collective-permute-start | bytes 1179656 | tf_op jit(solution)/shard_map/ppermute | solution.py:208
  83.4 0.7 pad_add_fusion.place_ref
  84.0 0.7 collective-permute-done.8.other_ref
  84.7 0.7 copy-done.5
  85.5 3.1 %iterate.1 = (bf16[1,16,256]{2,1,0:T(8,128)(2,1)}, f32[1,2,256]{2,1,0:T(2,128)}) custom-call(s32[2]{0:T(128)} %pad_add_fusion.place_ref, bf16[16,16,768]{2,1,0:T(8,128)(2,1)} %copy-done.1, bf16[16,16,768]{2,1,0:T(8,128)(2,1)} %copy-done.5, bf16[2,256,256]{2,1,0:T(8,128)(2,1)} %bitcast.22), custom_call_target="tpu_custom_call" | custom-call | tf_op jit(solution)/shard_map/iterate/pallas_call | solution.py:136
  (24 shorter events, 0.1 us)
Async XLA Ops:
  0.6 8.2 %copy-start.11 = (f32[8,128]{1,0:T(8,128)S(1)}, f32[8,128]{1,0:T(8,128)}, u32[]{:S(2)}) copy-start(f32[8,128]{1,0:T(8,128)} %param.10) | copy-start | bytes 12292
  5.5 7.8 %copy-start = (f32[8,256,256]{2,1,0:T(8,128)}, f32[8,256,256]{2,1,0:T(8,128)S(1)}, u32[]{:S(2)}) copy-start(f32[8,256,256]{2,1,0:T(8,128)S(1)} %fusion.2.own_ref) | copy-start | bytes 6291460
  5.5 57.8 %copy-start.9 = (bf16[1,512,16]{1,2,0:T(8,128)(2,1)S(1)}, bf16[1,512,16]{1,2,0:T(8,128)(2,1)}, u32[]{:S(2)}) copy-start(bf16[1,512,16]{1,2,0:T(8,128)(2,1)} %param.13) | copy-start | bytes 49156
  5.5 57.8 %copy-start.10 = (bf16[1,16,256]{2,1,0:T(8,128)(2,1)S(1)}, bf16[1,16,256]{2,1,0:T(8,128)(2,1)}, u32[]{:S(2)}) copy-start(bf16[1,16,256]{2,1,0:T(8,128)(2,1)} %param.14) | copy-start | bytes 24580
  5.5 7.8 %collective-permute-start = (f32[8,256,256]{2,1,0:T(8,128)S(1)}, f32[8,256,256]{2,1,0:T(8,128)}, u32[]{:S(2)}, u32[]{:S(2)}) collective-permute-start(f32[8,256,256]{2,1,0:T(8,128)S(1)} %fusion.2.own_ref), channel_id=1, source_target_pairs={{0,1},{1,0},{2,3},{3,2},{4,5},{5,4},{6,7},{7,6},{8,9},{9,8},{10,11... | collective-permute-start | bytes 6291464 | tf_op jit(solution)/shard_map/ppermute | solution.py:189
  8.8 3.9 %collective-permute-start.1 = (f32[8,128]{1,0:T(8,128)S(1)}, f32[8,128]{1,0:T(8,128)S(1)}, u32[]{:S(2)}, u32[]{:S(2)}) collective-permute-start(f32[8,128]{1,0:T(8,128)S(1)} %copy-done.11), channel_id=1, source_target_pairs={{0,1},{1,0},{2,3},{3,2},{4,5},{5,4},{6,7},{7,6},{8,9},{9,8},{10,11... | collective-permute-start | bytes 12296 | tf_op jit(solution)/shard_map/ppermute | solution.py:182
  19.0 15.4 %collective-permute-start.2 = (bf16[4,8,16,512]{3,2,1,0:T(8,128)(2,1)}, bf16[4,8,16,512]{3,2,1,0:T(8,128)(2,1)S(1)}, u32[]{:S(2)}, u32[]{:S(2)}) collective-permute-start(bf16[4,8,16,512]{3,2,1,0:T(8,128)(2,1)} %get-tuple-element.11), channel_id=1, source_target_pairs={{0,16},{1,65},{2,18},{3,67},{4,20},{5,69},{6,22},{7,71},{8,24},{9,... | collective-permute-start | bytes 1572872 | tf_op jit(solution)/shard_map/ppermute | solution.py:173
  19.0 15.4 %collective-permute-start.3 = (bf16[4,8,16,512]{3,2,1,0:T(8,128)(2,1)}, bf16[4,8,16,512]{3,2,1,0:T(8,128)(2,1)S(1)}, u32[]{:S(2)}, u32[]{:S(2)}) collective-permute-start(bf16[4,8,16,512]{3,2,1,0:T(8,128)(2,1)} %get-tuple-element.12), channel_id=1, source_target_pairs={{0,32},{1,129},{2,34},{3,131},{4,36},{5,133},{6,38},{7,135},{8,40}... | collective-permute-start | bytes 1572872 | tf_op jit(solution)/shard_map/ppermute | solution.py:173
  21.2 13.8 %collective-permute-start.4 = (bf16[4,8,16,512]{3,2,1,0:T(8,128)(2,1)}, bf16[4,8,16,512]{3,2,1,0:T(8,128)(2,1)S(1)}, u32[]{:S(2)}, u32[]{:S(2)}) collective-permute-start(bf16[4,8,16,512]{3,2,1,0:T(8,128)(2,1)} %get-tuple-element.13), channel_id=1, source_target_pairs={{0,48},{1,193},{2,50},{3,195},{4,52},{5,197},{6,54},{7,199},{8,56}... | collective-permute-start | bytes 1572872 | tf_op jit(solution)/shard_map/ppermute | solution.py:173
  34.4 0.8 copy-start.2
  34.4 1.0 %copy-start.3 = (bf16[4,8,16,512]{3,2,1,0:T(8,128)(2,1)}, bf16[4,8,16,512]{3,2,1,0:T(8,128)(2,1)S(1)}, u32[]{:S(2)}) copy-start(bf16[4,8,16,512]{3,2,1,0:T(8,128)(2,1)S(1)} %collective-permute-done.3.refs_2_) | copy-start | bytes 1572868
  35.0 0.8 copy-start.4
  38.2 6.9 %collective-permute-start.5 = (bf16[1,8,16,512]{3,2,1,0:T(8,128)(2,1)}, bf16[1,8,16,512]{3,2,1,0:T(8,128)(2,1)S(1)}, u32[]{:S(2)}, u32[]{:S(2)}) collective-permute-start(bf16[1,8,16,512]{3,2,1,0:T(8,128)(2,1)} %bitcast.28), channel_id=1, source_target_pairs={{0,64},{1,17},{2,66},{3,19},{4,68},{5,21},{6,70},{7,23},{8,72},{9,... | collective-permute-start | bytes 393224 | tf_op jit(solution)/shard_map/ppermute | solution.py:173
  38.3 6.9 %collective-permute-start.6 = (bf16[1,8,16,512]{3,2,1,0:T(8,128)(2,1)}, bf16[1,8,16,512]{3,2,1,0:T(8,128)(2,1)S(1)}, u32[]{:S(2)}, u32[]{:S(2)}) collective-permute-start(bf16[1,8,16,512]{3,2,1,0:T(8,128)(2,1)} %bitcast.27), channel_id=1, source_target_pairs={{0,128},{1,33},{2,130},{3,35},{4,132},{5,37},{6,134},{7,39},{8,136... | collective-permute-start | bytes 393224 | tf_op jit(solution)/shard_map/ppermute | solution.py:173
  40.7 5.0 %collective-permute-start.7 = (bf16[1,8,16,512]{3,2,1,0:T(8,128)(2,1)}, bf16[1,8,16,512]{3,2,1,0:T(8,128)(2,1)S(1)}, u32[]{:S(2)}, u32[]{:S(2)}) collective-permute-start(bf16[1,8,16,512]{3,2,1,0:T(8,128)(2,1)} %bitcast.26), channel_id=1, source_target_pairs={{0,192},{1,49},{2,194},{3,51},{4,196},{5,53},{6,198},{7,55},{8,200... | collective-permute-start | bytes 393224 | tf_op jit(solution)/shard_map/ppermute | solution.py:173
  45.2 0.6 copy-start.6
  45.2 0.7 copy-start.7
  45.7 0.6 copy-start.8
  77.5 7.2 %copy-start.1 = (bf16[16,16,768]{2,1,0:T(8,128)(2,1)}, bf16[16,16,768]{2,1,0:T(8,128)(2,1)S(1)}, u32[]{:S(2)}) copy-start(bf16[16,16,768]{2,1,0:T(8,128)(2,1)S(1)} %all_to_all.11.own_ref) | copy-start | bytes 1179652
  77.5 7.2 %collective-permute-start.8 = (bf16[16,16,768]{2,1,0:T(8,128)(2,1)S(1)}, bf16[16,16,768]{2,1,0:T(8,128)(2,1)S(1)}, u32[]{:S(2)}, u32[]{:S(2)}) collective-permute-start(bf16[16,16,768]{2,1,0:T(8,128)(2,1)S(1)} %all_to_all.11.own_ref), channel_id=1, source_target_pairs={{0,1},{1,0},{2,3},{3,2},{4,5},{5,4},{6,7},{7,6},{8,9},{9,8},{10,11... | collective-permute-start | bytes 1179656 | tf_op jit(solution)/shard_map/ppermute | solution.py:208
  84.7 0.7 copy-start.5

commit v3 on v2

--- a/solution.py
+++ b/solution.py
@@ -28,7 +28,7 @@
 
 
 def gram_kernel(target_ref, offset_ref, place_ref, own_ref, other_ref, eigen_ref, *refs):
-    out_refs, pad_ref = refs[:SIDE], refs[SIDE]
+    out_refs, pad_ref = refs[: 2 * SIDE], refs[2 * SIDE]
     core, first, second = place_ref[0], place_ref[1], place_ref[2]
     row = lax.broadcasted_iota(jnp.int32, (SEP_ROWS, IFACE), 0)
     column = lax.broadcasted_iota(jnp.int32, (SEP_ROWS, IFACE), 1)
@@ -64,7 +64,7 @@
         for d in range(SIDE):
             for e in range(SIDE):
                 k = (d * SIDE + e) * STRIP
-                out_refs[d][e, s] = total[k : k + STRIP, :]
+                out_refs[2 * d + e // 2][e % 2, s] = total[k : k + STRIP, :]
 
 
 VMEM = pl.BlockSpec(memory_space=pltpu.VMEM)
@@ -72,34 +72,15 @@
 
 
 def gram(target, offset, place, own, other, eigen):
-    piece = jax.ShapeDtypeStruct((SIDE, NSEP, STRIP, SEP_ROWS), jnp.bfloat16)
+    piece = jax.ShapeDtypeStruct((2, NSEP, STRIP, SEP_ROWS), jnp.bfloat16)
     return pl.pallas_call(
         gram_kernel,
         in_specs=[SMEM, SMEM, SMEM, VMEM, VMEM, VMEM],
-        out_specs=[VMEM] * SIDE,
-        out_shape=[piece] * SIDE,
+        out_specs=[VMEM] * (2 * SIDE),
+        out_shape=[piece] * (2 * SIDE),
         scratch_shapes=[pltpu.VMEM((LEAF_DEV + 1, SEP_ROWS, MODES), jnp.bfloat16)],
         name="gram",
     )(target, offset, place, own, other, eigen)
-
-
-def total_kernel(count, *refs):
-    sources, outs = refs[:count], refs[count:]
-    for k, out_ref in enumerate(outs):
-        for s in range(NSEP):
-            value = sum(ref[k, s].astype(jnp.float32) for ref in sources)
-            out_ref[s] = value.astype(jnp.bfloat16)
-
-
-def total(pieces):
-    lead = pieces[0].shape[0]
-    return pl.pallas_call(
-        functools.partial(total_kernel, len(pieces)),
-        in_specs=[VMEM] * len(pieces),
-        out_specs=[VMEM] * lead,
-        out_shape=[jax.ShapeDtypeStruct(pieces[0].shape[1:], jnp.bfloat16)] * lead,
-        name="total",
-    )(*pieces)
 
 
 def iterate_kernel(place_ref, own_ref, other_ref, turns_ref, out_ref, norms_ref, at_ref, x_ref):
@@ -169,9 +150,18 @@
     return pairs
 
 
-def scatter_stage(pieces, stage):
-    got = [lax.ppermute(pieces[d], AXES, plane_steps(d, stage)) for d in range(1, SIDE)]
-    return [pieces[0], *got]
+def add(*terms):
+    return sum(term.astype(jnp.float32) for term in terms).astype(jnp.bfloat16)
+
+
+def ring_scatter(pieces, stage):
+    up = functools.partial(lax.ppermute, axis_name=AXES, perm=plane_steps(1, stage))
+    down = functools.partial(lax.ppermute, axis_name=AXES, perm=plane_steps(SIDE - 1, stage))
+    own, ahead, opposite, behind = pieces
+    relay_down, relay_up = down(opposite[0]), up(opposite[1])
+    direct_down, direct_up = down(behind[1]), up(ahead[0])
+    last_down, last_up = down(add(behind[0], relay_down)), up(add(ahead[1], relay_up))
+    return (own[0], direct_up, last_down), (own[1], last_up, direct_down)
 
 
 def per_device(
@@ -190,10 +180,12 @@
     leaf = lax.axis_index("leaf").astype(jnp.int32)
     y, x = leaf >> 2, leaf & 3
     place = jnp.stack([core, jnp.where(core == 0, x, y), jnp.where(core == 0, y, x)])
-    pieces = gram(separator_of[:, 0], row_offset, place, own, other, eigen)
-    pieces = total(scatter_stage(pieces, 0))
-    pieces = [piece[None] for piece in pieces]
-    (plane_sum,) = total(scatter_stage(pieces, 1))
+    halves = gram(separator_of[:, 0], row_offset, place, own, other, eigen)
+    terms = ring_scatter([halves[2 * d : 2 * d + 2] for d in range(SIDE)], 0)
+    strips = [add(*[term[e % 2] for term in terms[e // 2]]) for e in range(SIDE)]
+    half = NSEP // 2
+    terms = ring_scatter([(strip[:half], strip[half:]) for strip in strips], 1)
+    plane_sum = jnp.concatenate([add(*terms[0]), add(*terms[1])], 0)
     got = lax.all_to_all(plane_sum, "sep", split_axis=0, concat_axis=0, tiled=True)
     correction = jnp.sum(got.astype(jnp.float32), 0)
     columns = (stiffness[0].T.astype(jnp.float32) - correction).astype(jnp.bfloat16)

time: 88.9 us -> 89.8 us (1.010)
  starting transfers between devices: 16.2 us -> 25.3 us
  waiting for transfers between devices: 20.5 us -> 15.9 us
  other arithmetic: 1.91 us -> 6.28 us
  Pallas kernels: 13 us -> 8.77 us
  blocking collectives: 29.2 us -> 26.8 us
  local copies, waits for them, and re-layouts: 2.26 us -> 0.81 us
    ppermute x6 -> x12, starting transfers between devices: 6.9 us -> 13.4 us  [the longest x4 5.68 us: ring_scatter(): relay_down, relay_up = (down(opposite[0]), up(opposite[1]))]
    ppermute x6 -> x12, waiting for transfers between devices: 16.6 us -> 12 us  [the longest x2 4.93 us: ring_scatter(): up(add(ahead[1], relay_up))]
    convert_element_type x0 -> x7, other arithmetic: none -> 4.32 us  [add(): sum((term.astype(jnp.float32) for term in terms)).astype(jnp.bfloat16)]
    pallas_call x2 -> x0, Pallas kernels: 4.25 us -> none  [total(): pl.pallas_call(functools.partial(total_kernel, len(pieces)), in_specs=[VM...]
    all_to_all x1, blocking collectives: 14 us -> 10.9 us  [per_device(): lax.all_to_all(jnp.broadcast_to(packed[None], (PLANE, *packed.shape)), 'l...]
    ppermute x1, starting transfers between devices: 5.89 us -> 8.5 us  [per_device(): theirs = lax.ppermute(mine, 'mode', SWAP)]
    unnamed x24 -> x12, local copies, waits for them, and re-layouts: 2.23 us -> 0.76 us
  transfers between devices with their start and end apart: 9 -> 15, of which waited for: 6 -> 9; matrix products, arithmetic and copies ran while one was open for 2% -> 7% of each run, Pallas kernels for 0% -> 0%
where the time goes in v3:
time: 89.8 us; the launch traced here: 89.5 us
  blocking collectives  26.8 us (30%)
  starting transfers between devices  25.3 us (28%)
  waiting for transfers between devices  15.9 us (18%)
  Pallas kernels  8.77 us (10%)
  other arithmetic  6.28 us (7%)
  matrix products  4.87 us (5%)
    all_to_all x1, blocking collectives, per_device(): lax.all_to_all(plane_sum, 'sep', split_axis=0, concat_axis=0, tiled=True)  15.9 us
    all_to_all x1, blocking collectives, per_device(): lax.all_to_all(jnp.broadcast_to(packed[None], (PLANE, *packed.shape)), 'l...  10.9 us
    ppermute x1, starting transfers between devices, per_device(): theirs = lax.ppermute(mine, 'mode', SWAP)  8.5 us
    ppermute x4, starting transfers between devices, ring_scatter(): relay_down, relay_up = (down(opposite[0]), up(opposite[1]))  5.68 us
    pallas_call x1, Pallas kernels, gram(): pl.pallas_call(gram_kernel, in_specs=[SMEM, SMEM, SMEM, VMEM, VMEM, VMEM]...  5.66 us
    ppermute x2, starting transfers between devices, ring_scatter(): down(add(behind[0], relay_down))  4.95 us
    ppermute x2, waiting for transfers between devices, ring_scatter(): up(add(ahead[1], relay_up))  4.93 us
    dot_general x1, matrix products, per_device(): jnp.einsum('ldw,ldm->lwm', coupling, modes, preferred_element_type=jnp.fl...  4.87 us
  transfers between devices with their start and end apart: 15, of which 9 were waited for; matrix products, arithmetic and copies ran while one was open for 7% of the time, Pallas kernels for 0%

profile of v3, /device:TPU:1, one launch (start us, length us, event | category | flops | bytes accessed | tf_op | source)
XLA Modules:
  0.0 89.5 jit_solution(1864828417153116723)
XLA Ops:
  0.6 4.9 %fusion.8.own_ref = f32[8,256,256]{2,1,0:T(8,128)S(1)} fusion(bf16[8,1024,256]{2,1,0:T(8,128)(2,1)} %param.9, bf16[8,1024,256]{2,1,0:T(8,128)(2,1)} %param.8), kind=kOutput, calls=%fused_computation.33 | convolution fusion | flops 1073741824 | bytes 10485760 | tf_op jit(solution)/shard_map/ldw,ldm->lwm/dot_general | solution.py:178
  5.5 3.3 %collective-permute-start = (f32[8,256,256]{2,1,0:T(8,128)S(1)}, f32[8,256,256]{2,1,0:T(8,128)}, u32[]{:S(2)}, u32[]{:S(2)}) collective-permute-start(f32[8,256,256]{2,1,0:T(8,128)S(1)} %fusion.8.own_ref), channel_id=1, source_target_pairs={{0,1},{1,0},{2,3},{3,2},{4,5},{5,4},{6,7},{7,6},{8,9},{9,8},{10,11... | collective-permute-start | bytes 6291464 | tf_op jit(solution)/shard_map/ppermute | solution.py:179
  8.9 0.7 pad_add_fusion.1.place_ref
  9.6 3.1 %collective-permute-done.1 = f32[8,128]{1,0:T(8,128)S(1)} collective-permute-done((f32[8,128]{1,0:T(8,128)S(1)}, f32[8,128]{1,0:T(8,128)S(1)}, u32[]{:S(2)}, u32[]{:S(2)}) %collective-permute-start.1) | collective-permute-done | bytes 4128 | tf_op jit(solution)/shard_map/ppermute | solution.py:172
  12.7 0.6 maximum_select_fusion.eigen_ref
  13.3 5.7 %gram.1 = (bf16[2,8,16,512]{3,2,1,0:T(8,128)(2,1)}, bf16[2,8,16,512]{3,2,1,0:T(8,128)(2,1)}, bf16[2,8,16,512]{3,2,1,0:T(8,128)(2,1)}, bf16[2,8,16,512]{3,2,1,0:T...) custom-call(s32[8]{0:T(128)} %bitcast.48, ...), custom_call_target="tpu_custom_call" | custom-call | tf_op jit(solution)/shard_map/gram/pallas_call | solution.py:76
  19.0 1.0 %collective-permute-start.3 = (bf16[2,8,16,512]{3,2,1,0:T(8,128)(2,1)}, bf16[2,8,16,512]{3,2,1,0:T(8,128)(2,1)S(1)}, u32[]{:S(2)}, u32[]{:S(2)}) collective-permute-start(bf16[2,8,16,512]{3,2,1,0:T(8,128)(2,1)} %get-tuple-element.13), channel_id=1, source_target_pairs={{0,48},{1,193},{2,50},{3,195},{4,52},{5,197},{6,54},{7,199},{8,56}... | collective-permute-start | bytes 786440 | tf_op jit(solution)/shard_map/ppermute | solution.py:161
  20.0 0.4 collective-permute-start.6
  20.5 4.2 %collective-permute-done.3 = bf16[2,8,16,512]{3,2,1,0:T(8,128)(2,1)S(1)} collective-permute-done((bf16[2,8,16,512]{3,2,1,0:T(8,128)(2,1)}, bf16[2,8,16,512]{3,2,1,0:T(8,128)(2,1)S(1)}, u32[]{:S(2)}, u32[]{:S(2)}) %collective-permute-start.3) | collective-permute-done | bytes 262176 | tf_op jit(solution)/shard_map/ppermute | solution.py:161
  24.7 1.0 %add_convert_fusion.1 = bf16[2,8,16,512]{3,2,1,0:T(8,128)(2,1)S(1)} fusion(bf16[2,8,16,512]{3,2,1,0:T(8,128)(2,1)S(1)} %collective-permute-done.3, bf16[2,8,16,512]{3,2,1,0:T(8,128)(2,1)} %get-tuple-element.12), kind=kLoop, calls=%fused_computation.1 | loop fusion | flops 524288 | bytes 786432 | tf_op jit(solution)/shard_map/convert_element_type | solution.py:154
  25.8 2.0 %collective-permute-start.4 = (bf16[2,8,16,512]{3,2,1,0:T(8,128)(2,1)S(1)}, bf16[2,8,16,512]{3,2,1,0:T(8,128)(2,1)S(1)}, u32[]{:S(2)}, u32[]{:S(2)}) collective-permute-start(bf16[2,8,16,512]{3,2,1,0:T(8,128)(2,1)S(1)} %add_convert_fusion.1), channel_id=1, source_target_pairs={{0,48},{1,193},{2,50},{3,195},{4,52},{5,197},{6,54},{7,199},{8,56}... | collective-permute-start | bytes 786440 | tf_op jit(solution)/shard_map/ppermute | solution.py:163
  27.9 1.0 %add_convert_fusion = bf16[2,8,16,512]{3,2,1,0:T(8,128)(2,1)S(1)} fusion(bf16[2,8,16,512]{3,2,1,0:T(8,128)(2,1)S(1)} %collective-permute-done.6, bf16[2,8,16,512]{3,2,1,0:T(8,128)(2,1)} %get-tuple-element.15), kind=kLoop, calls=%fused_computation | loop fusion | flops 524288 | bytes 786432 | tf_op jit(solution)/shard_map/convert_element_type | solution.py:154
  28.9 1.5 %collective-permute-start.7 = (bf16[2,8,16,512]{3,2,1,0:T(8,128)(2,1)S(1)}, bf16[2,8,16,512]{3,2,1,0:T(8,128)(2,1)S(1)}, u32[]{:S(2)}, u32[]{:S(2)}) collective-permute-start(bf16[2,8,16,512]{3,2,1,0:T(8,128)(2,1)S(1)} %add_convert_fusion), channel_id=1, source_target_pairs={{0,16},{1,65},{2,18},{3,67},{4,20},{5,69},{6,22},{7,71},{8,24},{9,... | collective-permute-start | bytes 786440 | tf_op jit(solution)/shard_map/ppermute | solution.py:163
  30.4 1.0 %collective-permute-done.4 = bf16[2,8,16,512]{3,2,1,0:T(8,128)(2,1)S(1)} collective-permute-done((bf16[2,8,16,512]{3,2,1,0:T(8,128)(2,1)S(1)}, bf16[2,8,16,512]{3,2,1,0:T(8,128)(2,1)S(1)}, u32[]{:S(2)}, u32[]{:S(2)}) %collective-permute-start.4) | collective-permute-done | bytes 262176 | tf_op jit(solution)/shard_map/ppermute | solution.py:163
  31.4 1.1 %add_convert_fusion.5 = (bf16[1,8,16,512]{3,2,1,0:T(8,128)(2,1)S(1)}, bf16[1,8,16,512]{3,2,1,0:T(8,128)(2,1)S(1)}) fusion(bf16[2,8,16,512]{3,2,1,0:T(8,128)(2,1)S(1)} %collective-permute-done.4, bf16[2,8,16,512]{3,2,1,0:T(8,128)(2,1)S(1)} %collective-permute-done.2, bf16[2,8,16,512]{3,2,1,0:T(8,128)(2,1)} %get-tuple-element.10), kind=kLoop, calls=%fused_computation.6 | loop fusion | flops 786432 | bytes 1048576 | tf_op jit(solution)/shard_map/convert_element_type | solution.py:154
  32.5 1.0 %collective-permute-start.5 = (bf16[4,16,512]{2,1,0:T(8,128)(2,1)S(1)}, bf16[4,16,512]{2,1,0:T(8,128)(2,1)S(1)}, u32[]{:S(2)}, u32[]{:S(2)}) collective-permute-start(bf16[4,16,512]{2,1,0:T(8,128)(2,1)S(1)} %slice_bitcast_fusion.6), channel_id=1, source_target_pairs={{0,64},{1,17},{2,66},{3,19},{4,68},{5,21},{6,70},{7,23},{8,72},{9,... | collective-permute-start | bytes 196616 | tf_op jit(solution)/shard_map/ppermute | solution.py:162
  33.5 0.7 collective-permute-done.8
  34.2 1.6 %collective-permute-done.7 = bf16[2,8,16,512]{3,2,1,0:T(8,128)(2,1)S(1)} collective-permute-done((bf16[2,8,16,512]{3,2,1,0:T(8,128)(2,1)S(1)}, bf16[2,8,16,512]{3,2,1,0:T(8,128)(2,1)S(1)}, u32[]{:S(2)}, u32[]{:S(2)}) %collective-permute-start.7) | collective-permute-done | bytes 262176 | tf_op jit(solution)/shard_map/ppermute | solution.py:163
  35.7 1.1 %add_convert_fusion.2 = (bf16[1,8,16,512]{3,2,1,0:T(8,128)(2,1)S(1)}, bf16[1,8,16,512]{3,2,1,0:T(8,128)(2,1)S(1)}) fusion(bf16[2,8,16,512]{3,2,1,0:T(8,128)(2,1)S(1)} %collective-permute-done.8, bf16[2,8,16,512]{3,2,1,0:T(8,128)(2,1)S(1)} %collective-permute-done.7, bf16[2,8,16,512]{3,2,1,0:T(8,128)(2,1)} %get-tuple-element.14), kind=kLoop, calls=%fused_computation.3 | loop fusion | flops 786432 | bytes 1048576 | tf_op jit(solution)/shard_map/convert_element_type | solution.py:154
  36.8 2.8 %collective-permute-start.9 = (bf16[4,16,512]{2,1,0:T(8,128)(2,1)S(1)}, bf16[4,16,512]{2,1,0:T(8,128)(2,1)S(1)}, u32[]{:S(2)}, u32[]{:S(2)}) collective-permute-start(bf16[4,16,512]{2,1,0:T(8,128)(2,1)S(1)} %get-tuple-element.24), channel_id=1, source_target_pairs={{0,192},{1,49},{2,194},{3,51},{4,196},{5,53},{6,198},{7,55},{8,200... | collective-permute-start | bytes 196616 | tf_op jit(solution)/shard_map/ppermute | solution.py:161
  39.8 1.4 %collective-permute-start.11 = (bf16[4,16,512]{2,1,0:T(8,128)(2,1)S(1)}, bf16[4,16,512]{2,1,0:T(8,128)(2,1)S(1)}, u32[]{:S(2)}, u32[]{:S(2)}) collective-permute-start(bf16[4,16,512]{2,1,0:T(8,128)(2,1)S(1)} %get-tuple-element.25), channel_id=1, source_target_pairs={{0,64},{1,17},{2,66},{3,19},{4,68},{5,21},{6,70},{7,23},{8,72},{9,... | collective-permute-start | bytes 196616 | tf_op jit(solution)/shard_map/ppermute | solution.py:161
  41.2 2.9 %collective-permute-start.10 = (bf16[4,16,512]{2,1,0:T(8,128)(2,1)S(1)}, bf16[4,16,512]{2,1,0:T(8,128)(2,1)S(1)}, u32[]{:S(2)}, u32[]{:S(2)}) collective-permute-start(bf16[4,16,512]{2,1,0:T(8,128)(2,1)S(1)} %fusion.3), channel_id=1, source_target_pairs={{0,192},{1,49},{2,194},{3,51},{4,196},{5,53},{6,198},{7,55},{8,200... | collective-permute-start | bytes 196616 | tf_op jit(solution)/shard_map/ppermute | solution.py:163
  44.1 0.2 collective-permute-done.11
  44.4 1.0 %collective-permute-done.10 = bf16[4,16,512]{2,1,0:T(8,128)(2,1)S(1)} collective-permute-done((bf16[4,16,512]{2,1,0:T(8,128)(2,1)S(1)}, bf16[4,16,512]{2,1,0:T(8,128)(2,1)S(1)}, u32[]{:S(2)}, u32[]{:S(2)}) %collective-permute-start.10) | collective-permute-done | bytes 65568 | tf_op jit(solution)/shard_map/ppermute | solution.py:163
  45.4 3.4 %collective-permute-done.12 = bf16[4,16,512]{2,1,0:T(8,128)(2,1)S(1)} collective-permute-done((bf16[4,16,512]{2,1,0:T(8,128)(2,1)S(1)}, bf16[4,16,512]{2,1,0:T(8,128)(2,1)S(1)}, u32[]{:S(2)}, u32[]{:S(2)}) %collective-permute-start.12) | collective-permute-done | bytes 65568 | tf_op jit(solution)/shard_map/ppermute | solution.py:163
  48.9 15.9 %all_to_all.10 = bf16[8,16,512]{2,1,0:T(8,128)(2,1)S(1)} all-to-all(bf16[8,16,512]{2,1,0:T(8,128)(2,1)S(1)} %pad_maximum_fusion), channel_id=1, replica_groups=mesh['leaf'=16,'sep'=8,'mode'=2] {'sep'}, dimensions={0} | all-to-all | bytes 262144 | tf_op jit(solution)/shard_map/all_to_all | solution.py:189
  64.9 10.9 %all_to_all.11.own_ref = bf16[16,16,768]{2,1,0:T(8,128)(2,1)S(1)} all-to-all(bf16[16,16,768]{2,1,0:T(8,128)(2,1)S(1)} %broadcast_in_dim.2), channel_id=1, replica_groups=mesh['leaf'=16,'sep'=8,'mode'=2] {'leaf'}, dimensions={0} | all-to-all | bytes 786432 | tf_op jit(solution)/shard_map/all_to_all | solution.py:193
  75.8 8.5 %collective-permute-start.14 = (bf16[16,16,768]{2,1,0:T(8,128)(2,1)S(1)}, bf16[16,16,768]{2,1,0:T(8,128)(2,1)S(1)}, u32[]{:S(2)}, u32[]{:S(2)}) collective-permute-start(bf16[16,16,768]{2,1,0:T(8,128)(2,1)S(1)} %all_to_all.11.own_ref), channel_id=1, source_target_pairs={{0,1},{1,0},{2,3},{3,2},{4,5},{5,4},{6,7},{7,6},{8,9},{9,8},{10,11... | collective-permute-start | bytes 1179656 | tf_op jit(solution)/shard_map/ppermute | solution.py:200
  84.3 0.6 pad_add_fusion.place_ref
  85.0 0.7 collective-permute-done.14.other_ref
  85.7 0.7 copy-done.2
  86.4 3.1 %iterate.1 = (bf16[1,16,256]{2,1,0:T(8,128)(2,1)}, f32[1,2,256]{2,1,0:T(2,128)}) custom-call(s32[2]{0:T(128)} %pad_add_fusion.place_ref, bf16[16,16,768]{2,1,0:T(8,128)(2,1)} %copy-done.1, bf16[16,16,768]{2,1,0:T(8,128)(2,1)} %copy-done.2, bf16[2,256,256]{2,1,0:T(8,128)(2,1)} %bitcast.46), custom_call_target="tpu_custom_call" | custom-call | tf_op jit(solution)/shard_map/iterate/pallas_call | solution.py:117
  (33 shorter events, 0.6 us)
Async XLA Ops:
  0.6 8.2 %copy-start.5 = (f32[8,128]{1,0:T(8,128)S(1)}, f32[8,128]{1,0:T(8,128)}, u32[]{:S(2)}) copy-start(f32[8,128]{1,0:T(8,128)} %param.10) | copy-start | bytes 12292
  5.5 7.8 %copy-start = (f32[8,256,256]{2,1,0:T(8,128)}, f32[8,256,256]{2,1,0:T(8,128)S(1)}, u32[]{:S(2)}) copy-start(f32[8,256,256]{2,1,0:T(8,128)S(1)} %fusion.8.own_ref) | copy-start | bytes 6291460
  5.5 7.8 %collective-permute-start = (f32[8,256,256]{2,1,0:T(8,128)S(1)}, f32[8,256,256]{2,1,0:T(8,128)}, u32[]{:S(2)}, u32[]{:S(2)}) collective-permute-start(f32[8,256,256]{2,1,0:T(8,128)S(1)} %fusion.8.own_ref), channel_id=1, source_target_pairs={{0,1},{1,0},{2,3},{3,2},{4,5},{5,4},{6,7},{7,6},{8,9},{9,8},{10,11... | collective-permute-start | bytes 6291464 | tf_op jit(solution)/shard_map/ppermute | solution.py:179
  8.8 3.9 %collective-permute-start.1 = (f32[8,128]{1,0:T(8,128)S(1)}, f32[8,128]{1,0:T(8,128)S(1)}, u32[]{:S(2)}, u32[]{:S(2)}) collective-permute-start(f32[8,128]{1,0:T(8,128)S(1)} %copy-done.5), channel_id=1, source_target_pairs={{0,1},{1,0},{2,3},{3,2},{4,5},{5,4},{6,7},{7,6},{8,9},{9,8},{10,11... | collective-permute-start | bytes 12296 | tf_op jit(solution)/shard_map/ppermute | solution.py:172
  13.3 51.5 %copy-start.3 = (bf16[1,512,16]{1,2,0:T(8,128)(2,1)S(1)}, bf16[1,512,16]{1,2,0:T(8,128)(2,1)}, u32[]{:S(2)}) copy-start(bf16[1,512,16]{1,2,0:T(8,128)(2,1)} %param.13) | copy-start | bytes 49156
  13.3 51.5 %copy-start.4 = (bf16[1,16,256]{2,1,0:T(8,128)(2,1)S(1)}, bf16[1,16,256]{2,1,0:T(8,128)(2,1)}, u32[]{:S(2)}) copy-start(bf16[1,16,256]{2,1,0:T(8,128)(2,1)} %param.14) | copy-start | bytes 24580
  19.0 5.7 %collective-permute-start.3 = (bf16[2,8,16,512]{3,2,1,0:T(8,128)(2,1)}, bf16[2,8,16,512]{3,2,1,0:T(8,128)(2,1)S(1)}, u32[]{:S(2)}, u32[]{:S(2)}) collective-permute-start(bf16[2,8,16,512]{3,2,1,0:T(8,128)(2,1)} %get-tuple-element.13), channel_id=1, source_target_pairs={{0,48},{1,193},{2,50},{3,195},{4,52},{5,197},{6,54},{7,199},{8,56}... | collective-permute-start | bytes 786440 | tf_op jit(solution)/shard_map/ppermute | solution.py:161
  20.0 7.9 %collective-permute-start.6 = (bf16[2,8,16,512]{3,2,1,0:T(8,128)(2,1)}, bf16[2,8,16,512]{3,2,1,0:T(8,128)(2,1)S(1)}, u32[]{:S(2)}, u32[]{:S(2)}) collective-permute-start(bf16[2,8,16,512]{3,2,1,0:T(8,128)(2,1)} %get-tuple-element.16), channel_id=1, source_target_pairs={{0,16},{1,65},{2,18},{3,67},{4,20},{5,69},{6,22},{7,71},{8,24},{9,... | collective-permute-start | bytes 786440 | tf_op jit(solution)/shard_map/ppermute | solution.py:161
  20.5 9.9 %collective-permute-start.2 = (bf16[2,8,16,512]{3,2,1,0:T(8,128)(2,1)}, bf16[2,8,16,512]{3,2,1,0:T(8,128)(2,1)S(1)}, u32[]{:S(2)}, u32[]{:S(2)}) collective-permute-start(bf16[2,8,16,512]{3,2,1,0:T(8,128)(2,1)} %get-tuple-element.11), channel_id=1, source_target_pairs={{0,16},{1,65},{2,18},{3,67},{4,20},{5,69},{6,22},{7,71},{8,24},{9,... | collective-permute-start | bytes 786440 | tf_op jit(solution)/shard_map/ppermute | solution.py:162
  25.8 5.6 %collective-permute-start.4 = (bf16[2,8,16,512]{3,2,1,0:T(8,128)(2,1)S(1)}, bf16[2,8,16,512]{3,2,1,0:T(8,128)(2,1)S(1)}, u32[]{:S(2)}, u32[]{:S(2)}) collective-permute-start(bf16[2,8,16,512]{3,2,1,0:T(8,128)(2,1)S(1)} %add_convert_fusion.1), channel_id=1, source_target_pairs={{0,48},{1,193},{2,50},{3,195},{4,52},{5,197},{6,54},{7,199},{8,56}... | collective-permute-start | bytes 786440 | tf_op jit(solution)/shard_map/ppermute | solution.py:163
  27.8 6.4 %collective-permute-start.8 = (bf16[2,8,16,512]{3,2,1,0:T(8,128)(2,1)}, bf16[2,8,16,512]{3,2,1,0:T(8,128)(2,1)S(1)}, u32[]{:S(2)}, u32[]{:S(2)}) collective-permute-start(bf16[2,8,16,512]{3,2,1,0:T(8,128)(2,1)} %get-tuple-element.17), channel_id=1, source_target_pairs={{0,48},{1,193},{2,50},{3,195},{4,52},{5,197},{6,54},{7,199},{8,56}... | collective-permute-start | bytes 786440 | tf_op jit(solution)/shard_map/ppermute | solution.py:162
  28.9 6.8 %collective-permute-start.7 = (bf16[2,8,16,512]{3,2,1,0:T(8,128)(2,1)S(1)}, bf16[2,8,16,512]{3,2,1,0:T(8,128)(2,1)S(1)}, u32[]{:S(2)}, u32[]{:S(2)}) collective-permute-start(bf16[2,8,16,512]{3,2,1,0:T(8,128)(2,1)S(1)} %add_convert_fusion), channel_id=1, source_target_pairs={{0,16},{1,65},{2,18},{3,67},{4,20},{5,69},{6,22},{7,71},{8,24},{9,... | collective-permute-start | bytes 786440 | tf_op jit(solution)/shard_map/ppermute | solution.py:163
  32.5 11.9 %collective-permute-start.5 = (bf16[4,16,512]{2,1,0:T(8,128)(2,1)S(1)}, bf16[4,16,512]{2,1,0:T(8,128)(2,1)S(1)}, u32[]{:S(2)}, u32[]{:S(2)}) collective-permute-start(bf16[4,16,512]{2,1,0:T(8,128)(2,1)S(1)} %slice_bitcast_fusion.6), channel_id=1, source_target_pairs={{0,64},{1,17},{2,66},{3,19},{4,68},{5,21},{6,70},{7,23},{8,72},{9,... | collective-permute-start | bytes 196616 | tf_op jit(solution)/shard_map/ppermute | solution.py:162
  36.8 4.3 %collective-permute-start.9 = (bf16[4,16,512]{2,1,0:T(8,128)(2,1)S(1)}, bf16[4,16,512]{2,1,0:T(8,128)(2,1)S(1)}, u32[]{:S(2)}, u32[]{:S(2)}) collective-permute-start(bf16[4,16,512]{2,1,0:T(8,128)(2,1)S(1)} %get-tuple-element.24), channel_id=1, source_target_pairs={{0,192},{1,49},{2,194},{3,51},{4,196},{5,53},{6,198},{7,55},{8,200... | collective-permute-start | bytes 196616 | tf_op jit(solution)/shard_map/ppermute | solution.py:161
  39.7 4.7 %collective-permute-start.13 = (bf16[4,16,512]{2,1,0:T(8,128)(2,1)S(1)}, bf16[4,16,512]{2,1,0:T(8,128)(2,1)S(1)}, u32[]{:S(2)}, u32[]{:S(2)}) collective-permute-start(bf16[4,16,512]{2,1,0:T(8,128)(2,1)S(1)} %slice_bitcast_fusion), channel_id=1, source_target_pairs={{0,192},{1,49},{2,194},{3,51},{4,196},{5,53},{6,198},{7,55},{8,200... | collective-permute-start | bytes 196616 | tf_op jit(solution)/shard_map/ppermute | solution.py:162
  39.8 4.5 %collective-permute-start.11 = (bf16[4,16,512]{2,1,0:T(8,128)(2,1)S(1)}, bf16[4,16,512]{2,1,0:T(8,128)(2,1)S(1)}, u32[]{:S(2)}, u32[]{:S(2)}) collective-permute-start(bf16[4,16,512]{2,1,0:T(8,128)(2,1)S(1)} %get-tuple-element.25), channel_id=1, source_target_pairs={{0,64},{1,17},{2,66},{3,19},{4,68},{5,21},{6,70},{7,23},{8,72},{9,... | collective-permute-start | bytes 196616 | tf_op jit(solution)/shard_map/ppermute | solution.py:161
  41.2 4.3 %collective-permute-start.10 = (bf16[4,16,512]{2,1,0:T(8,128)(2,1)S(1)}, bf16[4,16,512]{2,1,0:T(8,128)(2,1)S(1)}, u32[]{:S(2)}, u32[]{:S(2)}) collective-permute-start(bf16[4,16,512]{2,1,0:T(8,128)(2,1)S(1)} %fusion.3), channel_id=1, source_target_pairs={{0,192},{1,49},{2,194},{3,51},{4,196},{5,53},{6,198},{7,55},{8,200... | collective-permute-start | bytes 196616 | tf_op jit(solution)/shard_map/ppermute | solution.py:163
  44.3 4.5 %collective-permute-start.12 = (bf16[4,16,512]{2,1,0:T(8,128)(2,1)S(1)}, bf16[4,16,512]{2,1,0:T(8,128)(2,1)S(1)}, u32[]{:S(2)}, u32[]{:S(2)}) collective-permute-start(bf16[4,16,512]{2,1,0:T(8,128)(2,1)S(1)} %fusion), channel_id=1, source_target_pairs={{0,64},{1,17},{2,66},{3,19},{4,68},{5,21},{6,70},{7,23},{8,72},{9,... | collective-permute-start | bytes 196616 | tf_op jit(solution)/shard_map/ppermute | solution.py:163
  75.8 9.9 %copy-start.1 = (bf16[16,16,768]{2,1,0:T(8,128)(2,1)}, bf16[16,16,768]{2,1,0:T(8,128)(2,1)S(1)}, u32[]{:S(2)}) copy-start(bf16[16,16,768]{2,1,0:T(8,128)(2,1)S(1)} %all_to_all.11.own_ref) | copy-start | bytes 1179652
  75.8 9.8 %collective-permute-start.14 = (bf16[16,16,768]{2,1,0:T(8,128)(2,1)S(1)}, bf16[16,16,768]{2,1,0:T(8,128)(2,1)S(1)}, u32[]{:S(2)}, u32[]{:S(2)}) collective-permute-start(bf16[16,16,768]{2,1,0:T(8,128)(2,1)S(1)} %all_to_all.11.own_ref), channel_id=1, source_target_pairs={{0,1},{1,0},{2,3},{3,2},{4,5},{5,4},{6,7},{7,6},{8,9},{9,8},{10,11... | collective-permute-start | bytes 1179656 | tf_op jit(solution)/shard_map/ppermute | solution.py:200
  85.7 0.7 copy-start.2

commit v4 on v3

v4 whole, which is shorter than its diff:
```python
import functools

import jax
import jax.numpy as jnp
from jax import lax
from jax.experimental import pallas as pl
from jax.experimental.pallas import tpu as pltpu
from jax.sharding import PartitionSpec as P

SEP_ROWS = 512
IFACE = 256
MODES = 256
COLS = 256
NSEP = 8
LEAF_DEV = 8
PLANE = 16
TILES = 18
STRIP = 16
ITERS = 2
epsilon = 1e-06


def gram_kernel(target_ref, offset_ref, core_ref, own_ref, other_ref, eigen_ref, out_ref, pad_ref):
    core = core_ref[0]
    row = lax.broadcasted_iota(jnp.int32, (SEP_ROWS, IFACE), 0)
    column = lax.broadcasted_iota(jnp.int32, (SEP_ROWS, IFACE), 1)
    distance = row - column
    pad_ref[LEAF_DEV] = jnp.zeros((SEP_ROWS, MODES), jnp.bfloat16)
    for leaf in range(LEAF_DEV):
        inverse = 1.0 / jnp.sqrt(eigen_ref[leaf : leaf + 1, :])
        scaled = ((own_ref[leaf] + other_ref[leaf]) * inverse).astype(jnp.bfloat16)
        placing = (distance == offset_ref[leaf]).astype(jnp.bfloat16)
        pad_ref[leaf] = jnp.dot(placing, scaled, preferred_element_type=jnp.float32).astype(
            jnp.bfloat16
        )
    starts = [pl.multiple_of(32 * g + 16 * core, STRIP) for g in range(PLANE)]
    for s in range(NSEP):
        slots = [jnp.int32(LEAF_DEV), jnp.int32(LEAF_DEV)]
        for leaf in range(LEAF_DEV):
            hit = target_ref[leaf] == s
            later = hit & (slots[0] < LEAF_DEV)
            slots[1] = jnp.where(later, leaf, slots[1])
            slots[0] = jnp.where(hit & jnp.logical_not(later), leaf, slots[0])
        total = None
        for slot in slots:
            rows = jnp.concatenate([pad_ref[slot, pl.ds(x, STRIP), :] for x in starts], axis=0)
            product = lax.dot_general(
                rows, pad_ref[slot], (((1,), (1,)), ((), ())), preferred_element_type=jnp.float32
            )
            total = product if total is None else total + product
        lane = 32 * (s % 4)
        for g in range(PLANE):
            strip = total[g * STRIP : (g + 1) * STRIP, :]
            window = jnp.roll(strip, -32 * g, axis=1) if g else strip
            out_ref[g, 2 * s] = window[:, :128].astype(jnp.bfloat16)
            out_ref[g, 2 * s + 1] = window[:, 128:256].astype(jnp.bfloat16)
            rest = window[:, 256:384]
            rest = jnp.roll(rest, lane, axis=1) if lane else rest
            out_ref[g, 16 + s // 4, :, lane : lane + 32] = rest[:, lane : lane + 32].astype(
                jnp.bfloat16
            )


VMEM = pl.BlockSpec(memory_space=pltpu.VMEM)
SMEM = pl.BlockSpec(memory_space=pltpu.SMEM)


def gram(target, offset, core, own, other, eigen):
    return pl.pallas_call(
        gram_kernel,
        in_specs=[SMEM, SMEM, SMEM, VMEM, VMEM, VMEM],
        out_specs=VMEM,
        out_shape=jax.ShapeDtypeStruct((PLANE, TILES, STRIP, 128), jnp.bfloat16),
        scratch_shapes=[pltpu.VMEM((LEAF_DEV + 1, SEP_ROWS, MODES), jnp.bfloat16)],
        name="gram",
    )(target, offset, core, own, other, eigen)


def iterate_kernel(
    place_ref, own_ref, other_ref, turns_ref, out_ref, norms_ref, kt_ref, m_ref, high_ref, low_ref, x_ref
):
    core, device, sep = place_ref[0], place_ref[1], place_ref[2]
    lane = lax.broadcasted_iota(jnp.int32, (STRIP, 128), 1)
    halved = jnp.where(lane < 32, 0.5, 1.0)
    rest_weight = jnp.where(lane < 32, 0.5, 0.0)
    back = (128 - 32 * (sep & 3)) & 127
    for ref, offset in ((own_ref, 16 * core), (other_ref, 16 * (1 - core))):
        for g in range(PLANE):
            rows = pl.ds(pl.multiple_of(32 * g + offset, STRIP), STRIP)
            kt_ref[rows, :] = ref[g, :, :512]
            x_ref[rows, :] = ref[g, :, 512:768]
            first = ref[g, :, 768:896].astype(jnp.float32) + ref[g, :, 1152:1280].astype(jnp.float32)
            second = ref[g, :, 896:1024].astype(jnp.float32)
            rest = pltpu.roll(ref[g, :, 1024:1152].astype(jnp.float32), back, axis=1)
            window = jnp.concatenate(
                [first * halved, second, rest * rest_weight, jnp.zeros_like(second)], axis=1
            )
            m_ref[rows, :] = jnp.roll(window, 32 * g, axis=1) if g else window
    half = m_ref[...]
    operator = jnp.transpose(kt_ref[...].astype(jnp.float32) - half) - half
    high = operator.astype(jnp.bfloat16)
    high_ref[...] = high
    low_ref[...] = (operator - high.astype(jnp.float32)).astype(jnp.bfloat16)
    for step in range(ITERS):
        summed = jnp.dot(
            high_ref[...], x_ref[...], preferred_element_type=jnp.float32
        ) + jnp.dot(low_ref[...], x_ref[...], preferred_element_type=jnp.float32)
        scale = jnp.sqrt(jnp.sum(summed * summed, 0, keepdims=True) / SEP_ROWS + epsilon)
        norms_ref[0, pl.ds(step, 1), :] = scale
        normed = (summed / scale).astype(jnp.bfloat16)
        if step < ITERS - 1:
            x_ref[...] = jnp.dot(
                normed, turns_ref[step], preferred_element_type=jnp.float32
            ).astype(jnp.bfloat16)
        else:
            x_ref[...] = normed
            rows = x_ref[pl.ds(pl.multiple_of(16 * device, STRIP), STRIP), :]
            out_ref[0] = jnp.dot(
                rows, turns_ref[step], preferred_element_type=jnp.float32
            ).astype(jnp.bfloat16)


def iterate(place, own, other, turns):
    return pl.pallas_call(
        iterate_kernel,
        in_specs=[SMEM, VMEM, VMEM, VMEM],
        out_specs=[VMEM, VMEM],
        out_shape=[
            jax.ShapeDtypeStruct((1, STRIP, COLS), jnp.bfloat16),
            jax.ShapeDtypeStruct((1, ITERS, COLS), jnp.float32),
        ],
        scratch_shapes=[
            pltpu.VMEM((SEP_ROWS, SEP_ROWS), jnp.bfloat16),
            pltpu.VMEM((SEP_ROWS, SEP_ROWS), jnp.float32),
            pltpu.VMEM((SEP_ROWS, SEP_ROWS), jnp.bfloat16),
            pltpu.VMEM((SEP_ROWS, SEP_ROWS), jnp.bfloat16),
            pltpu.VMEM((SEP_ROWS, COLS), jnp.bfloat16),
        ],
        name="iterate",
    )(place, own, other, turns)


SWAP = [(0, 1), (1, 0)]

def per_device(
    modes, coupling, eigenvalues, separator_of, row_offset, stiffness, start_block, rotations
):
    core = lax.axis_index("mode").astype(jnp.int32)
    device = lax.axis_index(("leaf", "mode")).astype(jnp.int32)
    other_eigen = lax.ppermute(eigenvalues, "mode", SWAP)
    eigen = jnp.where(
        core == 0,
        jnp.concatenate([eigenvalues, other_eigen], 1),
        jnp.concatenate([other_eigen, eigenvalues], 1),
    )
    own = jnp.einsum("ldw,ldm->lwm", coupling, modes, preferred_element_type=jnp.float32)
    other = lax.ppermute(own, "mode", SWAP)
    sep = lax.axis_index("sep").astype(jnp.int32)
    pieces = gram(separator_of[:, 0], row_offset, core[None], own, other, eigen)
    got = lax.all_to_all(pieces, "leaf", split_axis=0, concat_axis=0, tiled=True)
    plane = jnp.sum(got.astype(jnp.float32), 0).astype(jnp.bfloat16)
    rest = jnp.broadcast_to(plane[16:, None], (2, 4, STRIP, 128)).reshape(NSEP, 1, STRIP, 128)
    routed = jnp.concatenate([plane[:16].reshape(NSEP, 2, STRIP, 128), rest], 1)
    got = lax.all_to_all(routed, "sep", split_axis=0, concat_axis=0, tiled=True)
    window = jnp.sum(got.astype(jnp.float32), 0)
    high = window.astype(jnp.bfloat16)
    low = (window[0] - high[0].astype(jnp.float32)).astype(jnp.bfloat16)
    packed = jnp.concatenate(
        [stiffness[0].T, start_block[0], high[0], high[1], high[2], low], 1
    )
    mine = lax.all_to_all(
        jnp.broadcast_to(packed[None], (PLANE, *packed.shape)),
        "leaf",
        split_axis=0,
        concat_axis=0,
        tiled=True,
    )
    theirs = lax.ppermute(mine, "mode", SWAP)
    return tuple(iterate(jnp.stack([core, device, sep]), mine, theirs, rotations[0]))


def solution(mesh):
    in_specs = (
        P(("leaf", "sep"), "mode", None),
        P(("leaf", "sep"), "mode", None),
        P(("leaf", "sep"), "mode"),
        P(("leaf", "sep"), None),
        P(("leaf", "sep")),
        P("sep", None, ("leaf", "mode")),
        P("sep", ("leaf", "mode"), None),
        P("sep", None, None, None),
    )
    out_specs = (P("sep", ("leaf", "mode"), None), P("sep", None, None))
    return jax.shard_map(
        per_device, mesh=mesh, in_specs=in_specs, out_specs=out_specs, check_vma=False
    )
```

time: 89.8 us -> 84 us (0.935)
  waiting for transfers between devices: 15.9 us -> 30.5 us
  blocking collectives: 26.8 us -> 15.2 us
  starting transfers between devices: 25.3 us -> 19.8 us
  other arithmetic: 6.28 us -> 2.05 us
    all_to_all x0 -> x2, waiting for transfers between devices: none -> 25.6 us  [the longest x1 18 us: per_device(): lax.all_to_all(pieces, 'leaf', split_axis=0, concat_axis=0, tiled=True)]
    all_to_all x1 -> x0, blocking collectives: 15.9 us -> none  [per_device(): lax.all_to_all(plane_sum, 'sep', split_axis=0, concat_axis=0, tiled=True)]
    ppermute x12 -> x0, starting transfers between devices: 13.4 us -> none  [the longest x4 5.68 us: ring_scatter(): relay_down, relay_up = (down(opposite[0]), up(opposite[1]))]
    all_to_all x0 -> x2, starting transfers between devices: none -> 13.3 us  [the longest x1 8.18 us: per_device(): got = lax.all_to_all(routed, 'sep', split_axis=0, concat_axis=0, tiled=True)]
    ppermute x12 -> x0, waiting for transfers between devices: 12 us -> none  [the longest x2 4.93 us: ring_scatter(): up(add(ahead[1], relay_up))]
    ppermute x1, starting transfers between devices: 8.5 us -> 3.14 us  [per_device(): theirs = lax.ppermute(mine, 'mode', SWAP)]
    convert_element_type x8 -> x1, other arithmetic: 4.33 us -> 0.01 us  [per_device(): high = window.astype(jnp.bfloat16)]
    all_to_all x1, blocking collectives: 10.9 us -> 15.2 us  [per_device(): lax.all_to_all(jnp.broadcast_to(packed[None], (PLANE, *packed.shape)), 'l...]
  transfers between devices with their start and end apart: 15 -> 5, of which waited for: 9 -> 4; matrix products, arithmetic and copies ran while one was open for 7% -> 1% of each run, Pallas kernels for 0% -> 0%
where the time goes in v4:
time: 84 us; the launch traced here: 83.7 us
  waiting for transfers between devices  30.5 us (36%)
  starting transfers between devices  19.8 us (24%)
  blocking collectives  15.2 us (18%)
  Pallas kernels  9.58 us (11%)
  matrix products  4.87 us (6%)
  other arithmetic  2.05 us (2%)
  local copies, waits for them, and re-layouts  0.95 us (1%)
    all_to_all x1, waiting for transfers between devices, per_device(): lax.all_to_all(pieces, 'leaf', split_axis=0, concat_axis=0, tiled=True)  18 us
    all_to_all x1, blocking collectives, per_device(): lax.all_to_all(jnp.broadcast_to(packed[None], (PLANE, *packed.shape)), 'l...  15.2 us
    all_to_all x1, starting transfers between devices, per_device(): got = lax.all_to_all(routed, 'sep', split_axis=0, concat_axis=0, tiled=True)  8.18 us
    all_to_all x1, waiting for transfers between devices, per_device(): got = lax.all_to_all(routed, 'sep', split_axis=0, concat_axis=0, tiled=True)  7.56 us
    pallas_call x1, Pallas kernels, gram(): pl.pallas_call(gram_kernel, in_specs=[SMEM, SMEM, SMEM, VMEM, VMEM, VMEM]...  5.53 us
    all_to_all x1, starting transfers between devices, per_device(): lax.all_to_all(pieces, 'leaf', split_axis=0, concat_axis=0, tiled=True)  5.09 us
    dot_general x1, matrix products, per_device(): jnp.einsum('ldw,ldm->lwm', coupling, modes, preferred_element_type=jnp.fl...  4.87 us
    pallas_call x1, Pallas kernels, iterate(): pl.pallas_call(iterate_kernel, in_specs=[SMEM, VMEM, VMEM, VMEM], out_spe...  4.05 us
  transfers between devices with their start and end apart: 5, of which 4 were waited for; matrix products, arithmetic and copies ran while one was open for 1% of the time, Pallas kernels for 0%

profile of v4, /device:TPU:1, one launch (start us, length us, event | category | flops | bytes accessed | tf_op | source)
XLA Modules:
  0.0 83.7 jit_solution(11116846067659915901)
XLA Ops:
  0.6 0.0 copy-start.5
  0.6 4.9 %fusion.2.own_ref = f32[8,256,256]{2,1,0:T(8,128)S(1)} fusion(bf16[8,1024,256]{2,1,0:T(8,128)(2,1)} %param.9, bf16[8,1024,256]{2,1,0:T(8,128)(2,1)} %param.8), kind=kOutput, calls=%fused_computation.16 | convolution fusion | flops 1073741824 | bytes 10485760 | tf_op jit(solution)/shard_map/ldw,ldm->lwm/dot_general | solution.py:156
  5.5 0.0 copy-start
  5.5 0.0 copy-start.3
  5.5 3.3 %collective-permute-start = (f32[8,256,256]{2,1,0:T(8,128)S(1)}, f32[8,256,256]{2,1,0:T(8,128)}, u32[]{:S(2)}, u32[]{:S(2)}) collective-permute-start(f32[8,256,256]{2,1,0:T(8,128)S(1)} %fusion.2.own_ref), channel_id=1, source_target_pairs={{0,1},{1,0},{2,3},{3,2},{4,5},{5,4},{6,7},{7,6},{8,9},{9,8},{10,11... | collective-permute-start | bytes 6291464 | tf_op jit(solution)/shard_map/ppermute | solution.py:157
  8.8 0.0 copy-done.5
  8.8 0.1 collective-permute-start.1
  8.9 3.8 %collective-permute-done.1 = f32[8,128]{1,0:T(8,128)S(1)} collective-permute-done((f32[8,128]{1,0:T(8,128)S(1)}, f32[8,128]{1,0:T(8,128)S(1)}, u32[]{:S(2)}, u32[]{:S(2)}) %collective-permute-start.1) | collective-permute-done | bytes 4128 | tf_op jit(solution)/shard_map/ppermute | solution.py:150
  12.7 0.6 maximum_select_fusion.eigen_ref
  13.3 0.0 collective-permute-done.other_ref
  13.3 0.0 copy-done
  13.4 0.0 copy-start.4
  13.4 5.5 %gram.1 = bf16[16,18,16,128]{3,2,1,0:T(8,128)(2,1)} custom-call(s32[8]{0:T(128)} %bitcast.40, s32[8]{0:T(128)} %offset_ref.1, s32[1]{0:T(128)} %bitcast.core_ref, f32[8,256,256]{2,1,0:T(8,128)} %copy-done, f32[8,256,256]{2,1,0:T(8,128)} %collective-permute-done.other_ref, f32[8,256]{1,0:T(8,128)} %maximum_select_fusion.eigen_ref), custom_call_target="tpu_custom_call" | custom-call | tf_op jit(solution)/shard_map/gram/pallas_call | solution.py:69
  18.9 5.1 %all-to-all-start = ((bf16[16,18,16,128]{3,2,1,0:T(8,128)(2,1)}), bf16[16,18,16,128]{3,2,1,0:T(8,128)(2,1)S(1)}, u32[]{:S(2)}, u32[]{:S(2)}) async-start(bf16[16,18,16,128]{3,2,1,0:T(8,128)(2,1)} %gram.1), calls=%async_computation | async-start | bytes 2359296 | tf_op jit(solution)/shard_map/all_to_all | solution.py:160
  24.0 0.0 copy-done.3
  24.0 18.0 %all-to-all-done = bf16[16,18,16,128]{3,2,1,0:T(8,128)(2,1)S(1)} async-done(((bf16[16,18,16,128]{3,2,1,0:T(8,128)(2,1)}), bf16[16,18,16,128]{3,2,1,0:T(8,128)(2,1)S(1)}, u32[]{:S(2)}, u32[]{:S(2)}) %all-to-all-start) | async-done | bytes 1179680 | tf_op jit(solution)/shard_map/all_to_all | solution.py:160
  42.0 0.2 reduce_sum.21
  42.2 0.6 pad_maximum_fusion
  42.8 8.2 %all-to-all-start.1 = ((bf16[8,3,16,128]{3,2,1,0:T(8,128)(2,1)}), bf16[8,3,16,128]{3,2,1,0:T(8,128)(2,1)S(1)}, u32[]{:S(2)}, u32[]{:S(2)}) async-start(bf16[8,3,16,128]{3,2,1,0:T(8,128)(2,1)} %pad_maximum_fusion), calls=%async_computation.1 | async-start | bytes 196608 | tf_op jit(solution)/shard_map/all_to_all | solution.py:164
  51.0 0.0 copy-done.4
  51.0 7.6 %all-to-all-done.1 = bf16[8,3,16,128]{3,2,1,0:T(8,128)(2,1)S(1)} async-done(((bf16[8,3,16,128]{3,2,1,0:T(8,128)(2,1)}), bf16[8,3,16,128]{3,2,1,0:T(8,128)(2,1)S(1)}, u32[]{:S(2)}, u32[]{:S(2)}) %all-to-all-start.1) | async-done | bytes 98336 | tf_op jit(solution)/shard_map/all_to_all | solution.py:164
  58.7 15.2 %all_to_all.15.own_ref = bf16[16,16,1280]{2,1,0:T(8,128)(2,1)S(1)} all-to-all(bf16[16,16,1280]{2,1,0:T(8,128)(2,1)S(1)} %broadcast_in_dim.5), channel_id=1, replica_groups=mesh['leaf'=16,'sep'=8,'mode'=2] {'leaf'}, dimensions={0} | all-to-all | bytes 1310720 | tf_op jit(solution)/shard_map/all_to_all | solution.py:171
  73.9 0.0 copy-start.1
  73.9 3.1 %collective-permute-start.2 = (bf16[16,16,1280]{2,1,0:T(8,128)(2,1)S(1)}, bf16[16,16,1280]{2,1,0:T(8,128)(2,1)S(1)}, u32[]{:S(2)}, u32[]{:S(2)}) collective-permute-start(bf16[16,16,1280]{2,1,0:T(8,128)(2,1)S(1)} %all_to_all.15.own_ref), channel_id=1, source_target_pairs={{0,1},{1,0},{2,3},{3,2},{4,5},{5,4},{6,7},{7,6},{8,9},{9,8},{10,11... | collective-permute-start | bytes 1966088 | tf_op jit(solution)/shard_map/ppermute | solution.py:178
  77.0 0.6 pad_add_fusion.place_ref
  77.7 1.1 %collective-permute-done.2.other_ref = bf16[16,16,1280]{2,1,0:T(8,128)(2,1)S(1)} collective-permute-done((bf16[16,16,1280]{2,1,0:T(8,128)(2,1)S(1)}, bf16[16,16,1280]{2,1,0:T(8,128)(2,1)S(1)}, u32[]{:S(2)}, u32[]{:S(2)}) %collective-permute-start.2) | collective-permute-done | bytes 655392 | tf_op jit(solution)/shard_map/ppermute | solution.py:178
  78.8 0.0 copy-start.2
  78.8 0.0 copy-done.1
  78.8 0.8 copy-done.2
  79.6 4.0 %iterate.1 = (bf16[1,16,256]{2,1,0:T(8,128)(2,1)}, f32[1,2,256]{2,1,0:T(2,128)}) custom-call(s32[3]{0:T(128)} %pad_add_fusion.place_ref, bf16[16,16,1280]{2,1,0:T(8,128)(2,1)} %copy-done.1, bf16[16,16,1280]{2,1,0:T(8,128)(2,1)} %copy-done.2, bf16[2,256,256]{2,1,0:T(8,128)(2,1)} %bitcast.38), custom_call_target="tpu_custom_call" | custom-call | tf_op jit(solution)/shard_map/iterate/pallas_call | solution.py:124
  (12 shorter events, 0.1 us)
Async XLA Ops:
  0.6 8.2 %copy-start.5 = (f32[8,128]{1,0:T(8,128)S(1)}, f32[8,128]{1,0:T(8,128)}, u32[]{:S(2)}) copy-start(f32[8,128]{1,0:T(8,128)} %param.10) | copy-start | bytes 12292
  5.5 7.8 %copy-start = (f32[8,256,256]{2,1,0:T(8,128)}, f32[8,256,256]{2,1,0:T(8,128)S(1)}, u32[]{:S(2)}) copy-start(f32[8,256,256]{2,1,0:T(8,128)S(1)} %fusion.2.own_ref) | copy-start | bytes 6291460
  5.5 18.5 %copy-start.3 = (bf16[1,512,16]{1,2,0:T(8,128)(2,1)S(1)}, bf16[1,512,16]{1,2,0:T(8,128)(2,1)}, u32[]{:S(2)}) copy-start(bf16[1,512,16]{1,2,0:T(8,128)(2,1)} %param.13) | copy-start | bytes 49156
  5.5 7.8 %collective-permute-start = (f32[8,256,256]{2,1,0:T(8,128)S(1)}, f32[8,256,256]{2,1,0:T(8,128)}, u32[]{:S(2)}, u32[]{:S(2)}) collective-permute-start(f32[8,256,256]{2,1,0:T(8,128)S(1)} %fusion.2.own_ref), channel_id=1, source_target_pairs={{0,1},{1,0},{2,3},{3,2},{4,5},{5,4},{6,7},{7,6},{8,9},{9,8},{10,11... | collective-permute-start | bytes 6291464 | tf_op jit(solution)/shard_map/ppermute | solution.py:157
  8.8 3.9 %collective-permute-start.1 = (f32[8,128]{1,0:T(8,128)S(1)}, f32[8,128]{1,0:T(8,128)S(1)}, u32[]{:S(2)}, u32[]{:S(2)}) collective-permute-start(f32[8,128]{1,0:T(8,128)S(1)} %copy-done.5), channel_id=1, source_target_pairs={{0,1},{1,0},{2,3},{3,2},{4,5},{5,4},{6,7},{7,6},{8,9},{9,8},{10,11... | collective-permute-start | bytes 12296 | tf_op jit(solution)/shard_map/ppermute | solution.py:150
  13.4 37.7 %copy-start.4 = (bf16[1,16,256]{2,1,0:T(8,128)(2,1)S(1)}, bf16[1,16,256]{2,1,0:T(8,128)(2,1)}, u32[]{:S(2)}) copy-start(bf16[1,16,256]{2,1,0:T(8,128)(2,1)} %param.14) | copy-start | bytes 24580
  18.9 23.1 %all-to-all-start = ((bf16[16,18,16,128]{3,2,1,0:T(8,128)(2,1)}), bf16[16,18,16,128]{3,2,1,0:T(8,128)(2,1)S(1)}, u32[]{:S(2)}, u32[]{:S(2)}) async-start(bf16[16,18,16,128]{3,2,1,0:T(8,128)(2,1)} %gram.1), calls=%async_computation | async-start | bytes 2359296 | tf_op jit(solution)/shard_map/all_to_all | solution.py:160
  42.8 15.8 %all-to-all-start.1 = ((bf16[8,3,16,128]{3,2,1,0:T(8,128)(2,1)}), bf16[8,3,16,128]{3,2,1,0:T(8,128)(2,1)S(1)}, u32[]{:S(2)}, u32[]{:S(2)}) async-start(bf16[8,3,16,128]{3,2,1,0:T(8,128)(2,1)} %pad_maximum_fusion), calls=%async_computation.1 | async-start | bytes 196608 | tf_op jit(solution)/shard_map/all_to_all | solution.py:164
  73.9 4.9 %copy-start.1 = (bf16[16,16,1280]{2,1,0:T(8,128)(2,1)}, bf16[16,16,1280]{2,1,0:T(8,128)(2,1)S(1)}, u32[]{:S(2)}) copy-start(bf16[16,16,1280]{2,1,0:T(8,128)(2,1)S(1)} %all_to_all.15.own_ref) | copy-start | bytes 1966084
  73.9 4.9 %collective-permute-start.2 = (bf16[16,16,1280]{2,1,0:T(8,128)(2,1)S(1)}, bf16[16,16,1280]{2,1,0:T(8,128)(2,1)S(1)}, u32[]{:S(2)}, u32[]{:S(2)}) collective-permute-start(bf16[16,16,1280]{2,1,0:T(8,128)(2,1)S(1)} %all_to_all.15.own_ref), channel_id=1, source_target_pairs={{0,1},{1,0},{2,3},{3,2},{4,5},{5,4},{6,7},{7,6},{8,9},{9,8},{10,11... | collective-permute-start | bytes 1966088 | tf_op jit(solution)/shard_map/ppermute | solution.py:178
  78.8 0.8 %copy-start.2 = (bf16[16,16,1280]{2,1,0:T(8,128)(2,1)}, bf16[16,16,1280]{2,1,0:T(8,128)(2,1)S(1)}, u32[]{:S(2)}) copy-start(bf16[16,16,1280]{2,1,0:T(8,128)(2,1)S(1)} %collective-permute-done.2.other_ref) | copy-start | bytes 1966084

commit v5 on v4

--- a/solution.py
+++ b/solution.py
@@ -20,15 +20,23 @@
 epsilon = 1e-06
 
 
-def gram_kernel(target_ref, offset_ref, core_ref, own_ref, other_ref, eigen_ref, out_ref, pad_ref):
+def gram_kernel(
+    target_ref, offset_ref, core_ref, own_ref, other_ref, eigen_ref, other_eigen_ref, out_ref, pad_ref
+):
     core = core_ref[0]
     row = lax.broadcasted_iota(jnp.int32, (SEP_ROWS, IFACE), 0)
     column = lax.broadcasted_iota(jnp.int32, (SEP_ROWS, IFACE), 1)
     distance = row - column
     pad_ref[LEAF_DEV] = jnp.zeros((SEP_ROWS, MODES), jnp.bfloat16)
+    mine, theirs = eigen_ref[...], other_eigen_ref[...]
+    eigen = jnp.concatenate(
+        [jnp.where(core == 0, mine, theirs), jnp.where(core == 0, theirs, mine)], axis=1
+    )
+    inverses = 1.0 / jnp.sqrt(eigen)
     for leaf in range(LEAF_DEV):
-        inverse = 1.0 / jnp.sqrt(eigen_ref[leaf : leaf + 1, :])
-        scaled = ((own_ref[leaf] + other_ref[leaf]) * inverse).astype(jnp.bfloat16)
+        inverse = inverses[leaf : leaf + 1, :]
+        product = own_ref[leaf].astype(jnp.float32) + other_ref[leaf].astype(jnp.float32)
+        scaled = (product * inverse).astype(jnp.bfloat16)
         placing = (distance == offset_ref[leaf]).astype(jnp.bfloat16)
         pad_ref[leaf] = jnp.dot(placing, scaled, preferred_element_type=jnp.float32).astype(
             jnp.bfloat16
@@ -61,19 +69,23 @@
             )
 
 
+def in_vmem(x):
+    return pltpu.with_memory_space_constraint(x, pltpu.VMEM)
+
+
 VMEM = pl.BlockSpec(memory_space=pltpu.VMEM)
 SMEM = pl.BlockSpec(memory_space=pltpu.SMEM)
 
 
-def gram(target, offset, core, own, other, eigen):
+def gram(target, offset, core, *arrays):
     return pl.pallas_call(
         gram_kernel,
-        in_specs=[SMEM, SMEM, SMEM, VMEM, VMEM, VMEM],
+        in_specs=[SMEM, SMEM, SMEM, VMEM, VMEM, VMEM, VMEM],
         out_specs=VMEM,
-        out_shape=jax.ShapeDtypeStruct((PLANE, TILES, STRIP, 128), jnp.bfloat16),
+        out_shape=pltpu.VMEM((PLANE, TILES, STRIP, 128), jnp.bfloat16),
         scratch_shapes=[pltpu.VMEM((LEAF_DEV + 1, SEP_ROWS, MODES), jnp.bfloat16)],
         name="gram",
-    )(target, offset, core, own, other, eigen)
+    )(target, offset, core, *[in_vmem(x) for x in arrays])
 
 
 def iterate_kernel(
@@ -137,7 +149,7 @@
             pltpu.VMEM((SEP_ROWS, COLS), jnp.bfloat16),
         ],
         name="iterate",
-    )(place, own, other, turns)
+    )(place, in_vmem(own), in_vmem(other), turns)
 
 
 SWAP = [(0, 1), (1, 0)]
@@ -148,15 +160,12 @@
     core = lax.axis_index("mode").astype(jnp.int32)
     device = lax.axis_index(("leaf", "mode")).astype(jnp.int32)
     other_eigen = lax.ppermute(eigenvalues, "mode", SWAP)
-    eigen = jnp.where(
-        core == 0,
-        jnp.concatenate([eigenvalues, other_eigen], 1),
-        jnp.concatenate([other_eigen, eigenvalues], 1),
-    )
-    own = jnp.einsum("ldw,ldm->lwm", coupling, modes, preferred_element_type=jnp.float32)
+    own = jnp.einsum("ldw,ldm->lwm", coupling, modes, preferred_element_type=jnp.float32).astype(
+        jnp.bfloat16
+    )
     other = lax.ppermute(own, "mode", SWAP)
     sep = lax.axis_index("sep").astype(jnp.int32)
-    pieces = gram(separator_of[:, 0], row_offset, core[None], own, other, eigen)
+    pieces = gram(separator_of[:, 0], row_offset, core[None], own, other, eigenvalues, other_eigen)
     got = lax.all_to_all(pieces, "leaf", split_axis=0, concat_axis=0, tiled=True)
     plane = jnp.sum(got.astype(jnp.float32), 0).astype(jnp.bfloat16)
     rest = jnp.broadcast_to(plane[16:, None], (2, 4, STRIP, 128)).reshape(NSEP, 1, STRIP, 128)

time: 84 us -> 79 us (0.940)
  Pallas kernels: 9.58 us -> 7.64 us
  waiting for transfers between devices: 30.5 us -> 28.9 us
  local copies, waits for them, and re-layouts: 0.95 us -> 0.11 us
    ppermute x1, waiting for transfers between devices: 3.81 us -> 2.18 us  [per_device(): other_eigen = lax.ppermute(eigenvalues, 'mode', SWAP)]
    pallas_call x1, Pallas kernels: 5.53 us -> 3.99 us  [gram(): pl.pallas_call(gram_kernel, in_specs=[SMEM, SMEM, SMEM, VMEM, VMEM, VMEM,...]
    unnamed x17 -> x11, local copies, waits for them, and re-layouts: 0.89 us -> 0.05 us
where the time goes in v5:
time: 79 us; the launch traced here: 78.7 us
  waiting for transfers between devices  28.9 us (37%)
  starting transfers between devices  19.8 us (25%)
  blocking collectives  15.2 us (19%)
  Pallas kernels  7.64 us (10%)
  matrix products  4.87 us (6%)
  other arithmetic  1.42 us (2%)
    all_to_all x1, waiting for transfers between devices, per_device(): lax.all_to_all(pieces, 'leaf', split_axis=0, concat_axis=0, tiled=True)  18 us
    all_to_all x1, blocking collectives, per_device(): lax.all_to_all(jnp.broadcast_to(packed[None], (PLANE, *packed.shape)), 'l...  15.2 us
    all_to_all x1, starting transfers between devices, per_device(): got = lax.all_to_all(routed, 'sep', split_axis=0, concat_axis=0, tiled=True)  8.18 us
    all_to_all x1, waiting for transfers between devices, per_device(): got = lax.all_to_all(routed, 'sep', split_axis=0, concat_axis=0, tiled=True)  7.56 us
    all_to_all x1, starting transfers between devices, per_device(): lax.all_to_all(pieces, 'leaf', split_axis=0, concat_axis=0, tiled=True)  5.05 us
    dot_general x1, matrix products, per_device(): jnp.einsum('ldw,ldm->lwm', coupling, modes, preferred_element_type=jnp.fl...  4.87 us
    pallas_call x1, Pallas kernels, gram(): pl.pallas_call(gram_kernel, in_specs=[SMEM, SMEM, SMEM, VMEM, VMEM, VMEM,...  3.99 us
    pallas_call x1, Pallas kernels, iterate(): pl.pallas_call(iterate_kernel, in_specs=[SMEM, VMEM, VMEM, VMEM], out_spe...  3.66 us
  transfers between devices with their start and end apart: 5, of which 4 were waited for; matrix products, arithmetic and copies ran while one was open for 1% of the time, Pallas kernels for 0%

profile of v5, /device:TPU:1, one launch (start us, length us, event | category | flops | bytes accessed | tf_op | source)
XLA Modules:
  0.0 78.7 jit_solution(613328935178483297)
XLA Ops:
  0.6 0.0 copy-start
  0.6 4.9 %convolution_convert_fusion.own_ref = bf16[8,256,256]{2,1,0:T(8,128)(2,1)S(1)} fusion(bf16[8,1024,256]{2,1,0:T(8,128)(2,1)} %param.9, bf16[8,1024,256]{2,1,0:T(8,128)(2,1)} %param.8), kind=kOutput, calls=%fused_computation | convolution fusion | flops 1074266112 | bytes 9437184 | tf_op jit(solution)/shard_map/ldw,ldm->lwm/dot_general | solution.py:163
  5.5 0.0 copy-start.1
  5.5 0.0 copy-start.2
  5.5 3.3 %collective-permute-start = (bf16[8,256,256]{2,1,0:T(8,128)(2,1)S(1)}, bf16[8,256,256]{2,1,0:T(8,128)(2,1)S(1)}, u32[]{:S(2)}, u32[]{:S(2)}) collective-permute-start(bf16[8,256,256]{2,1,0:T(8,128)(2,1)S(1)} %convolution_convert_fusion.own_ref), channel_id=1, source_target_pairs={{0,1},{1,0},{2,3},{3,2},{4,5},{5,4},{6,7},{7,6},{8,9},{9,8},{10,11... | collective-permute-start | bytes 3145736 | tf_op jit(solution)/shard_map/ppermute | solution.py:166
  8.8 0.0 copy-done
  8.8 0.1 collective-permute-start.1
  8.9 2.2 %collective-permute-done.1.other_eigen_ref = f32[8,128]{1,0:T(8,128)S(1)} collective-permute-done((f32[8,128]{1,0:T(8,128)S(1)}, f32[8,128]{1,0:T(8,128)S(1)}, u32[]{:S(2)}, u32[]{:S(2)}) %collective-permute-start.1) | collective-permute-done | bytes 4128 | tf_op jit(solution)/shard_map/ppermute | solution.py:162
  11.1 0.0 collective-permute-done.other_ref
  11.1 4.0 %gram.1 = bf16[16,18,16,128]{3,2,1,0:T(8,128)(2,1)} custom-call(s32[8]{0:T(128)} %bitcast.40, s32[8]{0:T(128)} %offset_ref.1, s32[1]{0:T(128)} %bitcast.core_ref, bf16[8,256,256]{2,1,0:T(8,128)(2,1)S(1)} %convolution_convert_fusion.own_ref, bf16[8,256,256]{2,1,0:T(8,128)(2,1)S(1)} %collective-permute-done.other_ref, f32[8,128]{1,0:T(8,128)S(1)} %copy-done, ...), custom_call_target="tpu_custom_call" | custom-call | tf_op jit(solution)/shard_map/gram/pallas_call | solution.py:81
  15.1 5.1 %all-to-all-start = ((bf16[16,18,16,128]{3,2,1,0:T(8,128)(2,1)}), bf16[16,18,16,128]{3,2,1,0:T(8,128)(2,1)S(1)}, u32[]{:S(2)}, u32[]{:S(2)}) async-start(bf16[16,18,16,128]{3,2,1,0:T(8,128)(2,1)} %gram.1), calls=%async_computation | async-start | bytes 2359296 | tf_op jit(solution)/shard_map/all_to_all | solution.py:169
  20.2 0.0 copy-done.1
  20.2 18.0 %all-to-all-done = bf16[16,18,16,128]{3,2,1,0:T(8,128)(2,1)S(1)} async-done(((bf16[16,18,16,128]{3,2,1,0:T(8,128)(2,1)}), bf16[16,18,16,128]{3,2,1,0:T(8,128)(2,1)S(1)}, u32[]{:S(2)}, u32[]{:S(2)}) %all-to-all-start) | async-done | bytes 1179680 | tf_op jit(solution)/shard_map/all_to_all | solution.py:169
  38.2 0.2 reduce_sum.21
  38.4 0.6 pad_maximum_fusion
  39.1 8.2 %all-to-all-start.1 = ((bf16[8,3,16,128]{3,2,1,0:T(8,128)(2,1)}), bf16[8,3,16,128]{3,2,1,0:T(8,128)(2,1)S(1)}, u32[]{:S(2)}, u32[]{:S(2)}) async-start(bf16[8,3,16,128]{3,2,1,0:T(8,128)(2,1)} %pad_maximum_fusion), calls=%async_computation.1 | async-start | bytes 196608 | tf_op jit(solution)/shard_map/all_to_all | solution.py:173
  47.3 0.0 copy-done.2
  47.3 7.6 %all-to-all-done.1 = bf16[8,3,16,128]{3,2,1,0:T(8,128)(2,1)S(1)} async-done(((bf16[8,3,16,128]{3,2,1,0:T(8,128)(2,1)}), bf16[8,3,16,128]{3,2,1,0:T(8,128)(2,1)S(1)}, u32[]{:S(2)}, u32[]{:S(2)}) %all-to-all-start.1) | async-done | bytes 98336 | tf_op jit(solution)/shard_map/all_to_all | solution.py:173
  55.0 15.2 %all_to_all.15.own_ref = bf16[16,16,1280]{2,1,0:T(8,128)(2,1)S(1)} all-to-all(bf16[16,16,1280]{2,1,0:T(8,128)(2,1)S(1)} %broadcast_in_dim.5), channel_id=1, replica_groups=mesh['leaf'=16,'sep'=8,'mode'=2] {'leaf'}, dimensions={0} | all-to-all | bytes 1310720 | tf_op jit(solution)/shard_map/all_to_all | solution.py:180
  70.1 3.1 %collective-permute-start.2 = (bf16[16,16,1280]{2,1,0:T(8,128)(2,1)S(1)}, bf16[16,16,1280]{2,1,0:T(8,128)(2,1)S(1)}, u32[]{:S(2)}, u32[]{:S(2)}) collective-permute-start(bf16[16,16,1280]{2,1,0:T(8,128)(2,1)S(1)} %all_to_all.15.own_ref), channel_id=1, source_target_pairs={{0,1},{1,0},{2,3},{3,2},{4,5},{5,4},{6,7},{7,6},{8,9},{9,8},{10,11... | collective-permute-start | bytes 1966088 | tf_op jit(solution)/shard_map/ppermute | solution.py:187
  73.3 0.6 pad_add_fusion.place_ref
  73.9 1.1 %collective-permute-done.2.other_ref = bf16[16,16,1280]{2,1,0:T(8,128)(2,1)S(1)} collective-permute-done((bf16[16,16,1280]{2,1,0:T(8,128)(2,1)S(1)}, bf16[16,16,1280]{2,1,0:T(8,128)(2,1)S(1)}, u32[]{:S(2)}, u32[]{:S(2)}) %collective-permute-start.2) | collective-permute-done | bytes 655392 | tf_op jit(solution)/shard_map/ppermute | solution.py:187
  75.0 3.7 %iterate.1 = (bf16[1,16,256]{2,1,0:T(8,128)(2,1)}, f32[1,2,256]{2,1,0:T(2,128)}) custom-call(s32[3]{0:T(128)} %pad_add_fusion.place_ref, bf16[16,16,1280]{2,1,0:T(8,128)(2,1)S(1)} %all_to_all.15.own_ref, bf16[16,16,1280]{2,1,0:T(8,128)(2,1)S(1)} %collective-permute-done.2.other_ref, bf16[2,256,256]{2,1,0:T(8,128)(2,1)} %bitcast.38), custom_call_target="tpu_custom_call" | custom-call | tf_op jit(solution)/shard_map/iterate/pallas_call | solution.py:136
  (12 shorter events, 0.1 us)
Async XLA Ops:
  0.6 8.2 %copy-start = (f32[8,128]{1,0:T(8,128)S(1)}, f32[8,128]{1,0:T(8,128)}, u32[]{:S(2)}) copy-start(f32[8,128]{1,0:T(8,128)} %eigen_ref.1) | copy-start | bytes 12292
  5.5 14.7 %copy-start.1 = (bf16[1,512,16]{1,2,0:T(8,128)(2,1)S(1)}, bf16[1,512,16]{1,2,0:T(8,128)(2,1)}, u32[]{:S(2)}) copy-start(bf16[1,512,16]{1,2,0:T(8,128)(2,1)} %param.13) | copy-start | bytes 49156
  5.5 41.7 %copy-start.2 = (bf16[1,16,256]{2,1,0:T(8,128)(2,1)S(1)}, bf16[1,16,256]{2,1,0:T(8,128)(2,1)}, u32[]{:S(2)}) copy-start(bf16[1,16,256]{2,1,0:T(8,128)(2,1)} %param.14) | copy-start | bytes 24580
  5.5 5.6 %collective-permute-start = (bf16[8,256,256]{2,1,0:T(8,128)(2,1)S(1)}, bf16[8,256,256]{2,1,0:T(8,128)(2,1)S(1)}, u32[]{:S(2)}, u32[]{:S(2)}) collective-permute-start(bf16[8,256,256]{2,1,0:T(8,128)(2,1)S(1)} %convolution_convert_fusion.own_ref), channel_id=1, source_target_pairs={{0,1},{1,0},{2,3},{3,2},{4,5},{5,4},{6,7},{7,6},{8,9},{9,8},{10,11... | collective-permute-start | bytes 3145736 | tf_op jit(solution)/shard_map/ppermute | solution.py:166
  8.8 2.3 %collective-permute-start.1 = (f32[8,128]{1,0:T(8,128)S(1)}, f32[8,128]{1,0:T(8,128)S(1)}, u32[]{:S(2)}, u32[]{:S(2)}) collective-permute-start(f32[8,128]{1,0:T(8,128)S(1)} %copy-done), channel_id=1, source_target_pairs={{0,1},{1,0},{2,3},{3,2},{4,5},{5,4},{6,7},{7,6},{8,9},{9,8},{10,11... | collective-permute-start | bytes 12296 | tf_op jit(solution)/shard_map/ppermute | solution.py:162
  15.1 23.1 %all-to-all-start = ((bf16[16,18,16,128]{3,2,1,0:T(8,128)(2,1)}), bf16[16,18,16,128]{3,2,1,0:T(8,128)(2,1)S(1)}, u32[]{:S(2)}, u32[]{:S(2)}) async-start(bf16[16,18,16,128]{3,2,1,0:T(8,128)(2,1)} %gram.1), calls=%async_computation | async-start | bytes 2359296 | tf_op jit(solution)/shard_map/all_to_all | solution.py:169
  39.1 15.8 %all-to-all-start.1 = ((bf16[8,3,16,128]{3,2,1,0:T(8,128)(2,1)}), bf16[8,3,16,128]{3,2,1,0:T(8,128)(2,1)S(1)}, u32[]{:S(2)}, u32[]{:S(2)}) async-start(bf16[8,3,16,128]{3,2,1,0:T(8,128)(2,1)} %pad_maximum_fusion), calls=%async_computation.1 | async-start | bytes 196608 | tf_op jit(solution)/shard_map/all_to_all | solution.py:173
  70.1 4.9 %collective-permute-start.2 = (bf16[16,16,1280]{2,1,0:T(8,128)(2,1)S(1)}, bf16[16,16,1280]{2,1,0:T(8,128)(2,1)S(1)}, u32[]{:S(2)}, u32[]{:S(2)}) collective-permute-start(bf16[16,16,1280]{2,1,0:T(8,128)(2,1)S(1)} %all_to_all.15.own_ref), channel_id=1, source_target_pairs={{0,1},{1,0},{2,3},{3,2},{4,5},{5,4},{6,7},{7,6},{8,9},{9,8},{10,11... | collective-permute-start | bytes 1966088 | tf_op jit(solution)/shard_map/ppermute | solution.py:187

commit v6 on v5

--- a/solution.py
+++ b/solution.py
@@ -21,27 +21,43 @@
 
 
 def gram_kernel(
-    target_ref, offset_ref, core_ref, own_ref, other_ref, eigen_ref, other_eigen_ref, out_ref, pad_ref
+    target_ref, offset_ref, core_ref, own_ref, other_ref, eigen_ref, other_eigen_ref, out_ref, window_ref, *pad_refs
 ):
     core = core_ref[0]
-    row = lax.broadcasted_iota(jnp.int32, (SEP_ROWS, IFACE), 0)
-    column = lax.broadcasted_iota(jnp.int32, (SEP_ROWS, IFACE), 1)
+    reach = IFACE + STRIP
+    row = lax.broadcasted_iota(jnp.int32, (reach, IFACE), 0)
+    column = lax.broadcasted_iota(jnp.int32, (reach, IFACE), 1)
     distance = row - column
-    pad_ref[LEAF_DEV] = jnp.zeros((SEP_ROWS, MODES), jnp.bfloat16)
     mine, theirs = eigen_ref[...], other_eigen_ref[...]
     eigen = jnp.concatenate(
         [jnp.where(core == 0, mine, theirs), jnp.where(core == 0, theirs, mine)], axis=1
     )
     inverses = 1.0 / jnp.sqrt(eigen)
+    starts = [pl.multiple_of(32 * g + 16 * core, STRIP) for g in range(PLANE)]
+    window_ref[LEAF_DEV] = jnp.zeros((PLANE, STRIP, 384), jnp.float32)
     for leaf in range(LEAF_DEV):
-        inverse = inverses[leaf : leaf + 1, :]
         product = own_ref[leaf].astype(jnp.float32) + other_ref[leaf].astype(jnp.float32)
-        scaled = (product * inverse).astype(jnp.bfloat16)
-        placing = (distance == offset_ref[leaf]).astype(jnp.bfloat16)
-        pad_ref[leaf] = jnp.dot(placing, scaled, preferred_element_type=jnp.float32).astype(
-            jnp.bfloat16
+        scaled = (product * inverses[leaf : leaf + 1, :]).astype(jnp.bfloat16)
+        offset = offset_ref[leaf]
+        aligned = pl.multiple_of((offset >> 4) << 4, STRIP)
+        placing = (distance == (offset & 15)).astype(jnp.bfloat16)
+        pad_ref = pad_refs[leaf]
+        pad_ref[...] = jnp.zeros_like(pad_ref)
+        pad_ref[pl.ds(aligned, reach), :] = jnp.dot(
+            placing, scaled, preferred_element_type=jnp.float32
+        ).astype(jnp.bfloat16)
+    for leaf in range(LEAF_DEV):
+        pad_ref = pad_refs[leaf]
+        rows = jnp.concatenate([pad_ref[pl.ds(x, STRIP), :] for x in starts], axis=0)
+        total = lax.dot_general(
+            rows,
+            pad_ref[:SEP_ROWS, :],
+            (((1,), (1,)), ((), ())),
+            preferred_element_type=jnp.float32,
         )
-    starts = [pl.multiple_of(32 * g + 16 * core, STRIP) for g in range(PLANE)]
+        for g in range(PLANE):
+            strip = total[g * STRIP : (g + 1) * STRIP, :]
+            window_ref[leaf, g] = (pltpu.roll(strip, SEP_ROWS - 32 * g, axis=1) if g else strip)[:, :384]
     for s in range(NSEP):
         slots = [jnp.int32(LEAF_DEV), jnp.int32(LEAF_DEV)]
         for leaf in range(LEAF_DEV):
@@ -49,21 +65,13 @@
             later = hit & (slots[0] < LEAF_DEV)
             slots[1] = jnp.where(later, leaf, slots[1])
             slots[0] = jnp.where(hit & jnp.logical_not(later), leaf, slots[0])
-        total = None
-        for slot in slots:
-            rows = jnp.concatenate([pad_ref[slot, pl.ds(x, STRIP), :] for x in starts], axis=0)
-            product = lax.dot_general(
-                rows, pad_ref[slot], (((1,), (1,)), ((), ())), preferred_element_type=jnp.float32
-            )
-            total = product if total is None else total + product
         lane = 32 * (s % 4)
         for g in range(PLANE):
-            strip = total[g * STRIP : (g + 1) * STRIP, :]
-            window = jnp.roll(strip, -32 * g, axis=1) if g else strip
+            window = window_ref[slots[0], g] + window_ref[slots[1], g]
             out_ref[g, 2 * s] = window[:, :128].astype(jnp.bfloat16)
             out_ref[g, 2 * s + 1] = window[:, 128:256].astype(jnp.bfloat16)
             rest = window[:, 256:384]
-            rest = jnp.roll(rest, lane, axis=1) if lane else rest
+            rest = pltpu.roll(rest, lane, axis=1) if lane else rest
             out_ref[g, 16 + s // 4, :, lane : lane + 32] = rest[:, lane : lane + 32].astype(
                 jnp.bfloat16
             )
@@ -83,13 +91,44 @@
         in_specs=[SMEM, SMEM, SMEM, VMEM, VMEM, VMEM, VMEM],
         out_specs=VMEM,
         out_shape=pltpu.VMEM((PLANE, TILES, STRIP, 128), jnp.bfloat16),
-        scratch_shapes=[pltpu.VMEM((LEAF_DEV + 1, SEP_ROWS, MODES), jnp.bfloat16)],
+        scratch_shapes=[
+            pltpu.VMEM((LEAF_DEV + 1, PLANE, STRIP, 384), jnp.float32),
+            *[pltpu.VMEM((SEP_ROWS + STRIP, MODES), jnp.bfloat16)] * LEAF_DEV,
+        ],
+        compiler_params=pltpu.CompilerParams(vmem_limit_bytes=24 << 20),
         name="gram",
     )(target, offset, core, *[in_vmem(x) for x in arrays])
 
 
+def route_kernel(got_ref, out_ref):
+    def total(tile):
+        parts = [got_ref[k, tile].astype(jnp.float32) for k in range(PLANE)]
+        while len(parts) > 1:
+            parts = [a + b for a, b in zip(parts[::2], parts[1::2])]
+        return parts[0].astype(jnp.bfloat16)
+
+    for s in range(NSEP):
+        out_ref[s, 0] = total(2 * s)
+        out_ref[s, 1] = total(2 * s + 1)
+    for k in range(2):
+        rest = total(16 + k)
+        for s in range(4 * k, 4 * k + 4):
+            out_ref[s, 2] = rest
+
+
+def route(got):
+    return pl.pallas_call(
+        route_kernel,
+        in_specs=[VMEM],
+        out_specs=VMEM,
+        out_shape=pltpu.VMEM((NSEP, 3, STRIP, 128), jnp.bfloat16),
+        compiler_params=pltpu.CompilerParams(vmem_limit_bytes=8 << 20),
+        name="route",
+    )(in_vmem(got))
+
+
 def iterate_kernel(
-    place_ref, own_ref, other_ref, turns_ref, out_ref, norms_ref, kt_ref, m_ref, high_ref, low_ref, x_ref
+    place_ref, own_ref, other_ref, turns_ref, out_ref, norms_ref, kt_ref, m_ref, high_ref, x_ref
 ):
     core, device, sep = place_ref[0], place_ref[1], place_ref[2]
     lane = lax.broadcasted_iota(jnp.int32, (STRIP, 128), 1)
@@ -101,22 +140,32 @@
             rows = pl.ds(pl.multiple_of(32 * g + offset, STRIP), STRIP)
             kt_ref[rows, :] = ref[g, :, :512]
             x_ref[rows, :] = ref[g, :, 512:768]
-            first = ref[g, :, 768:896].astype(jnp.float32) + ref[g, :, 1152:1280].astype(jnp.float32)
+            rest = pltpu.roll(ref[g, :, 1024:1152].astype(jnp.float32), back, axis=1)
+            low = jnp.where(lane < 32, pltpu.roll(rest, 96, axis=1), 0.0)
+            first = ref[g, :, 768:896].astype(jnp.float32) + low
             second = ref[g, :, 896:1024].astype(jnp.float32)
-            rest = pltpu.roll(ref[g, :, 1024:1152].astype(jnp.float32), back, axis=1)
             window = jnp.concatenate(
                 [first * halved, second, rest * rest_weight, jnp.zeros_like(second)], axis=1
             )
-            m_ref[rows, :] = jnp.roll(window, 32 * g, axis=1) if g else window
+            m_ref[rows, :] = pltpu.roll(window, 32 * g, axis=1) if g else window
     half = m_ref[...]
     operator = jnp.transpose(kt_ref[...].astype(jnp.float32) - half) - half
     high = operator.astype(jnp.bfloat16)
     high_ref[...] = high
-    low_ref[...] = (operator - high.astype(jnp.float32)).astype(jnp.bfloat16)
+    error = operator - high.astype(jnp.float32)
+    across = lax.broadcasted_iota(jnp.int32, (128, 128), 0)
+    along = lax.broadcasted_iota(jnp.int32, (128, 128), 1)
+    low = jnp.concatenate(
+        [
+            jnp.sum(jnp.where(across == along, error[k : k + 128, k : k + 128], 0.0), 1, keepdims=True)
+            for k in range(0, SEP_ROWS, 128)
+        ],
+        axis=0,
+    )
     for step in range(ITERS):
-        summed = jnp.dot(
-            high_ref[...], x_ref[...], preferred_element_type=jnp.float32
-        ) + jnp.dot(low_ref[...], x_ref[...], preferred_element_type=jnp.float32)
+        block = x_ref[...]
+        summed = jnp.dot(high_ref[...], block, preferred_element_type=jnp.float32)
+        summed = summed + low * block.astype(jnp.float32)
         scale = jnp.sqrt(jnp.sum(summed * summed, 0, keepdims=True) / SEP_ROWS + epsilon)
         norms_ref[0, pl.ds(step, 1), :] = scale
         normed = (summed / scale).astype(jnp.bfloat16)
@@ -145,11 +194,11 @@
             pltpu.VMEM((SEP_ROWS, SEP_ROWS), jnp.bfloat16),
             pltpu.VMEM((SEP_ROWS, SEP_ROWS), jnp.float32),
             pltpu.VMEM((SEP_ROWS, SEP_ROWS), jnp.bfloat16),
-            pltpu.VMEM((SEP_ROWS, SEP_ROWS), jnp.bfloat16),
             pltpu.VMEM((SEP_ROWS, COLS), jnp.bfloat16),
         ],
+        compiler_params=pltpu.CompilerParams(vmem_limit_bytes=16 << 20),
         name="iterate",
-    )(place, in_vmem(own), in_vmem(other), turns)
+    )(place, in_vmem(own), in_vmem(other), in_vmem(turns))
 
 
 SWAP = [(0, 1), (1, 0)]
@@ -167,16 +216,13 @@
     sep = lax.axis_index("sep").astype(jnp.int32)
     pieces = gram(separator_of[:, 0], row_offset, core[None], own, other, eigenvalues, other_eigen)
     got = lax.all_to_all(pieces, "leaf", split_axis=0, concat_axis=0, tiled=True)
-    plane = jnp.sum(got.astype(jnp.float32), 0).astype(jnp.bfloat16)
-    rest = jnp.broadcast_to(plane[16:, None], (2, 4, STRIP, 128)).reshape(NSEP, 1, STRIP, 128)
-    routed = jnp.concatenate([plane[:16].reshape(NSEP, 2, STRIP, 128), rest], 1)
-    got = lax.all_to_all(routed, "sep", split_axis=0, concat_axis=0, tiled=True)
+    got = lax.all_to_all(route(got), "sep", split_axis=0, concat_axis=0, tiled=True)
     window = jnp.sum(got.astype(jnp.float32), 0)
     high = window.astype(jnp.bfloat16)
     low = (window[0] - high[0].astype(jnp.float32)).astype(jnp.bfloat16)
-    packed = jnp.concatenate(
-        [stiffness[0].T, start_block[0], high[0], high[1], high[2], low], 1
-    )
+    group = lax.broadcasted_iota(jnp.int32, (STRIP, 128), 1) >> 5
+    rest = jnp.where(group == (sep & 3), high[2], jnp.concatenate([low[:, :32]] * 4, 1))
+    packed = jnp.concatenate([stiffness[0].T, start_block[0], high[0], high[1], rest], 1)
     mine = lax.all_to_all(
         jnp.broadcast_to(packed[None], (PLANE, *packed.shape)),
         "leaf",

time: 79 us -> 77.1 us (0.976)
  other arithmetic: 1.42 us -> 0.2 us
    pallas_call x0 -> x1, Pallas kernels: none -> 0.79 us  [route(): pl.pallas_call(route_kernel, in_specs=[VMEM], out_specs=VMEM, out_shape=p...]
  transfers between devices with their start and end apart: 5 -> 5, of which waited for: 4 -> 4; matrix products, arithmetic and copies ran while one was open for 1% -> 0% of each run, Pallas kernels for 0% -> 0%
where the time goes in v6:
time: 77.1 us; the launch traced here: 76.8 us
  waiting for transfers between devices  29.2 us (38%)
  starting transfers between devices  19.8 us (26%)
  blocking collectives  14.5 us (19%)
  Pallas kernels  7.28 us (9%)
  matrix products  4.88 us (6%)
  between operations  0.78 us (1%)
    all_to_all x1, waiting for transfers between devices, per_device(): lax.all_to_all(pieces, 'leaf', split_axis=0, concat_axis=0, tiled=True)  17.9 us
    all_to_all x1, blocking collectives, per_device(): lax.all_to_all(jnp.broadcast_to(packed[None], (PLANE, *packed.shape)), 'l...  14.5 us
    all_to_all x1, starting transfers between devices, per_device(): lax.all_to_all(route(got), 'sep', split_axis=0, concat_axis=0, tiled=True)  8.15 us
    all_to_all x1, waiting for transfers between devices, per_device(): lax.all_to_all(route(got), 'sep', split_axis=0, concat_axis=0, tiled=True)  7.56 us
    all_to_all x1, starting transfers between devices, per_device(): lax.all_to_all(pieces, 'leaf', split_axis=0, concat_axis=0, tiled=True)  5.06 us
    dot_general x1, matrix products, per_device(): jnp.einsum('ldw,ldm->lwm', coupling, modes, preferred_element_type=jnp.fl...  4.88 us
    pallas_call x1, Pallas kernels, gram(): pl.pallas_call(gram_kernel, in_specs=[SMEM, SMEM, SMEM, VMEM, VMEM, VMEM,...  3.6 us
    ppermute x1, starting transfers between devices, per_device(): other = lax.ppermute(own, 'mode', SWAP)  3.29 us
  transfers between devices with their start and end apart: 5, of which 4 were waited for; matrix products, arithmetic and copies ran while one was open for 0% of the time, Pallas kernels for 0%

profile of v6, /device:TPU:1, one launch (start us, length us, event | category | flops | bytes accessed | tf_op | source)
XLA Modules:
  0.0 76.8 jit_solution(2186921993418187161)
XLA Ops:
  0.6 0.0 copy-start.1
  0.6 0.0 copy-start.2
  0.7 0.0 copy-start.3
  0.7 4.9 %convolution_convert_fusion.own_ref = bf16[8,256,256]{2,1,0:T(8,128)(2,1)S(1)} fusion(bf16[8,1024,256]{2,1,0:T(8,128)(2,1)} %param.9, bf16[8,1024,256]{2,1,0:T(8,128)(2,1)} %param.8), kind=kOutput, calls=%fused_computation | convolution fusion | flops 1074266112 | bytes 9437184 | tf_op jit(solution)/shard_map/ldw,ldm->lwm/dot_general | solution.py:212
  5.5 0.0 copy-start.4
  5.6 0.0 copy-start.5
  5.6 3.3 %collective-permute-start = (bf16[8,256,256]{2,1,0:T(8,128)(2,1)S(1)}, bf16[8,256,256]{2,1,0:T(8,128)(2,1)S(1)}, u32[]{:S(2)}, u32[]{:S(2)}) collective-permute-start(bf16[8,256,256]{2,1,0:T(8,128)(2,1)S(1)} %convolution_convert_fusion.own_ref), channel_id=1, source_target_pairs={{0,1},{1,0},{2,3},{3,2},{4,5},{5,4},{6,7},{7,6},{8,9},{9,8},{10,11... | collective-permute-start | bytes 3145736 | tf_op jit(solution)/shard_map/ppermute | solution.py:215
  8.9 0.0 copy-done.1
  8.9 0.1 collective-permute-start.1
  9.0 2.2 %collective-permute-done.1.other_eigen_ref = f32[8,128]{1,0:T(8,128)S(1)} collective-permute-done((f32[8,128]{1,0:T(8,128)S(1)}, f32[8,128]{1,0:T(8,128)S(1)}, u32[]{:S(2)}, u32[]{:S(2)}) %collective-permute-start.1) | collective-permute-done | bytes 4128 | tf_op jit(solution)/shard_map/ppermute | solution.py:211
  11.2 0.0 collective-permute-done.other_ref
  11.2 0.0 copy-done.2
  11.2 0.0 copy-done.3
  11.2 0.0 copy-start
  11.2 3.6 %gram.1 = bf16[16,18,16,128]{3,2,1,0:T(8,128)(2,1)} custom-call(s32[8]{0:T(128)S(1)} %bitcast.30, s32[8]{0:T(128)S(1)} %copy-done.3, s32[1]{0:T(128)} %bitcast.core_ref, bf16[8,256,256]{2,1,0:T(8,128)(2,1)S(1)} %convolution_convert_fusion.own_ref, bf16[8,256,256]{2,1,0:T(8,128)(2,1)S(1)} %collective-permute-done.other_ref, f32[8,128]{1,0:T(8,128)S(1)} %copy-done.1, ...), custom_call_target="tpu_custom_call" | custom-call | tf_op jit(solution)/shard_map/gram/pallas_call | solution.py:89
  14.8 5.1 %all-to-all-start = ((bf16[16,18,16,128]{3,2,1,0:T(8,128)(2,1)}), bf16[16,18,16,128]{3,2,1,0:T(8,128)(2,1)S(1)}, u32[]{:S(2)}, u32[]{:S(2)}) async-start(bf16[16,18,16,128]{3,2,1,0:T(8,128)(2,1)} %gram.1), calls=%async_computation | async-start | bytes 2359296 | tf_op jit(solution)/shard_map/all_to_all | solution.py:218
  19.9 0.0 copy-done.4
  19.9 17.9 %all-to-all-done.got_ref = bf16[16,18,16,128]{3,2,1,0:T(8,128)(2,1)S(1)} async-done(((bf16[16,18,16,128]{3,2,1,0:T(8,128)(2,1)}), bf16[16,18,16,128]{3,2,1,0:T(8,128)(2,1)S(1)}, u32[]{:S(2)}, u32[]{:S(2)}) %all-to-all-start) | async-done | bytes 1179680 | tf_op jit(solution)/shard_map/all_to_all | solution.py:218
  37.8 0.8 %route.1 = bf16[8,3,16,128]{3,2,1,0:T(8,128)(2,1)} custom-call(bf16[16,18,16,128]{3,2,1,0:T(8,128)(2,1)S(1)} %all-to-all-done.got_ref), custom_call_target="tpu_custom_call" | custom-call | tf_op jit(solution)/shard_map/route/pallas_call | solution.py:120
  38.6 8.1 %all-to-all-start.1 = ((bf16[8,3,16,128]{3,2,1,0:T(8,128)(2,1)}), bf16[8,3,16,128]{3,2,1,0:T(8,128)(2,1)S(1)}, u32[]{:S(2)}, u32[]{:S(2)}) async-start(bf16[8,3,16,128]{3,2,1,0:T(8,128)(2,1)} %route.1), calls=%async_computation.1 | async-start | bytes 196608 | tf_op jit(solution)/shard_map/all_to_all | solution.py:219
  46.8 0.0 copy-done.5
  46.8 7.6 %all-to-all-done.1 = bf16[8,3,16,128]{3,2,1,0:T(8,128)(2,1)S(1)} async-done(((bf16[8,3,16,128]{3,2,1,0:T(8,128)(2,1)}), bf16[8,3,16,128]{3,2,1,0:T(8,128)(2,1)S(1)}, u32[]{:S(2)}, u32[]{:S(2)}) %all-to-all-start.1) | async-done | bytes 98336 | tf_op jit(solution)/shard_map/all_to_all | solution.py:219
  54.4 0.1 constant_dynamic-update-slice_fusion
  54.6 14.5 %all_to_all.15.own_ref = bf16[16,16,1152]{2,1,0:T(8,128)(2,1)S(1)} all-to-all(bf16[16,16,1152]{2,1,0:T(8,128)(2,1)S(1)} %broadcast_in_dim.2), channel_id=1, replica_groups=mesh['leaf'=16,'sep'=8,'mode'=2] {'leaf'}, dimensions={0} | all-to-all | bytes 1179648 | tf_op jit(solution)/shard_map/all_to_all | solution.py:226
  69.1 3.2 %collective-permute-start.2 = (bf16[16,16,1152]{2,1,0:T(8,128)(2,1)S(1)}, bf16[16,16,1152]{2,1,0:T(8,128)(2,1)S(1)}, u32[]{:S(2)}, u32[]{:S(2)}) collective-permute-start(bf16[16,16,1152]{2,1,0:T(8,128)(2,1)S(1)} %all_to_all.15.own_ref), channel_id=1, source_target_pairs={{0,1},{1,0},{2,3},{3,2},{4,5},{5,4},{6,7},{7,6},{8,9},{9,8},{10,11... | collective-permute-start | bytes 1769480 | tf_op jit(solution)/shard_map/ppermute | solution.py:233
  72.3 0.1 pad_add_fusion.place_ref
  72.3 1.6 %collective-permute-done.2.other_ref = bf16[16,16,1152]{2,1,0:T(8,128)(2,1)S(1)} collective-permute-done((bf16[16,16,1152]{2,1,0:T(8,128)(2,1)S(1)}, bf16[16,16,1152]{2,1,0:T(8,128)(2,1)S(1)}, u32[]{:S(2)}, u32[]{:S(2)}) %collective-permute-start.2) | collective-permute-done | bytes 589856 | tf_op jit(solution)/shard_map/ppermute | solution.py:233
  73.9 0.0 copy-done
  73.9 2.9 %iterate.1 = (bf16[1,16,256]{2,1,0:T(8,128)(2,1)}, f32[1,2,256]{2,1,0:T(2,128)}) custom-call(s32[3]{0:T(128)S(1)} %pad_add_fusion.place_ref, bf16[16,16,1152]{2,1,0:T(8,128)(2,1)S(1)} %all_to_all.15.own_ref, bf16[16,16,1152]{2,1,0:T(8,128)(2,1)S(1)} %collective-permute-done.2.other_ref, bf16[2,256,256]{2,1,0:T(8,128)(2,1)S(1)} %bitcast.29), custom_call_target="tpu_custom_call" | custom-call | tf_op jit(solution)/shard_map/iterate/pallas_call | solution.py:185
  (11 shorter events, 0.1 us)
Async XLA Ops:
  0.6 8.2 %copy-start.1 = (f32[8,128]{1,0:T(8,128)S(1)}, f32[8,128]{1,0:T(8,128)}, u32[]{:S(2)}) copy-start(f32[8,128]{1,0:T(8,128)} %eigen_ref.1) | copy-start | bytes 12292
  0.6 10.5 %copy-start.2 = (s32[8,1]{0,1:T(1,128)S(1)}, s32[8,1]{0,1:T(1,128)}, u32[]{:S(2)}) copy-start(s32[8,1]{0,1:T(1,128)} %param.11) | copy-start | bytes 100
  0.7 10.5 %copy-start.3 = (s32[8]{0:T(128)S(1)}, s32[8]{0:T(128)}, u32[]{:S(2)}) copy-start(s32[8]{0:T(128)} %offset_ref.1) | copy-start | bytes 100
  5.5 14.3 %copy-start.4 = (bf16[1,512,16]{1,2,0:T(8,128)(2,1)S(1)}, bf16[1,512,16]{1,2,0:T(8,128)(2,1)}, u32[]{:S(2)}) copy-start(bf16[1,512,16]{1,2,0:T(8,128)(2,1)} %param.13) | copy-start | bytes 49156
  5.6 41.2 %copy-start.5 = (bf16[1,16,256]{2,1,0:T(8,128)(2,1)S(1)}, bf16[1,16,256]{2,1,0:T(8,128)(2,1)}, u32[]{:S(2)}) copy-start(bf16[1,16,256]{2,1,0:T(8,128)(2,1)} %param.14) | copy-start | bytes 24580
  5.6 5.6 %collective-permute-start = (bf16[8,256,256]{2,1,0:T(8,128)(2,1)S(1)}, bf16[8,256,256]{2,1,0:T(8,128)(2,1)S(1)}, u32[]{:S(2)}, u32[]{:S(2)}) collective-permute-start(bf16[8,256,256]{2,1,0:T(8,128)(2,1)S(1)} %convolution_convert_fusion.own_ref), channel_id=1, source_target_pairs={{0,1},{1,0},{2,3},{3,2},{4,5},{5,4},{6,7},{7,6},{8,9},{9,8},{10,11... | collective-permute-start | bytes 3145736 | tf_op jit(solution)/shard_map/ppermute | solution.py:215
  8.9 2.3 %collective-permute-start.1 = (f32[8,128]{1,0:T(8,128)S(1)}, f32[8,128]{1,0:T(8,128)S(1)}, u32[]{:S(2)}, u32[]{:S(2)}) collective-permute-start(f32[8,128]{1,0:T(8,128)S(1)} %copy-done.1), channel_id=1, source_target_pairs={{0,1},{1,0},{2,3},{3,2},{4,5},{5,4},{6,7},{7,6},{8,9},{9,8},{10,11... | collective-permute-start | bytes 12296 | tf_op jit(solution)/shard_map/ppermute | solution.py:211
  11.2 62.7 %copy-start = (bf16[1,2,256,256]{3,2,1,0:T(8,128)(2,1)S(1)}, bf16[1,2,256,256]{3,2,1,0:T(8,128)(2,1)}, u32[]{:S(2)}) copy-start(bf16[1,2,256,256]{3,2,1,0:T(8,128)(2,1)} %param.15) | copy-start | bytes 786436
  14.8 23.0 %all-to-all-start = ((bf16[16,18,16,128]{3,2,1,0:T(8,128)(2,1)}), bf16[16,18,16,128]{3,2,1,0:T(8,128)(2,1)S(1)}, u32[]{:S(2)}, u32[]{:S(2)}) async-start(bf16[16,18,16,128]{3,2,1,0:T(8,128)(2,1)} %gram.1), calls=%async_computation | async-start | bytes 2359296 | tf_op jit(solution)/shard_map/all_to_all | solution.py:218
  38.6 15.7 %all-to-all-start.1 = ((bf16[8,3,16,128]{3,2,1,0:T(8,128)(2,1)}), bf16[8,3,16,128]{3,2,1,0:T(8,128)(2,1)S(1)}, u32[]{:S(2)}, u32[]{:S(2)}) async-start(bf16[8,3,16,128]{3,2,1,0:T(8,128)(2,1)} %route.1), calls=%async_computation.1 | async-start | bytes 196608 | tf_op jit(solution)/shard_map/all_to_all | solution.py:219
  69.1 4.8 %collective-permute-start.2 = (bf16[16,16,1152]{2,1,0:T(8,128)(2,1)S(1)}, bf16[16,16,1152]{2,1,0:T(8,128)(2,1)S(1)}, u32[]{:S(2)}, u32[]{:S(2)}) collective-permute-start(bf16[16,16,1152]{2,1,0:T(8,128)(2,1)S(1)} %all_to_all.15.own_ref), channel_id=1, source_target_pairs={{0,1},{1,0},{2,3},{3,2},{4,5},{5,4},{6,7},{7,6},{8,9},{9,8},{10,11... | collective-permute-start | bytes 1769480 | tf_op jit(solution)/shard_map/ppermute | solution.py:233

commit v7 on v6

--- a/solution.py
+++ b/solution.py
@@ -14,16 +14,25 @@
 NSEP = 8
 LEAF_DEV = 8
 PLANE = 16
+SIDE = 4
+GROUPS = 8
 TILES = 18
 STRIP = 16
 ITERS = 2
 epsilon = 1e-06
 
 
+def place_of(d, e, place_ref):
+    one = (place_ref[1] + d) & (SIDE - 1)
+    two = (place_ref[2] + e) & (SIDE - 1)
+    return jnp.where(place_ref[0] == 0, two * SIDE + one, one * SIDE + two)
+
+
 def gram_kernel(
-    target_ref, offset_ref, core_ref, own_ref, other_ref, eigen_ref, other_eigen_ref, out_ref, window_ref, *pad_refs
+    target_ref, offset_ref, place_ref, own_ref, other_ref, eigen_ref, other_eigen_ref, *refs
 ):
-    core = core_ref[0]
+    out_refs, window_ref, pad_refs = refs[:SIDE], refs[SIDE], refs[SIDE + 1 :]
+    core = place_ref[0]
     reach = IFACE + STRIP
     row = lax.broadcasted_iota(jnp.int32, (reach, IFACE), 0)
     column = lax.broadcasted_iota(jnp.int32, (reach, IFACE), 1)
@@ -58,6 +67,7 @@
         for g in range(PLANE):
             strip = total[g * STRIP : (g + 1) * STRIP, :]
             window_ref[leaf, g] = (pltpu.roll(strip, SEP_ROWS - 32 * g, axis=1) if g else strip)[:, :384]
+    places = [place_of(k // SIDE, k % SIDE, place_ref) for k in range(PLANE)]
     for s in range(NSEP):
         slots = [jnp.int32(LEAF_DEV), jnp.int32(LEAF_DEV)]
         for leaf in range(LEAF_DEV):
@@ -66,13 +76,15 @@
             slots[1] = jnp.where(later, leaf, slots[1])
             slots[0] = jnp.where(hit & jnp.logical_not(later), leaf, slots[0])
         lane = 32 * (s % 4)
-        for g in range(PLANE):
+        for k in range(PLANE):
+            g = places[k]
+            out_ref, e = out_refs[k // SIDE], k % SIDE
             window = window_ref[slots[0], g] + window_ref[slots[1], g]
-            out_ref[g, 2 * s] = window[:, :128].astype(jnp.bfloat16)
-            out_ref[g, 2 * s + 1] = window[:, 128:256].astype(jnp.bfloat16)
+            out_ref[e, 2 * s] = window[:, :128].astype(jnp.bfloat16)
+            out_ref[e, 2 * s + 1] = window[:, 128:256].astype(jnp.bfloat16)
             rest = window[:, 256:384]
             rest = pltpu.roll(rest, lane, axis=1) if lane else rest
-            out_ref[g, 16 + s // 4, :, lane : lane + 32] = rest[:, lane : lane + 32].astype(
+            out_ref[e, 16 + s // 4, :, lane : lane + 32] = rest[:, lane : lane + 32].astype(
                 jnp.bfloat16
             )
 
@@ -85,46 +97,52 @@
 SMEM = pl.BlockSpec(memory_space=pltpu.SMEM)
 
 
-def gram(target, offset, core, *arrays):
+def gram(target, offset, place, *arrays):
     return pl.pallas_call(
         gram_kernel,
         in_specs=[SMEM, SMEM, SMEM, VMEM, VMEM, VMEM, VMEM],
-        out_specs=VMEM,
-        out_shape=pltpu.VMEM((PLANE, TILES, STRIP, 128), jnp.bfloat16),
+        out_specs=[VMEM] * SIDE,
+        out_shape=[jax.ShapeDtypeStruct((SIDE, TILES, STRIP, 128), jnp.bfloat16)] * SIDE,
         scratch_shapes=[
             pltpu.VMEM((LEAF_DEV + 1, PLANE, STRIP, 384), jnp.float32),
             *[pltpu.VMEM((SEP_ROWS + STRIP, MODES), jnp.bfloat16)] * LEAF_DEV,
         ],
         compiler_params=pltpu.CompilerParams(vmem_limit_bytes=24 << 20),
         name="gram",
-    )(target, offset, core, *[in_vmem(x) for x in arrays])
-
-
-def route_kernel(got_ref, out_ref):
-    def total(tile):
-        parts = [got_ref[k, tile].astype(jnp.float32) for k in range(PLANE)]
-        while len(parts) > 1:
-            parts = [a + b for a, b in zip(parts[::2], parts[1::2])]
-        return parts[0].astype(jnp.bfloat16)
-
+    )(target, offset, place, *[in_vmem(x) for x in arrays])
+
+
+def total(refs, *where):
+    return sum(ref[where].astype(jnp.float32) for ref in refs).astype(jnp.bfloat16)
+
+
+def split_kernel(*refs):
+    sources, outs = refs[:SIDE], refs[SIDE:]
+    for e in range(SIDE):
+        for tile in range(TILES):
+            outs[e][tile] = total(sources, e, tile)
+
+
+def route_kernel(*refs):
+    sources, out_ref = refs[:SIDE], refs[SIDE]
     for s in range(NSEP):
-        out_ref[s, 0] = total(2 * s)
-        out_ref[s, 1] = total(2 * s + 1)
+        out_ref[s, 0] = total(sources, 2 * s)
+        out_ref[s, 1] = total(sources, 2 * s + 1)
     for k in range(2):
-        rest = total(16 + k)
+        rest = total(sources, 16 + k)
         for s in range(4 * k, 4 * k + 4):
             out_ref[s, 2] = rest
 
 
-def route(got):
+def combine(kernel, pieces, shapes):
     return pl.pallas_call(
-        route_kernel,
-        in_specs=[VMEM],
-        out_specs=VMEM,
-        out_shape=pltpu.VMEM((NSEP, 3, STRIP, 128), jnp.bfloat16),
+        kernel,
+        in_specs=[VMEM] * SIDE,
+        out_specs=[VMEM] * len(shapes),
+        out_shape=[jax.ShapeDtypeStruct(shape, jnp.bfloat16) for shape in shapes],
         compiler_params=pltpu.CompilerParams(vmem_limit_bytes=8 << 20),
-        name="route",
-    )(in_vmem(got))
+        name=kernel.__name__,
+    )(*[in_vmem(piece) for piece in pieces])
 
 
 def iterate_kernel(
@@ -202,6 +220,31 @@
 
 
 SWAP = [(0, 1), (1, 0)]
+AXES = ("leaf", "sep", "mode")
+
+
+def index_of(y, x, z, core):
+    return ((y * SIDE + x) * GROUPS + z) * 2 + core
+
+
+def plane_steps(step, stage):
+    pairs = []
+    for y in range(SIDE):
+        for x in range(SIDE):
+            for z in range(GROUPS):
+                for core in range(2):
+                    along_x = (core + stage) % 2 == 0
+                    to = (y, (x + step) % SIDE) if along_x else ((y + step) % SIDE, x)
+                    pairs.append((index_of(y, x, z, core), index_of(*to, z, core)))
+    return pairs
+
+
+def scatter_stage(pieces, stage):
+    got = [lax.ppermute(pieces[d], AXES, plane_steps(d, stage)) for d in ORDER]
+    return [pieces[0], *got]
+
+
+ORDER = (1, 3, 2)
 
 def per_device(
     modes, coupling, eigenvalues, separator_of, row_offset, stiffness, start_block, rotations
@@ -214,9 +257,14 @@
     )
     other = lax.ppermute(own, "mode", SWAP)
     sep = lax.axis_index("sep").astype(jnp.int32)
-    pieces = gram(separator_of[:, 0], row_offset, core[None], own, other, eigenvalues, other_eigen)
-    got = lax.all_to_all(pieces, "leaf", split_axis=0, concat_axis=0, tiled=True)
-    got = lax.all_to_all(route(got), "sep", split_axis=0, concat_axis=0, tiled=True)
+    leaf = lax.axis_index("leaf").astype(jnp.int32)
+    y, x = leaf >> 2, leaf & 3
+    place = jnp.stack([core, jnp.where(core == 0, x, y), jnp.where(core == 0, y, x)])
+    pieces = gram(separator_of[:, 0], row_offset, place, own, other, eigenvalues, other_eigen)
+    piece = (TILES, STRIP, 128)
+    pieces = combine(split_kernel, scatter_stage(pieces, 0), [piece] * SIDE)
+    (routed,) = combine(route_kernel, scatter_stage(pieces, 1), [(NSEP, 3, STRIP, 128)])
+    got = lax.all_to_all(routed, "sep", split_axis=0, concat_axis=0, tiled=True)
     window = jnp.sum(got.astype(jnp.float32), 0)
     high = window.astype(jnp.bfloat16)
     low = (window[0] - high[0].astype(jnp.float32)).astype(jnp.bfloat16)

time: 77.1 us -> 72.4 us (0.939)
  waiting for transfers between devices: 29.2 us -> 21.4 us
  starting transfers between devices: 19.8 us -> 23.5 us
  local copies, waits for them, and re-layouts: 0.1 us -> 1.5 us
  blocking collectives: 14.5 us -> 13.2 us
  Pallas kernels: 7.28 us -> 6.4 us
    all_to_all x2 -> x1, waiting for transfers between devices: 25.5 us -> 6.98 us  [per_device(): got = lax.all_to_all(routed, 'sep', split_axis=0, concat_axis=0, tiled=True)]
    ppermute x0 -> x6, waiting for transfers between devices: none -> 10.8 us  [scatter_stage(): got = [lax.ppermute(pieces[d], AXES, plane_steps(d, stage)) for d in ORDER]]
    ppermute x0 -> x6, starting transfers between devices: none -> 6.25 us  [scatter_stage(): got = [lax.ppermute(pieces[d], AXES, plane_steps(d, stage)) for d in ORDER]]
    all_to_all x2 -> x1, starting transfers between devices: 13.2 us -> 7.7 us  [per_device(): got = lax.all_to_all(routed, 'sep', split_axis=0, concat_axis=0, tiled=True)]
    ppermute x1, starting transfers between devices: 3.18 us -> 6.12 us  [per_device(): theirs = lax.ppermute(mine, 'mode', SWAP)]
    unnamed x16 -> x12, local copies, waits for them, and re-layouts: 0.05 us -> 1.45 us
    all_to_all x1, blocking collectives: 14.5 us -> 13.2 us  [per_device(): lax.all_to_all(jnp.broadcast_to(packed[None], (PLANE, *packed.shape)), 'l...]
    pallas_call x1, Pallas kernels: 3.6 us -> 2.7 us  [gram(): pl.pallas_call(gram_kernel, in_specs=[SMEM, SMEM, SMEM, VMEM, VMEM, VMEM,...]
  transfers between devices with their start and end apart: 5 -> 10, of which waited for: 4 -> 6; matrix products, arithmetic and copies ran while one was open for 0% -> 2% of each run, Pallas kernels for 0% -> 0%
where the time goes in v7:
time: 72.4 us; the launch traced here: 72 us
  starting transfers between devices  23.5 us (32%)
  waiting for transfers between devices  21.4 us (30%)
  blocking collectives  13.2 us (18%)
  Pallas kernels  6.4 us (9%)
  matrix products  4.88 us (7%)
  local copies, waits for them, and re-layouts  1.5 us (2%)
  between operations  0.74 us (1%)
    all_to_all x1, blocking collectives, per_device(): lax.all_to_all(jnp.broadcast_to(packed[None], (PLANE, *packed.shape)), 'l...  13.2 us
    ppermute x6, waiting for transfers between devices, scatter_stage(): got = [lax.ppermute(pieces[d], AXES, plane_steps(d, stage)) for d in ORDER]  10.8 us
    all_to_all x1, starting transfers between devices, per_device(): got = lax.all_to_all(routed, 'sep', split_axis=0, concat_axis=0, tiled=True)  7.7 us
    all_to_all x1, waiting for transfers between devices, per_device(): got = lax.all_to_all(routed, 'sep', split_axis=0, concat_axis=0, tiled=True)  6.98 us
    ppermute x6, starting transfers between devices, scatter_stage(): got = [lax.ppermute(pieces[d], AXES, plane_steps(d, stage)) for d in ORDER]  6.25 us
    ppermute x1, starting transfers between devices, per_device(): theirs = lax.ppermute(mine, 'mode', SWAP)  6.12 us
    dot_general x1, matrix products, per_device(): jnp.einsum('ldw,ldm->lwm', coupling, modes, preferred_element_type=jnp.fl...  4.88 us
    ppermute x1, starting transfers between devices, per_device(): other = lax.ppermute(own, 'mode', SWAP)  3.29 us
  transfers between devices with their start and end apart: 10, of which 6 were waited for; matrix products, arithmetic and copies ran while one was open for 2% of the time, Pallas kernels for 0%

profile of v7, /device:TPU:1, one launch (start us, length us, event | category | flops | bytes accessed | tf_op | source)
XLA Modules:
  0.0 72.0 jit_solution(18422843138812558950)
XLA Ops:
  0.7 4.9 %convolution_convert_fusion.own_ref = bf16[8,256,256]{2,1,0:T(8,128)(2,1)S(1)} fusion(bf16[8,1024,256]{2,1,0:T(8,128)(2,1)} %param.9, bf16[8,1024,256]{2,1,0:T(8,128)(2,1)} %param.8), kind=kOutput, calls=%fused_computation | convolution fusion | flops 1074266112 | bytes 9437184 | tf_op jit(solution)/shard_map/ldw,ldm->lwm/dot_general | solution.py:255
  5.5 0.0 copy-start
  5.6 3.3 %collective-permute-start = (bf16[8,256,256]{2,1,0:T(8,128)(2,1)S(1)}, bf16[8,256,256]{2,1,0:T(8,128)(2,1)S(1)}, u32[]{:S(2)}, u32[]{:S(2)}) collective-permute-start(bf16[8,256,256]{2,1,0:T(8,128)(2,1)S(1)} %convolution_convert_fusion.own_ref), channel_id=1, source_target_pairs={{0,1},{1,0},{2,3},{3,2},{4,5},{5,4},{6,7},{7,6},{8,9},{9,8},{10,11... | collective-permute-start | bytes 3145736 | tf_op jit(solution)/shard_map/ppermute | solution.py:258
  8.8 0.1 collective-permute-start.1
  9.0 0.1 pad_add_fusion.1.place_ref
  9.0 2.1 %collective-permute-done.1.other_eigen_ref = f32[8,128]{1,0:T(8,128)S(1)} collective-permute-done((f32[8,128]{1,0:T(8,128)S(1)}, f32[8,128]{1,0:T(8,128)S(1)}, u32[]{:S(2)}, u32[]{:S(2)}) %collective-permute-start.1) | collective-permute-done | bytes 4128 | tf_op jit(solution)/shard_map/ppermute | solution.py:254
  11.1 0.0 collective-permute-done.other_ref
  11.1 2.7 %gram.1 = (bf16[4,18,16,128]{3,2,1,0:T(8,128)(2,1)S(1)}, bf16[4,18,16,128]{3,2,1,0:T(8,128)(2,1)S(1)}, bf16[4,18,16,128]{3,2,1,0:T(8,128)(2,1)S(1)}, bf16[4,18,16,128]{3,2,1,0:T(8,128)(2,1)S(1)}) custom-call(s32[8]{0:T(128)S(1)} %bitcast.32, s32[8]{0:T(128)S(1)} %copy-done.3, s32[3]{0:T(128)S(1)} %pad_add_fusion.1.place_ref, ...), custom_call_target="tpu_custom_call" | custom-call | tf_op jit(solution)/shard_map/gram/pallas_call | solution.py:101
  13.8 0.1 collective-permute-start.2
  13.9 2.7 %collective-permute-start.3 = (bf16[4,18,16,128]{3,2,1,0:T(8,128)(2,1)S(1)}, bf16[4,18,16,128]{3,2,1,0:T(8,128)(2,1)S(1)}, u32[]{:S(2)}, u32[]{:S(2)}) collective-permute-start(bf16[4,18,16,128]{3,2,1,0:T(8,128)(2,1)S(1)} %get-tuple-element.12), channel_id=1, source_target_pairs={{0,48},{1,193},{2,50},{3,195},{4,52},{5,197},{6,54},{7,199},{8,56}... | collective-permute-start | bytes 884744 | tf_op jit(solution)/shard_map/ppermute | solution.py:243
  16.6 0.0 collective-permute-start.4
  16.6 0.7 bitcast_dynamic-update-slice_fusion
  17.3 6.8 %collective-permute-done.2.refs_1_ = bf16[4,18,16,128]{3,2,1,0:T(8,128)(2,1)S(1)} collective-permute-done((bf16[4,18,16,128]{3,2,1,0:T(8,128)(2,1)S(1)}, bf16[4,18,16,128]{3,2,1,0:T(8,128)(2,1)S(1)}, u32[]{:S(2)}, u32[]{:S(2)}) %collective-permute-start.2) | collective-permute-done | bytes 294944 | tf_op jit(solution)/shard_map/ppermute | solution.py:243
  24.2 0.0 collective-permute-done.3.refs_2_
  24.2 0.0 collective-permute-done.4.refs_3_
  24.2 0.1 split_kernel.1
  24.3 0.5 collective-permute-start.5
  24.8 2.2 %collective-permute-start.6 = (bf16[18,16,128]{2,1,0:T(8,128)(2,1)S(1)}, bf16[18,16,128]{2,1,0:T(8,128)(2,1)S(1)}, u32[]{:S(2)}, u32[]{:S(2)}) collective-permute-start(bf16[18,16,128]{2,1,0:T(8,128)(2,1)S(1)} %get-tuple-element.16), channel_id=1, source_target_pairs={{0,192},{1,49},{2,194},{3,51},{4,196},{5,53},{6,198},{7,55},{8,200... | collective-permute-start | bytes 221192 | tf_op jit(solution)/shard_map/ppermute | solution.py:243
  27.1 0.8 %collective-permute-start.7 = (bf16[18,16,128]{2,1,0:T(8,128)(2,1)S(1)}, bf16[18,16,128]{2,1,0:T(8,128)(2,1)S(1)}, u32[]{:S(2)}, u32[]{:S(2)}) collective-permute-start(bf16[18,16,128]{2,1,0:T(8,128)(2,1)S(1)} %get-tuple-element.17), channel_id=1, source_target_pairs={{0,128},{1,33},{2,130},{3,35},{4,132},{5,37},{6,134},{7,39},{8,136... | collective-permute-start | bytes 221192 | tf_op jit(solution)/shard_map/ppermute | solution.py:243
  27.8 1.0 %collective-permute-done.5.refs_1_ = bf16[18,16,128]{2,1,0:T(8,128)(2,1)S(1)} collective-permute-done((bf16[18,16,128]{2,1,0:T(8,128)(2,1)S(1)}, bf16[18,16,128]{2,1,0:T(8,128)(2,1)S(1)}, u32[]{:S(2)}, u32[]{:S(2)}) %collective-permute-start.5) | collective-permute-done | bytes 73760 | tf_op jit(solution)/shard_map/ppermute | solution.py:243
  28.8 0.0 collective-permute-done.6.refs_2_
  28.8 3.0 %collective-permute-done.7.refs_3_ = bf16[18,16,128]{2,1,0:T(8,128)(2,1)S(1)} collective-permute-done((bf16[18,16,128]{2,1,0:T(8,128)(2,1)S(1)}, bf16[18,16,128]{2,1,0:T(8,128)(2,1)S(1)}, u32[]{:S(2)}, u32[]{:S(2)}) %collective-permute-start.7) | collective-permute-done | bytes 73760 | tf_op jit(solution)/shard_map/ppermute | solution.py:243
  31.8 0.7 route_kernel.1
  32.5 7.7 %all-to-all-start = ((bf16[8,3,16,128]{3,2,1,0:T(8,128)(2,1)}), bf16[8,3,16,128]{3,2,1,0:T(8,128)(2,1)S(1)}, u32[]{:S(2)}, u32[]{:S(2)}) async-start(bf16[8,3,16,128]{3,2,1,0:T(8,128)(2,1)} %route_kernel.1), calls=%async_computation | async-start | bytes 196608 | tf_op jit(solution)/shard_map/all_to_all | solution.py:267
  40.2 0.7 constant_dynamic-update-slice_fusion.3
  40.9 7.0 %all-to-all-done = bf16[8,3,16,128]{3,2,1,0:T(8,128)(2,1)S(1)} async-done(((bf16[8,3,16,128]{3,2,1,0:T(8,128)(2,1)}), bf16[8,3,16,128]{3,2,1,0:T(8,128)(2,1)S(1)}, u32[]{:S(2)}, u32[]{:S(2)}) %all-to-all-start) | async-done | bytes 98336 | tf_op jit(solution)/shard_map/all_to_all | solution.py:267
  47.9 0.1 constant_dynamic-update-slice_fusion
  48.1 13.2 %all_to_all.10.own_ref = bf16[16,16,1152]{2,1,0:T(8,128)(2,1)S(1)} all-to-all(bf16[16,16,1152]{2,1,0:T(8,128)(2,1)S(1)} %broadcast_in_dim.2), channel_id=1, replica_groups=mesh['leaf'=16,'sep'=8,'mode'=2] {'leaf'}, dimensions={0} | all-to-all | bytes 1179648 | tf_op jit(solution)/shard_map/all_to_all | solution.py:274
  61.3 6.1 %collective-permute-start.8 = (bf16[16,16,1152]{2,1,0:T(8,128)(2,1)S(1)}, bf16[16,16,1152]{2,1,0:T(8,128)(2,1)S(1)}, u32[]{:S(2)}, u32[]{:S(2)}) collective-permute-start(bf16[16,16,1152]{2,1,0:T(8,128)(2,1)S(1)} %all_to_all.10.own_ref), channel_id=1, source_target_pairs={{0,1},{1,0},{2,3},{3,2},{4,5},{5,4},{6,7},{7,6},{8,9},{9,8},{10,11... | collective-permute-start | bytes 1769480 | tf_op jit(solution)/shard_map/ppermute | solution.py:281
  67.4 0.1 pad_add_fusion.place_ref
  67.5 1.6 %collective-permute-done.8.other_ref = bf16[16,16,1152]{2,1,0:T(8,128)(2,1)S(1)} collective-permute-done((bf16[16,16,1152]{2,1,0:T(8,128)(2,1)S(1)}, bf16[16,16,1152]{2,1,0:T(8,128)(2,1)S(1)}, u32[]{:S(2)}, u32[]{:S(2)}) %collective-permute-start.8) | collective-permute-done | bytes 589856 | tf_op jit(solution)/shard_map/ppermute | solution.py:281
  69.1 2.9 %iterate.1 = (bf16[1,16,256]{2,1,0:T(8,128)(2,1)}, f32[1,2,256]{2,1,0:T(2,128)}) custom-call(s32[3]{0:T(128)S(1)} %pad_add_fusion.place_ref, bf16[16,16,1152]{2,1,0:T(8,128)(2,1)S(1)} %all_to_all.10.own_ref, bf16[16,16,1152]{2,1,0:T(8,128)(2,1)S(1)} %collective-permute-done.8.other_ref, bf16[2,256,256]{2,1,0:T(8,128)(2,1)S(1)} %bitcast.31), custom_call_target="tpu_custom_call" | custom-call | tf_op jit(solution)/shard_map/iterate/pallas_call | solution.py:203
  (16 shorter events, 0.1 us)
Async XLA Ops:
  0.6 8.2 %copy-start.1 = (f32[8,128]{1,0:T(8,128)S(1)}, f32[8,128]{1,0:T(8,128)}, u32[]{:S(2)}) copy-start(f32[8,128]{1,0:T(8,128)} %eigen_ref.1) | copy-start | bytes 12292
  0.6 10.5 %copy-start.2 = (s32[8,1]{0,1:T(1,128)S(1)}, s32[8,1]{0,1:T(1,128)}, u32[]{:S(2)}) copy-start(s32[8,1]{0,1:T(1,128)} %param.11) | copy-start | bytes 100
  0.7 10.5 %copy-start.3 = (s32[8]{0:T(128)S(1)}, s32[8]{0:T(128)}, u32[]{:S(2)}) copy-start(s32[8]{0:T(128)} %offset_ref.1) | copy-start | bytes 100
  5.5 63.5 %copy-start = (bf16[1,2,256,256]{3,2,1,0:T(8,128)(2,1)S(1)}, bf16[1,2,256,256]{3,2,1,0:T(8,128)(2,1)}, u32[]{:S(2)}) copy-start(bf16[1,2,256,256]{3,2,1,0:T(8,128)(2,1)} %param.15) | copy-start | bytes 786436
  5.6 5.6 %collective-permute-start = (bf16[8,256,256]{2,1,0:T(8,128)(2,1)S(1)}, bf16[8,256,256]{2,1,0:T(8,128)(2,1)S(1)}, u32[]{:S(2)}, u32[]{:S(2)}) collective-permute-start(bf16[8,256,256]{2,1,0:T(8,128)(2,1)S(1)} %convolution_convert_fusion.own_ref), channel_id=1, source_target_pairs={{0,1},{1,0},{2,3},{3,2},{4,5},{5,4},{6,7},{7,6},{8,9},{9,8},{10,11... | collective-permute-start | bytes 3145736 | tf_op jit(solution)/shard_map/ppermute | solution.py:258
  8.8 2.3 %collective-permute-start.1 = (f32[8,128]{1,0:T(8,128)S(1)}, f32[8,128]{1,0:T(8,128)S(1)}, u32[]{:S(2)}, u32[]{:S(2)}) collective-permute-start(f32[8,128]{1,0:T(8,128)S(1)} %copy-done.1), channel_id=1, source_target_pairs={{0,1},{1,0},{2,3},{3,2},{4,5},{5,4},{6,7},{7,6},{8,9},{9,8},{10,11... | collective-permute-start | bytes 12296 | tf_op jit(solution)/shard_map/ppermute | solution.py:254
  13.8 10.3 %collective-permute-start.2 = (bf16[4,18,16,128]{3,2,1,0:T(8,128)(2,1)S(1)}, bf16[4,18,16,128]{3,2,1,0:T(8,128)(2,1)S(1)}, u32[]{:S(2)}, u32[]{:S(2)}) collective-permute-start(bf16[4,18,16,128]{3,2,1,0:T(8,128)(2,1)S(1)} %get-tuple-element.11), channel_id=1, source_target_pairs={{0,16},{1,65},{2,18},{3,67},{4,20},{5,69},{6,22},{7,71},{8,24},{9,... | collective-permute-start | bytes 884744 | tf_op jit(solution)/shard_map/ppermute | solution.py:243
  13.9 10.2 %collective-permute-start.3 = (bf16[4,18,16,128]{3,2,1,0:T(8,128)(2,1)S(1)}, bf16[4,18,16,128]{3,2,1,0:T(8,128)(2,1)S(1)}, u32[]{:S(2)}, u32[]{:S(2)}) collective-permute-start(bf16[4,18,16,128]{3,2,1,0:T(8,128)(2,1)S(1)} %get-tuple-element.12), channel_id=1, source_target_pairs={{0,48},{1,193},{2,50},{3,195},{4,52},{5,197},{6,54},{7,199},{8,56}... | collective-permute-start | bytes 884744 | tf_op jit(solution)/shard_map/ppermute | solution.py:243
  16.6 7.6 %collective-permute-start.4 = (bf16[4,18,16,128]{3,2,1,0:T(8,128)(2,1)S(1)}, bf16[4,18,16,128]{3,2,1,0:T(8,128)(2,1)S(1)}, u32[]{:S(2)}, u32[]{:S(2)}) collective-permute-start(bf16[4,18,16,128]{3,2,1,0:T(8,128)(2,1)S(1)} %get-tuple-element.13), channel_id=1, source_target_pairs={{0,32},{1,129},{2,34},{3,131},{4,36},{5,133},{6,38},{7,135},{8,40}... | collective-permute-start | bytes 884744 | tf_op jit(solution)/shard_map/ppermute | solution.py:243
  24.3 4.5 %collective-permute-start.5 = (bf16[18,16,128]{2,1,0:T(8,128)(2,1)S(1)}, bf16[18,16,128]{2,1,0:T(8,128)(2,1)S(1)}, u32[]{:S(2)}, u32[]{:S(2)}) collective-permute-start(bf16[18,16,128]{2,1,0:T(8,128)(2,1)S(1)} %get-tuple-element.15), channel_id=1, source_target_pairs={{0,64},{1,17},{2,66},{3,19},{4,68},{5,21},{6,70},{7,23},{8,72},{9,... | collective-permute-start | bytes 221192 | tf_op jit(solution)/shard_map/ppermute | solution.py:243
  24.8 4.0 %collective-permute-start.6 = (bf16[18,16,128]{2,1,0:T(8,128)(2,1)S(1)}, bf16[18,16,128]{2,1,0:T(8,128)(2,1)S(1)}, u32[]{:S(2)}, u32[]{:S(2)}) collective-permute-start(bf16[18,16,128]{2,1,0:T(8,128)(2,1)S(1)} %get-tuple-element.16), channel_id=1, source_target_pairs={{0,192},{1,49},{2,194},{3,51},{4,196},{5,53},{6,198},{7,55},{8,200... | collective-permute-start | bytes 221192 | tf_op jit(solution)/shard_map/ppermute | solution.py:243
  27.1 4.7 %collective-permute-start.7 = (bf16[18,16,128]{2,1,0:T(8,128)(2,1)S(1)}, bf16[18,16,128]{2,1,0:T(8,128)(2,1)S(1)}, u32[]{:S(2)}, u32[]{:S(2)}) collective-permute-start(bf16[18,16,128]{2,1,0:T(8,128)(2,1)S(1)} %get-tuple-element.17), channel_id=1, source_target_pairs={{0,128},{1,33},{2,130},{3,35},{4,132},{5,37},{6,134},{7,39},{8,136... | collective-permute-start | bytes 221192 | tf_op jit(solution)/shard_map/ppermute | solution.py:243
  32.5 15.4 %all-to-all-start = ((bf16[8,3,16,128]{3,2,1,0:T(8,128)(2,1)}), bf16[8,3,16,128]{3,2,1,0:T(8,128)(2,1)S(1)}, u32[]{:S(2)}, u32[]{:S(2)}) async-start(bf16[8,3,16,128]{3,2,1,0:T(8,128)(2,1)} %route_kernel.1), calls=%async_computation | async-start | bytes 196608 | tf_op jit(solution)/shard_map/all_to_all | solution.py:267
  61.3 7.7 %collective-permute-start.8 = (bf16[16,16,1152]{2,1,0:T(8,128)(2,1)S(1)}, bf16[16,16,1152]{2,1,0:T(8,128)(2,1)S(1)}, u32[]{:S(2)}, u32[]{:S(2)}) collective-permute-start(bf16[16,16,1152]{2,1,0:T(8,128)(2,1)S(1)} %all_to_all.10.own_ref), channel_id=1, source_target_pairs={{0,1},{1,0},{2,3},{3,2},{4,5},{5,4},{6,7},{7,6},{8,9},{9,8},{10,11... | collective-permute-start | bytes 1769480 | tf_op jit(solution)/shard_map/ppermute | solution.py:281

commit v8 on v7

--- a/solution.py
+++ b/solution.py
@@ -146,22 +146,30 @@
 
 
 def iterate_kernel(
-    place_ref, own_ref, other_ref, turns_ref, out_ref, norms_ref, kt_ref, m_ref, high_ref, x_ref
+    place_ref, own_ref, other_ref, known_ref, known_other_ref, turns_ref, out_ref, norms_ref, kt_ref, m_ref, high_ref, x_ref
 ):
     core, device, sep = place_ref[0], place_ref[1], place_ref[2]
+    leaf = device >> 1
+    y, x = leaf >> 2, leaf & 3
     lane = lax.broadcasted_iota(jnp.int32, (STRIP, 128), 1)
     halved = jnp.where(lane < 32, 0.5, 1.0)
     rest_weight = jnp.where(lane < 32, 0.5, 0.0)
     back = (128 - 32 * (sep & 3)) & 127
-    for ref, offset in ((own_ref, 16 * core), (other_ref, 16 * (1 - core))):
+    for ref, known, which in ((own_ref, known_ref, core), (other_ref, known_other_ref, 1 - core)):
+        for e in range(SIDE):
+            for d in range(SIDE):
+                up = (y - jnp.where(which == 0, e, d)) & (SIDE - 1)
+                over = (x - jnp.where(which == 0, d, e)) & (SIDE - 1)
+                start = 32 * (up * SIDE + over) + 16 * which
+                rows = pl.ds(pl.multiple_of(start, STRIP), STRIP)
+                kt_ref[rows, :] = known[e, d, :, :SEP_ROWS]
+                x_ref[rows, :] = known[e, d, :, SEP_ROWS:]
         for g in range(PLANE):
-            rows = pl.ds(pl.multiple_of(32 * g + offset, STRIP), STRIP)
-            kt_ref[rows, :] = ref[g, :, :512]
-            x_ref[rows, :] = ref[g, :, 512:768]
-            rest = pltpu.roll(ref[g, :, 1024:1152].astype(jnp.float32), back, axis=1)
+            rows = pl.ds(pl.multiple_of(32 * g + 16 * which, STRIP), STRIP)
+            rest = pltpu.roll(ref[g, :, 256:384].astype(jnp.float32), back, axis=1)
             low = jnp.where(lane < 32, pltpu.roll(rest, 96, axis=1), 0.0)
-            first = ref[g, :, 768:896].astype(jnp.float32) + low
-            second = ref[g, :, 896:1024].astype(jnp.float32)
+            first = ref[g, :, :128].astype(jnp.float32) + low
+            second = ref[g, :, 128:256].astype(jnp.float32)
             window = jnp.concatenate(
                 [first * halved, second, rest * rest_weight, jnp.zeros_like(second)], axis=1
             )
@@ -199,10 +207,10 @@
             ).astype(jnp.bfloat16)
 
 
-def iterate(place, own, other, turns):
+def iterate(place, *arrays):
     return pl.pallas_call(
         iterate_kernel,
-        in_specs=[SMEM, VMEM, VMEM, VMEM],
+        in_specs=[SMEM] + [VMEM] * len(arrays),
         out_specs=[VMEM, VMEM],
         out_shape=[
             jax.ShapeDtypeStruct((1, STRIP, COLS), jnp.bfloat16),
@@ -216,7 +224,7 @@
         ],
         compiler_params=pltpu.CompilerParams(vmem_limit_bytes=16 << 20),
         name="iterate",
-    )(place, in_vmem(own), in_vmem(other), in_vmem(turns))
+    )(place, *[in_vmem(array) for array in arrays])
 
 
 SWAP = [(0, 1), (1, 0)]
@@ -239,6 +247,15 @@
     return pairs
 
 
+def after(value, earlier):
+    return lax.optimization_barrier((value, earlier))[0]
+
+
+def gather_stage(value, stage):
+    got = [lax.ppermute(value, AXES, plane_steps(d, stage)) for d in ORDER]
+    return jnp.stack([value, got[0], got[2], got[1]])
+
+
 def scatter_stage(pieces, stage):
     got = [lax.ppermute(pieces[d], AXES, plane_steps(d, stage)) for d in ORDER]
     return [pieces[0], *got]
@@ -262,15 +279,19 @@
     place = jnp.stack([core, jnp.where(core == 0, x, y), jnp.where(core == 0, y, x)])
     pieces = gram(separator_of[:, 0], row_offset, place, own, other, eigenvalues, other_eigen)
     piece = (TILES, STRIP, 128)
+    known = jnp.concatenate([stiffness[0].T, start_block[0]], 1)
+    near = gather_stage(after(known, pieces[0]), 0)
     pieces = combine(split_kernel, scatter_stage(pieces, 0), [piece] * SIDE)
+    known = gather_stage(after(near, pieces[0]), 1)
     (routed,) = combine(route_kernel, scatter_stage(pieces, 1), [(NSEP, 3, STRIP, 128)])
+    known_other = lax.ppermute(after(known, routed), "mode", SWAP)
     got = lax.all_to_all(routed, "sep", split_axis=0, concat_axis=0, tiled=True)
     window = jnp.sum(got.astype(jnp.float32), 0)
     high = window.astype(jnp.bfloat16)
     low = (window[0] - high[0].astype(jnp.float32)).astype(jnp.bfloat16)
     group = lax.broadcasted_iota(jnp.int32, (STRIP, 128), 1) >> 5
     rest = jnp.where(group == (sep & 3), high[2], jnp.concatenate([low[:, :32]] * 4, 1))
-    packed = jnp.concatenate([stiffness[0].T, start_block[0], high[0], high[1], rest], 1)
+    packed = jnp.concatenate([high[0], high[1], rest], 1)
     mine = lax.all_to_all(
         jnp.broadcast_to(packed[None], (PLANE, *packed.shape)),
         "leaf",
@@ -279,7 +300,8 @@
         tiled=True,
     )
     theirs = lax.ppermute(mine, "mode", SWAP)
-    return tuple(iterate(jnp.stack([core, device, sep]), mine, theirs, rotations[0]))
+    place = jnp.stack([core, device, sep])
+    return tuple(iterate(place, mine, theirs, known, known_other, rotations[0]))
 
 
 def solution(mesh):

time: 72.4 us -> 69.9 us (0.965)
  starting transfers between devices: 23.5 us -> 31.8 us
  waiting for transfers between devices: 21.4 us -> 13.5 us
  local copies, waits for them, and re-layouts: 1.5 us -> 0.05 us
  blocking collectives: 13.2 us -> 11.8 us
    ppermute x0 -> x7, starting transfers between devices: none -> 9.11 us  [the longest x6 6.09 us: gather_stage(): got = [lax.ppermute(value, AXES, plane_steps(d, stage)) for d in ORDER]]
    ppermute x6, waiting for transfers between devices: 10.8 us -> 5.44 us  [scatter_stage(): got = [lax.ppermute(pieces[d], AXES, plane_steps(d, stage)) for d in ORDER]]
    all_to_all x1, waiting for transfers between devices: 6.98 us -> 4.56 us  [per_device(): got = lax.all_to_all(routed, 'sep', split_axis=0, concat_axis=0, tiled=True)]
    all_to_all x1, blocking collectives: 13.2 us -> 11.8 us  [per_device(): lax.all_to_all(jnp.broadcast_to(packed[None], (PLANE, *packed.shape)), 'l...]
    unnamed x12, local copies, waits for them, and re-layouts: 1.45 us -> 0.03 us
  transfers between devices with their start and end apart: 10 -> 17, of which waited for: 6 -> 6; matrix products, arithmetic and copies ran while one was open for 2% -> 1% of each run, Pallas kernels for 0% -> 1%
where the time goes in v8:
time: 69.9 us; the launch traced here: 69.6 us
  starting transfers between devices  31.8 us (45%)
  waiting for transfers between devices  13.5 us (19%)
  blocking collectives  11.8 us (17%)
  Pallas kernels  6.42 us (9%)
  matrix products  4.89 us (7%)
  between operations  0.81 us (1%)
    all_to_all x1, blocking collectives, per_device(): lax.all_to_all(jnp.broadcast_to(packed[None], (PLANE, *packed.shape)), 'l...  11.8 us
    all_to_all x1, starting transfers between devices, per_device(): got = lax.all_to_all(routed, 'sep', split_axis=0, concat_axis=0, tiled=True)  7.44 us
    ppermute x6, starting transfers between devices, gather_stage(): got = [lax.ppermute(value, AXES, plane_steps(d, stage)) for d in ORDER]  6.09 us
    ppermute x6, starting transfers between devices, scatter_stage(): got = [lax.ppermute(pieces[d], AXES, plane_steps(d, stage)) for d in ORDER]  6.07 us
    ppermute x1, starting transfers between devices, per_device(): theirs = lax.ppermute(mine, 'mode', SWAP)  5.83 us
    ppermute x6, waiting for transfers between devices, scatter_stage(): got = [lax.ppermute(pieces[d], AXES, plane_steps(d, stage)) for d in ORDER]  5.44 us
    dot_general x1, matrix products, per_device(): jnp.einsum('ldw,ldm->lwm', coupling, modes, preferred_element_type=jnp.fl...  4.89 us
    all_to_all x1, waiting for transfers between devices, per_device(): got = lax.all_to_all(routed, 'sep', split_axis=0, concat_axis=0, tiled=True)  4.56 us
  transfers between devices with their start and end apart: 17, of which 6 were waited for; matrix products, arithmetic and copies ran while one was open for 1% of the time, Pallas kernels for 1%

profile of v8, /device:TPU:1, one launch (start us, length us, event | category | flops | bytes accessed | tf_op | source)
XLA Modules:
  0.0 69.6 jit_solution(1557788065922251799)
XLA Ops:
  0.7 4.9 %convolution_convert_fusion.own_ref = bf16[8,256,256]{2,1,0:T(8,128)(2,1)S(1)} fusion(bf16[8,1024,256]{2,1,0:T(8,128)(2,1)} %param.9, bf16[8,1024,256]{2,1,0:T(8,128)(2,1)} %param.8), kind=kOutput, calls=%fused_computation | convolution fusion | flops 1074266112 | bytes 9437184 | tf_op jit(solution)/shard_map/ldw,ldm->lwm/dot_general | solution.py:272
  5.6 0.0 copy-start
  5.6 3.3 %collective-permute-start = (bf16[8,256,256]{2,1,0:T(8,128)(2,1)S(1)}, bf16[8,256,256]{2,1,0:T(8,128)(2,1)S(1)}, u32[]{:S(2)}, u32[]{:S(2)}) collective-permute-start(bf16[8,256,256]{2,1,0:T(8,128)(2,1)S(1)} %convolution_convert_fusion.own_ref), channel_id=1, source_target_pairs={{0,1},{1,0},{2,3},{3,2},{4,5},{5,4},{6,7},{7,6},{8,9},{9,8},{10,11... | collective-permute-start | bytes 3145736 | tf_op jit(solution)/shard_map/ppermute | solution.py:275
  8.9 0.1 collective-permute-start.1
  9.0 0.1 pad_add_fusion.1.place_ref
  9.1 2.1 %collective-permute-done.1.other_eigen_ref = f32[8,128]{1,0:T(8,128)S(1)} collective-permute-done((f32[8,128]{1,0:T(8,128)S(1)}, f32[8,128]{1,0:T(8,128)S(1)}, u32[]{:S(2)}, u32[]{:S(2)}) %collective-permute-start.1) | collective-permute-done | bytes 4128 | tf_op jit(solution)/shard_map/ppermute | solution.py:271
  11.2 2.7 %gram.1 = (bf16[4,18,16,128]{3,2,1,0:T(8,128)(2,1)S(1)}, bf16[4,18,16,128]{3,2,1,0:T(8,128)(2,1)S(1)}, bf16[4,18,16,128]{3,2,1,0:T(8,128)(2,1)S(1)}, bf16[4,18,16,128]{3,2,1,0:T(8,128)(2,1)S(1)}) custom-call(s32[8]{0:T(128)S(1)} %bitcast.32, s32[8]{0:T(128)S(1)} %copy-done.3, s32[3]{0:T(128)S(1)} %pad_add_fusion.1.place_ref, ...), custom_call_target="tpu_custom_call" | custom-call | tf_op jit(solution)/shard_map/gram/pallas_call | solution.py:101
  13.9 0.1 collective-permute-start.2
  14.0 2.7 %collective-permute-start.3 = (bf16[4,18,16,128]{3,2,1,0:T(8,128)(2,1)S(1)}, bf16[4,18,16,128]{3,2,1,0:T(8,128)(2,1)S(1)}, u32[]{:S(2)}, u32[]{:S(2)}) collective-permute-start(bf16[4,18,16,128]{3,2,1,0:T(8,128)(2,1)S(1)} %get-tuple-element.15), channel_id=1, source_target_pairs={{0,48},{1,193},{2,50},{3,195},{4,52},{5,197},{6,54},{7,199},{8,56}... | collective-permute-start | bytes 884744 | tf_op jit(solution)/shard_map/ppermute | solution.py:260
  16.6 1.3 %collective-permute-start.11 = (bf16[16,768]{1,0:T(8,128)(2,1)S(1)}, bf16[16,768]{1,0:T(8,128)(2,1)S(1)}, u32[]{:S(2)}, u32[]{:S(2)}) collective-permute-start(bf16[16,768]{1,0:T(8,128)(2,1)S(1)} %pad_maximum_fusion.2), channel_id=1, source_target_pairs={{0,48},{1,193},{2,50},{3,195},{4,52},{5,197},{6,54},{7,199},{8,56}... | collective-permute-start | bytes 73736 | tf_op jit(solution)/shard_map/ppermute | solution.py:255
  18.0 1.8 %collective-permute-start.10 = (bf16[16,768]{1,0:T(8,128)(2,1)S(1)}, bf16[16,768]{1,0:T(8,128)(2,1)S(1)}, u32[]{:S(2)}, u32[]{:S(2)}) collective-permute-start(bf16[16,768]{1,0:T(8,128)(2,1)S(1)} %pad_maximum_fusion.2), channel_id=1, source_target_pairs={{0,32},{1,129},{2,34},{3,131},{4,36},{5,133},{6,38},{7,135},{8,40}... | collective-permute-start | bytes 73736 | tf_op jit(solution)/shard_map/ppermute | solution.py:255
  19.8 4.7 %collective-permute-done.2.refs_1_ = bf16[4,18,16,128]{3,2,1,0:T(8,128)(2,1)S(1)} collective-permute-done((bf16[4,18,16,128]{3,2,1,0:T(8,128)(2,1)S(1)}, bf16[4,18,16,128]{3,2,1,0:T(8,128)(2,1)S(1)}, u32[]{:S(2)}, u32[]{:S(2)}) %collective-permute-start.2) | collective-permute-done | bytes 294944 | tf_op jit(solution)/shard_map/ppermute | solution.py:260
  24.5 0.1 split_kernel.1
  24.6 0.3 collective-permute-start.5
  24.9 2.4 %collective-permute-start.6 = (bf16[18,16,128]{2,1,0:T(8,128)(2,1)S(1)}, bf16[18,16,128]{2,1,0:T(8,128)(2,1)S(1)}, u32[]{:S(2)}, u32[]{:S(2)}) collective-permute-start(bf16[18,16,128]{2,1,0:T(8,128)(2,1)S(1)} %get-tuple-element.19), channel_id=1, source_target_pairs={{0,192},{1,49},{2,194},{3,51},{4,196},{5,53},{6,198},{7,55},{8,200... | collective-permute-start | bytes 221192 | tf_op jit(solution)/shard_map/ppermute | solution.py:260
  27.4 0.6 collective-permute-start.7
  27.9 0.4 collective-permute-done.9
  28.3 0.6 collective-permute-start.14
  28.9 1.8 %collective-permute-start.13 = (bf16[4,16,768]{2,1,0:T(8,128)(2,1)S(1)}, bf16[4,16,768]{2,1,0:T(8,128)(2,1)S(1)}, u32[]{:S(2)}, u32[]{:S(2)}) collective-permute-start(bf16[4,16,768]{2,1,0:T(8,128)(2,1)S(1)} %pad_maximum_fusion.1), channel_id=1, source_target_pairs={{0,128},{1,33},{2,130},{3,35},{4,132},{5,37},{6,134},{7,39},{8,136... | collective-permute-start | bytes 294920 | tf_op jit(solution)/shard_map/ppermute | solution.py:255
  30.7 0.6 collective-permute-start.12
  31.3 0.8 %collective-permute-done.7.refs_3_ = bf16[18,16,128]{2,1,0:T(8,128)(2,1)S(1)} collective-permute-done((bf16[18,16,128]{2,1,0:T(8,128)(2,1)S(1)}, bf16[18,16,128]{2,1,0:T(8,128)(2,1)S(1)}, u32[]{:S(2)}, u32[]{:S(2)}) %collective-permute-start.7) | collective-permute-done | bytes 73760 | tf_op jit(solution)/shard_map/ppermute | solution.py:260
  32.1 0.7 route_kernel.1
  32.8 7.4 %all-to-all-start = ((bf16[8,3,16,128]{3,2,1,0:T(8,128)(2,1)}), bf16[8,3,16,128]{3,2,1,0:T(8,128)(2,1)S(1)}, u32[]{:S(2)}, u32[]{:S(2)}) async-start(bf16[8,3,16,128]{3,2,1,0:T(8,128)(2,1)} %route_kernel.1), calls=%async_computation | async-start | bytes 196608 | tf_op jit(solution)/shard_map/all_to_all | solution.py:288
  40.2 0.1 pad_maximum_fusion.known_ref
  40.3 3.0 %collective-permute-start.15 = (bf16[4,4,16,768]{3,2,1,0:T(8,128)(2,1)S(1)}, bf16[4,4,16,768]{3,2,1,0:T(8,128)(2,1)S(1)}, u32[]{:S(2)}, u32[]{:S(2)}) collective-permute-start(bf16[4,4,16,768]{3,2,1,0:T(8,128)(2,1)S(1)} %pad_maximum_fusion.known_ref), channel_id=1, source_target_pairs={{0,1},{1,0},{2,3},{3,2},{4,5},{5,4},{6,7},{7,6},{8,9},{9,8},{10,11... | collective-permute-start | bytes 1179656 | tf_op jit(solution)/shard_map/ppermute | solution.py:287
  43.3 4.6 %all-to-all-done = bf16[8,3,16,128]{3,2,1,0:T(8,128)(2,1)S(1)} async-done(((bf16[8,3,16,128]{3,2,1,0:T(8,128)(2,1)}), bf16[8,3,16,128]{3,2,1,0:T(8,128)(2,1)S(1)}, u32[]{:S(2)}, u32[]{:S(2)}) %all-to-all-start) | async-done | bytes 98336 | tf_op jit(solution)/shard_map/all_to_all | solution.py:288
  47.9 0.1 fusion.1
  48.1 11.8 %all_to_all.10.own_ref = bf16[16,16,384]{2,1,0:T(8,128)(2,1)S(1)} all-to-all(bf16[16,16,384]{2,1,0:T(8,128)(2,1)S(1)} %broadcast_in_dim.2), channel_id=1, replica_groups=mesh['leaf'=16,'sep'=8,'mode'=2] {'leaf'}, dimensions={0} | all-to-all | bytes 393216 | tf_op jit(solution)/shard_map/all_to_all | solution.py:295
  59.8 5.8 %collective-permute-start.8 = (bf16[16,16,384]{2,1,0:T(8,128)(2,1)S(1)}, bf16[16,16,384]{2,1,0:T(8,128)(2,1)S(1)}, u32[]{:S(2)}, u32[]{:S(2)}) collective-permute-start(bf16[16,16,384]{2,1,0:T(8,128)(2,1)S(1)} %all_to_all.10.own_ref), channel_id=1, source_target_pairs={{0,1},{1,0},{2,3},{3,2},{4,5},{5,4},{6,7},{7,6},{8,9},{9,8},{10,11... | collective-permute-start | bytes 589832 | tf_op jit(solution)/shard_map/ppermute | solution.py:302
  65.7 0.1 pad_add_fusion.place_ref
  65.7 1.0 %collective-permute-done.8.other_ref = bf16[16,16,384]{2,1,0:T(8,128)(2,1)S(1)} collective-permute-done((bf16[16,16,384]{2,1,0:T(8,128)(2,1)S(1)}, bf16[16,16,384]{2,1,0:T(8,128)(2,1)S(1)}, u32[]{:S(2)}, u32[]{:S(2)}) %collective-permute-start.8) | collective-permute-done | bytes 196640 | tf_op jit(solution)/shard_map/ppermute | solution.py:302
  66.7 2.9 %iterate.1 = (bf16[1,16,256]{2,1,0:T(8,128)(2,1)}, f32[1,2,256]{2,1,0:T(2,128)}) custom-call(s32[3]{0:T(128)S(1)} %pad_add_fusion.place_ref, bf16[16,16,384]{2,1,0:T(8,128)(2,1)S(1)} %all_to_all.10.own_ref, bf16[16,16,384]{2,1,0:T(8,128)(2,1)S(1)} %collective-permute-done.8.other_ref, bf16[4,4,16,768]{3,2,1,0:T(8,128)(2,1)S(1)} %pad_maximum_fusion.known_ref, ...), custom_call_target="tpu_custom_call" | custom-call | tf_op jit(solution)/shard_map/iterate/pallas_call | solution.py:211
  (34 shorter events, 0.1 us)
Async XLA Ops:
  0.6 8.2 %copy-start.1 = (f32[8,128]{1,0:T(8,128)S(1)}, f32[8,128]{1,0:T(8,128)}, u32[]{:S(2)}) copy-start(f32[8,128]{1,0:T(8,128)} %eigen_ref.1) | copy-start | bytes 12292
  0.6 10.5 %copy-start.2 = (s32[8,1]{0,1:T(1,128)S(1)}, s32[8,1]{0,1:T(1,128)}, u32[]{:S(2)}) copy-start(s32[8,1]{0,1:T(1,128)} %param.11) | copy-start | bytes 100
  0.7 10.5 %copy-start.3 = (s32[8]{0:T(128)S(1)}, s32[8]{0:T(128)}, u32[]{:S(2)}) copy-start(s32[8]{0:T(128)} %offset_ref.1) | copy-start | bytes 100
  0.7 16.0 %copy-start.5 = (bf16[1,16,256]{2,1,0:T(8,128)(2,1)S(1)}, bf16[1,16,256]{2,1,0:T(8,128)(2,1)}, u32[]{:S(2)}) copy-start(bf16[1,16,256]{2,1,0:T(8,128)(2,1)} %param.14) | copy-start | bytes 24580
  0.7 16.0 %copy-start.4 = (bf16[1,512,16]{1,2,0:T(8,128)(2,1)S(1)}, bf16[1,512,16]{1,2,0:T(8,128)(2,1)}, u32[]{:S(2)}) copy-start(bf16[1,512,16]{1,2,0:T(8,128)(2,1)} %param.13) | copy-start | bytes 49156
  5.6 61.2 %copy-start = (bf16[1,2,256,256]{3,2,1,0:T(8,128)(2,1)S(1)}, bf16[1,2,256,256]{3,2,1,0:T(8,128)(2,1)}, u32[]{:S(2)}) copy-start(bf16[1,2,256,256]{3,2,1,0:T(8,128)(2,1)} %param.15) | copy-start | bytes 786436
  5.6 5.6 %collective-permute-start = (bf16[8,256,256]{2,1,0:T(8,128)(2,1)S(1)}, bf16[8,256,256]{2,1,0:T(8,128)(2,1)S(1)}, u32[]{:S(2)}, u32[]{:S(2)}) collective-permute-start(bf16[8,256,256]{2,1,0:T(8,128)(2,1)S(1)} %convolution_convert_fusion.own_ref), channel_id=1, source_target_pairs={{0,1},{1,0},{2,3},{3,2},{4,5},{5,4},{6,7},{7,6},{8,9},{9,8},{10,11... | collective-permute-start | bytes 3145736 | tf_op jit(solution)/shard_map/ppermute | solution.py:275
  8.9 2.3 %collective-permute-start.1 = (f32[8,128]{1,0:T(8,128)S(1)}, f32[8,128]{1,0:T(8,128)S(1)}, u32[]{:S(2)}, u32[]{:S(2)}) collective-permute-start(f32[8,128]{1,0:T(8,128)S(1)} %copy-done.1), channel_id=1, source_target_pairs={{0,1},{1,0},{2,3},{3,2},{4,5},{5,4},{6,7},{7,6},{8,9},{9,8},{10,11... | collective-permute-start | bytes 12296 | tf_op jit(solution)/shard_map/ppermute | solution.py:271
  13.9 10.6 %collective-permute-start.2 = (bf16[4,18,16,128]{3,2,1,0:T(8,128)(2,1)S(1)}, bf16[4,18,16,128]{3,2,1,0:T(8,128)(2,1)S(1)}, u32[]{:S(2)}, u32[]{:S(2)}) collective-permute-start(bf16[4,18,16,128]{3,2,1,0:T(8,128)(2,1)S(1)} %get-tuple-element.14), channel_id=1, source_target_pairs={{0,16},{1,65},{2,18},{3,67},{4,20},{5,69},{6,22},{7,71},{8,24},{9,... | collective-permute-start | bytes 884744 | tf_op jit(solution)/shard_map/ppermute | solution.py:260
  14.0 10.5 %collective-permute-start.3 = (bf16[4,18,16,128]{3,2,1,0:T(8,128)(2,1)S(1)}, bf16[4,18,16,128]{3,2,1,0:T(8,128)(2,1)S(1)}, u32[]{:S(2)}, u32[]{:S(2)}) collective-permute-start(bf16[4,18,16,128]{3,2,1,0:T(8,128)(2,1)S(1)} %get-tuple-element.15), channel_id=1, source_target_pairs={{0,48},{1,193},{2,50},{3,195},{4,52},{5,197},{6,54},{7,199},{8,56}... | collective-permute-start | bytes 884744 | tf_op jit(solution)/shard_map/ppermute | solution.py:260
  16.6 7.8 %collective-permute-start.4 = (bf16[4,18,16,128]{3,2,1,0:T(8,128)(2,1)S(1)}, bf16[4,18,16,128]{3,2,1,0:T(8,128)(2,1)S(1)}, u32[]{:S(2)}, u32[]{:S(2)}) collective-permute-start(bf16[4,18,16,128]{3,2,1,0:T(8,128)(2,1)S(1)} %get-tuple-element.16), channel_id=1, source_target_pairs={{0,32},{1,129},{2,34},{3,131},{4,36},{5,133},{6,38},{7,135},{8,40}... | collective-permute-start | bytes 884744 | tf_op jit(solution)/shard_map/ppermute | solution.py:260
  16.6 10.7 %collective-permute-start.11 = (bf16[16,768]{1,0:T(8,128)(2,1)S(1)}, bf16[16,768]{1,0:T(8,128)(2,1)S(1)}, u32[]{:S(2)}, u32[]{:S(2)}) collective-permute-start(bf16[16,768]{1,0:T(8,128)(2,1)S(1)} %pad_maximum_fusion.2), channel_id=1, source_target_pairs={{0,48},{1,193},{2,50},{3,195},{4,52},{5,197},{6,54},{7,199},{8,56}... | collective-permute-start | bytes 73736 | tf_op jit(solution)/shard_map/ppermute | solution.py:255
  18.0 10.0 %collective-permute-start.10 = (bf16[16,768]{1,0:T(8,128)(2,1)S(1)}, bf16[16,768]{1,0:T(8,128)(2,1)S(1)}, u32[]{:S(2)}, u32[]{:S(2)}) collective-permute-start(bf16[16,768]{1,0:T(8,128)(2,1)S(1)} %pad_maximum_fusion.2), channel_id=1, source_target_pairs={{0,32},{1,129},{2,34},{3,131},{4,36},{5,133},{6,38},{7,135},{8,40}... | collective-permute-start | bytes 73736 | tf_op jit(solution)/shard_map/ppermute | solution.py:255
  24.4 3.9 %collective-permute-start.9 = (bf16[16,768]{1,0:T(8,128)(2,1)S(1)}, bf16[16,768]{1,0:T(8,128)(2,1)S(1)}, u32[]{:S(2)}, u32[]{:S(2)}) collective-permute-start(bf16[16,768]{1,0:T(8,128)(2,1)S(1)} %pad_maximum_fusion.2), channel_id=1, source_target_pairs={{0,16},{1,65},{2,18},{3,67},{4,20},{5,69},{6,22},{7,71},{8,24},{9,... | collective-permute-start | bytes 73736 | tf_op jit(solution)/shard_map/ppermute | solution.py:255
  24.6 6.1 %collective-permute-start.5 = (bf16[18,16,128]{2,1,0:T(8,128)(2,1)S(1)}, bf16[18,16,128]{2,1,0:T(8,128)(2,1)S(1)}, u32[]{:S(2)}, u32[]{:S(2)}) collective-permute-start(bf16[18,16,128]{2,1,0:T(8,128)(2,1)S(1)} %get-tuple-element.18), channel_id=1, source_target_pairs={{0,64},{1,17},{2,66},{3,19},{4,68},{5,21},{6,70},{7,23},{8,72},{9,... | collective-permute-start | bytes 221192 | tf_op jit(solution)/shard_map/ppermute | solution.py:260
  24.9 6.4 %collective-permute-start.6 = (bf16[18,16,128]{2,1,0:T(8,128)(2,1)S(1)}, bf16[18,16,128]{2,1,0:T(8,128)(2,1)S(1)}, u32[]{:S(2)}, u32[]{:S(2)}) collective-permute-start(bf16[18,16,128]{2,1,0:T(8,128)(2,1)S(1)} %get-tuple-element.19), channel_id=1, source_target_pairs={{0,192},{1,49},{2,194},{3,51},{4,196},{5,53},{6,198},{7,55},{8,200... | collective-permute-start | bytes 221192 | tf_op jit(solution)/shard_map/ppermute | solution.py:260
  27.4 4.7 %collective-permute-start.7 = (bf16[18,16,128]{2,1,0:T(8,128)(2,1)S(1)}, bf16[18,16,128]{2,1,0:T(8,128)(2,1)S(1)}, u32[]{:S(2)}, u32[]{:S(2)}) collective-permute-start(bf16[18,16,128]{2,1,0:T(8,128)(2,1)S(1)} %get-tuple-element.20), channel_id=1, source_target_pairs={{0,128},{1,33},{2,130},{3,35},{4,132},{5,37},{6,134},{7,39},{8,136... | collective-permute-start | bytes 221192 | tf_op jit(solution)/shard_map/ppermute | solution.py:260
  28.3 11.9 %collective-permute-start.14 = (bf16[4,16,768]{2,1,0:T(8,128)(2,1)S(1)}, bf16[4,16,768]{2,1,0:T(8,128)(2,1)S(1)}, u32[]{:S(2)}, u32[]{:S(2)}) collective-permute-start(bf16[4,16,768]{2,1,0:T(8,128)(2,1)S(1)} %pad_maximum_fusion.1), channel_id=1, source_target_pairs={{0,192},{1,49},{2,194},{3,51},{4,196},{5,53},{6,198},{7,55},{8,200... | collective-permute-start | bytes 294920 | tf_op jit(solution)/shard_map/ppermute | solution.py:255
  28.9 11.3 %collective-permute-start.13 = (bf16[4,16,768]{2,1,0:T(8,128)(2,1)S(1)}, bf16[4,16,768]{2,1,0:T(8,128)(2,1)S(1)}, u32[]{:S(2)}, u32[]{:S(2)}) collective-permute-start(bf16[4,16,768]{2,1,0:T(8,128)(2,1)S(1)} %pad_maximum_fusion.1), channel_id=1, source_target_pairs={{0,128},{1,33},{2,130},{3,35},{4,132},{5,37},{6,134},{7,39},{8,136... | collective-permute-start | bytes 294920 | tf_op jit(solution)/shard_map/ppermute | solution.py:255
  30.7 9.5 %collective-permute-start.12 = (bf16[4,16,768]{2,1,0:T(8,128)(2,1)S(1)}, bf16[4,16,768]{2,1,0:T(8,128)(2,1)S(1)}, u32[]{:S(2)}, u32[]{:S(2)}) collective-permute-start(bf16[4,16,768]{2,1,0:T(8,128)(2,1)S(1)} %pad_maximum_fusion.1), channel_id=1, source_target_pairs={{0,64},{1,17},{2,66},{3,19},{4,68},{5,21},{6,70},{7,23},{8,72},{9,... | collective-permute-start | bytes 294920 | tf_op jit(solution)/shard_map/ppermute | solution.py:255
  32.8 15.1 %all-to-all-start = ((bf16[8,3,16,128]{3,2,1,0:T(8,128)(2,1)}), bf16[8,3,16,128]{3,2,1,0:T(8,128)(2,1)S(1)}, u32[]{:S(2)}, u32[]{:S(2)}) async-start(bf16[8,3,16,128]{3,2,1,0:T(8,128)(2,1)} %route_kernel.1), calls=%async_computation | async-start | bytes 196608 | tf_op jit(solution)/shard_map/all_to_all | solution.py:288
  40.3 25.4 %collective-permute-start.15 = (bf16[4,4,16,768]{3,2,1,0:T(8,128)(2,1)S(1)}, bf16[4,4,16,768]{3,2,1,0:T(8,128)(2,1)S(1)}, u32[]{:S(2)}, u32[]{:S(2)}) collective-permute-start(bf16[4,4,16,768]{3,2,1,0:T(8,128)(2,1)S(1)} %pad_maximum_fusion.known_ref), channel_id=1, source_target_pairs={{0,1},{1,0},{2,3},{3,2},{4,5},{5,4},{6,7},{7,6},{8,9},{9,8},{10,11... | collective-permute-start | bytes 1179656 | tf_op jit(solution)/shard_map/ppermute | solution.py:287
  59.8 6.9 %collective-permute-start.8 = (bf16[16,16,384]{2,1,0:T(8,128)(2,1)S(1)}, bf16[16,16,384]{2,1,0:T(8,128)(2,1)S(1)}, u32[]{:S(2)}, u32[]{:S(2)}) collective-permute-start(bf16[16,16,384]{2,1,0:T(8,128)(2,1)S(1)} %all_to_all.10.own_ref), channel_id=1, source_target_pairs={{0,1},{1,0},{2,3},{3,2},{4,5},{5,4},{6,7},{7,6},{8,9},{9,8},{10,11... | collective-permute-start | bytes 589832 | tf_op jit(solution)/shard_map/ppermute | solution.py:302

commit v9 on v8

--- a/solution.py
+++ b/solution.py
@@ -20,6 +20,26 @@
 STRIP = 16
 ITERS = 2
 epsilon = 1e-06
+
+
+def project_kernel(coupling_ref, modes_ref, out_ref):
+    out_ref[0] = lax.dot_general(
+        coupling_ref[0], modes_ref[0], (((0,), (0,)), ((), ())), preferred_element_type=jnp.float32
+    ).astype(jnp.bfloat16)
+
+
+def project(coupling, modes):
+    count, rows, columns = coupling.shape
+    block = pl.BlockSpec((1, rows, columns), lambda l: (l, 0, 0))
+    return pl.pallas_call(
+        project_kernel,
+        grid=(count,),
+        in_specs=[block, block],
+        out_specs=pl.BlockSpec((1, columns, columns), lambda l: (l, 0, 0)),
+        out_shape=jax.ShapeDtypeStruct((count, columns, columns), jnp.bfloat16),
+        compiler_params=pltpu.CompilerParams(vmem_limit_bytes=16 << 20),
+        name="project",
+    )(*[pltpu.with_memory_space_constraint(x, pltpu.HBM) for x in (coupling, modes)])
 
 
 def place_of(d, e, place_ref):
@@ -146,7 +166,7 @@
 
 
 def iterate_kernel(
-    place_ref, own_ref, other_ref, known_ref, known_other_ref, turns_ref, out_ref, norms_ref, kt_ref, m_ref, high_ref, x_ref
+    place_ref, window_ref, known_ref, known_other_ref, turns_ref, out_ref, norms_ref, kt_ref, m_ref, high_ref, x_ref
 ):
     core, device, sep = place_ref[0], place_ref[1], place_ref[2]
     leaf = device >> 1
@@ -155,7 +175,7 @@
     halved = jnp.where(lane < 32, 0.5, 1.0)
     rest_weight = jnp.where(lane < 32, 0.5, 0.0)
     back = (128 - 32 * (sep & 3)) & 127
-    for ref, known, which in ((own_ref, known_ref, core), (other_ref, known_other_ref, 1 - core)):
+    for known, which in ((known_ref, core), (known_other_ref, 1 - core)):
         for e in range(SIDE):
             for d in range(SIDE):
                 up = (y - jnp.where(which == 0, e, d)) & (SIDE - 1)
@@ -164,16 +184,16 @@
                 rows = pl.ds(pl.multiple_of(start, STRIP), STRIP)
                 kt_ref[rows, :] = known[e, d, :, :SEP_ROWS]
                 x_ref[rows, :] = known[e, d, :, SEP_ROWS:]
-        for g in range(PLANE):
-            rows = pl.ds(pl.multiple_of(32 * g + 16 * which, STRIP), STRIP)
-            rest = pltpu.roll(ref[g, :, 256:384].astype(jnp.float32), back, axis=1)
-            low = jnp.where(lane < 32, pltpu.roll(rest, 96, axis=1), 0.0)
-            first = ref[g, :, :128].astype(jnp.float32) + low
-            second = ref[g, :, 128:256].astype(jnp.float32)
-            window = jnp.concatenate(
-                [first * halved, second, rest * rest_weight, jnp.zeros_like(second)], axis=1
-            )
-            m_ref[rows, :] = pltpu.roll(window, 32 * g, axis=1) if g else window
+    for k in range(2 * PLANE):
+        rest = pltpu.roll(window_ref[k, :, 256:384].astype(jnp.float32), back, axis=1)
+        low = jnp.where(lane < 32, pltpu.roll(rest, 96, axis=1), 0.0)
+        first = window_ref[k, :, :128].astype(jnp.float32) + low
+        second = window_ref[k, :, 128:256].astype(jnp.float32)
+        window = jnp.concatenate(
+            [first * halved, second, rest * rest_weight, jnp.zeros_like(second)], axis=1
+        )
+        shift = 32 * (k // 2)
+        m_ref[STRIP * k : STRIP * (k + 1), :] = pltpu.roll(window, shift, axis=1) if shift else window
     half = m_ref[...]
     operator = jnp.transpose(kt_ref[...].astype(jnp.float32) - half) - half
     high = operator.astype(jnp.bfloat16)
@@ -269,9 +289,7 @@
     core = lax.axis_index("mode").astype(jnp.int32)
     device = lax.axis_index(("leaf", "mode")).astype(jnp.int32)
     other_eigen = lax.ppermute(eigenvalues, "mode", SWAP)
-    own = jnp.einsum("ldw,ldm->lwm", coupling, modes, preferred_element_type=jnp.float32).astype(
-        jnp.bfloat16
-    )
+    own = project(coupling, modes)
     other = lax.ppermute(own, "mode", SWAP)
     sep = lax.axis_index("sep").astype(jnp.int32)
     leaf = lax.axis_index("leaf").astype(jnp.int32)
@@ -292,16 +310,15 @@
     group = lax.broadcasted_iota(jnp.int32, (STRIP, 128), 1) >> 5
     rest = jnp.where(group == (sep & 3), high[2], jnp.concatenate([low[:, :32]] * 4, 1))
     packed = jnp.concatenate([high[0], high[1], rest], 1)
-    mine = lax.all_to_all(
-        jnp.broadcast_to(packed[None], (PLANE, *packed.shape)),
-        "leaf",
+    windows = lax.all_to_all(
+        jnp.broadcast_to(packed[None], (2 * PLANE, *packed.shape)),
+        ("leaf", "mode"),
         split_axis=0,
         concat_axis=0,
         tiled=True,
     )
-    theirs = lax.ppermute(mine, "mode", SWAP)
     place = jnp.stack([core, device, sep])
-    return tuple(iterate(place, mine, theirs, known, known_other, rotations[0]))
+    return tuple(iterate(place, windows, known, known_other, rotations[0]))
 
 
 def solution(mesh):

time: 69.9 us -> 73.8 us (1.056)
  blocking collectives: 11.8 us -> 0 us
  waiting for transfers between devices: 13.5 us -> 22.6 us
  Pallas kernels: 6.42 us -> 13.3 us
  matrix products: 4.89 us -> 0 us
  starting transfers between devices: 31.8 us -> 35.5 us
  local copies, waits for them, and re-layouts: 0.05 us -> 0.81 us
    all_to_all x1 -> x0, blocking collectives: 11.8 us -> none  [per_device(): lax.all_to_all(jnp.broadcast_to(packed[None], (PLANE, *packed.shape)), 'l...]
    all_to_all x0 -> x1, waiting for transfers between devices: none -> 10.1 us  [per_device(): lax.all_to_all(jnp.broadcast_to(packed[None], (2 * PLANE, *packed.shape))...]
    all_to_all x0 -> x1, starting transfers between devices: none -> 9.5 us  [per_device(): lax.all_to_all(jnp.broadcast_to(packed[None], (2 * PLANE, *packed.shape))...]
    pallas_call x0 -> x1, Pallas kernels: none -> 6.85 us  [project(): pl.pallas_call(project_kernel, grid=(count,), in_specs=[block, block], ou...]
    ppermute x1 -> x0, starting transfers between devices: 5.83 us -> none  [per_device(): theirs = lax.ppermute(mine, 'mode', SWAP)]
    dot_general x1 -> x0, matrix products: 4.89 us -> none  [per_device(): jnp.einsum('ldw,ldm->lwm', coupling, modes, preferred_element_type=jnp.fl...]
    ppermute x1 -> x0, waiting for transfers between devices: 0.99 us -> none  [per_device(): theirs = lax.ppermute(mine, 'mode', SWAP)]
    broadcast_in_dim x1, local copies, waits for them, and re-layouts: 0.02 us -> 0.78 us  [per_device(): jnp.broadcast_to(packed[None], (2 * PLANE, *packed.shape))]
  transfers between devices with their start and end apart: 17 -> 17, of which waited for: 6 -> 6; matrix products, arithmetic and copies ran while one was open for 1% -> 2% of each run, Pallas kernels for 1% -> 1%
where the time goes in v9:
time: 73.8 us; the launch traced here: 73.4 us
  starting transfers between devices  35.5 us (48%)
  waiting for transfers between devices  22.6 us (31%)
  Pallas kernels  13.3 us (18%)
  between operations  0.82 us (1%)
  local copies, waits for them, and re-layouts  0.81 us (1%)
    all_to_all x1, waiting for transfers between devices, per_device(): lax.all_to_all(jnp.broadcast_to(packed[None], (2 * PLANE, *packed.shape))...  10.1 us
    all_to_all x1, starting transfers between devices, per_device(): lax.all_to_all(jnp.broadcast_to(packed[None], (2 * PLANE, *packed.shape))...  9.5 us
    all_to_all x1, starting transfers between devices, per_device(): got = lax.all_to_all(routed, 'sep', split_axis=0, concat_axis=0, tiled=True)  7.45 us
    pallas_call x1, Pallas kernels, project(): pl.pallas_call(project_kernel, grid=(count,), in_specs=[block, block], ou...  6.85 us
    ppermute x6, starting transfers between devices, gather_stage(): got = [lax.ppermute(value, AXES, plane_steps(d, stage)) for d in ORDER]  6.09 us
    ppermute x6, starting transfers between devices, scatter_stage(): got = [lax.ppermute(pieces[d], AXES, plane_steps(d, stage)) for d in ORDER]  6.08 us
    ppermute x6, waiting for transfers between devices, scatter_stage(): got = [lax.ppermute(pieces[d], AXES, plane_steps(d, stage)) for d in ORDER]  5.44 us
    all_to_all x1, waiting for transfers between devices, per_device(): got = lax.all_to_all(routed, 'sep', split_axis=0, concat_axis=0, tiled=True)  4.56 us
  transfers between devices with their start and end apart: 17, of which 6 were waited for; matrix products, arithmetic and copies ran while one was open for 2% of the time, Pallas kernels for 1%

profile of v9, /device:TPU:1, one launch (start us, length us, event | category | flops | bytes accessed | tf_op | source)
XLA Modules:
  0.0 73.4 jit_solution(15687899191393317154)
XLA Ops:
  0.7 6.8 %project.1.own_ref = bf16[8,256,256]{2,1,0:T(8,128)(2,1)S(1)} custom-call(bf16[8,1024,256]{2,1,0:T(8,128)(2,1)} %coupling_ref.1, bf16[8,1024,256]{2,1,0:T(8,128)(2,1)} %modes_ref.1), custom_call_target="tpu_custom_call" | custom-call | tf_op jit(solution)/shard_map/project/pallas_call | solution.py:34
  7.5 0.0 copy-start
  7.5 3.3 %collective-permute-start = (bf16[8,256,256]{2,1,0:T(8,128)(2,1)S(1)}, bf16[8,256,256]{2,1,0:T(8,128)(2,1)S(1)}, u32[]{:S(2)}, u32[]{:S(2)}) collective-permute-start(bf16[8,256,256]{2,1,0:T(8,128)(2,1)S(1)} %project.1.own_ref), channel_id=1, source_target_pairs={{0,1},{1,0},{2,3},{3,2},{4,5},{5,4},{6,7},{7,6},{8,9},{9,8},{10,11... | collective-permute-start | bytes 3145736 | tf_op jit(solution)/shard_map/ppermute | solution.py:293
  10.8 0.1 collective-permute-start.1
  10.9 0.1 pad_add_fusion.1.place_ref
  11.0 2.1 %collective-permute-done.1.other_eigen_ref = f32[8,128]{1,0:T(8,128)S(1)} collective-permute-done((f32[8,128]{1,0:T(8,128)S(1)}, f32[8,128]{1,0:T(8,128)S(1)}, u32[]{:S(2)}, u32[]{:S(2)}) %collective-permute-start.1) | collective-permute-done | bytes 4128 | tf_op jit(solution)/shard_map/ppermute | solution.py:291
  13.1 2.7 %gram.1 = (bf16[4,18,16,128]{3,2,1,0:T(8,128)(2,1)S(1)}, bf16[4,18,16,128]{3,2,1,0:T(8,128)(2,1)S(1)}, bf16[4,18,16,128]{3,2,1,0:T(8,128)(2,1)S(1)}, bf16[4,18,16,128]{3,2,1,0:T(8,128)(2,1)S(1)}) custom-call(s32[8]{0:T(128)S(1)} %bitcast.30, s32[8]{0:T(128)S(1)} %copy-done.3, s32[3]{0:T(128)S(1)} %pad_add_fusion.1.place_ref, ...), custom_call_target="tpu_custom_call" | custom-call | tf_op jit(solution)/shard_map/gram/pallas_call | solution.py:121
  15.8 0.1 collective-permute-start.2
  15.9 2.7 %collective-permute-start.3 = (bf16[4,18,16,128]{3,2,1,0:T(8,128)(2,1)S(1)}, bf16[4,18,16,128]{3,2,1,0:T(8,128)(2,1)S(1)}, u32[]{:S(2)}, u32[]{:S(2)}) collective-permute-start(bf16[4,18,16,128]{3,2,1,0:T(8,128)(2,1)S(1)} %get-tuple-element.15), channel_id=1, source_target_pairs={{0,48},{1,193},{2,50},{3,195},{4,52},{5,197},{6,54},{7,199},{8,56}... | collective-permute-start | bytes 884744 | tf_op jit(solution)/shard_map/ppermute | solution.py:280
  18.6 1.3 %collective-permute-start.10 = (bf16[16,768]{1,0:T(8,128)(2,1)S(1)}, bf16[16,768]{1,0:T(8,128)(2,1)S(1)}, u32[]{:S(2)}, u32[]{:S(2)}) collective-permute-start(bf16[16,768]{1,0:T(8,128)(2,1)S(1)} %pad_maximum_fusion.2), channel_id=1, source_target_pairs={{0,48},{1,193},{2,50},{3,195},{4,52},{5,197},{6,54},{7,199},{8,56}... | collective-permute-start | bytes 73736 | tf_op jit(solution)/shard_map/ppermute | solution.py:275
  19.9 1.8 %collective-permute-start.9 = (bf16[16,768]{1,0:T(8,128)(2,1)S(1)}, bf16[16,768]{1,0:T(8,128)(2,1)S(1)}, u32[]{:S(2)}, u32[]{:S(2)}) collective-permute-start(bf16[16,768]{1,0:T(8,128)(2,1)S(1)} %pad_maximum_fusion.2), channel_id=1, source_target_pairs={{0,32},{1,129},{2,34},{3,131},{4,36},{5,133},{6,38},{7,135},{8,40}... | collective-permute-start | bytes 73736 | tf_op jit(solution)/shard_map/ppermute | solution.py:275
  21.7 4.7 %collective-permute-done.2.refs_1_ = bf16[4,18,16,128]{3,2,1,0:T(8,128)(2,1)S(1)} collective-permute-done((bf16[4,18,16,128]{3,2,1,0:T(8,128)(2,1)S(1)}, bf16[4,18,16,128]{3,2,1,0:T(8,128)(2,1)S(1)}, u32[]{:S(2)}, u32[]{:S(2)}) %collective-permute-start.2) | collective-permute-done | bytes 294944 | tf_op jit(solution)/shard_map/ppermute | solution.py:280
  26.4 0.1 split_kernel.1
  26.6 0.3 collective-permute-start.5
  26.9 2.4 %collective-permute-start.6 = (bf16[18,16,128]{2,1,0:T(8,128)(2,1)S(1)}, bf16[18,16,128]{2,1,0:T(8,128)(2,1)S(1)}, u32[]{:S(2)}, u32[]{:S(2)}) collective-permute-start(bf16[18,16,128]{2,1,0:T(8,128)(2,1)S(1)} %get-tuple-element.19), channel_id=1, source_target_pairs={{0,192},{1,49},{2,194},{3,51},{4,196},{5,53},{6,198},{7,55},{8,200... | collective-permute-start | bytes 221192 | tf_op jit(solution)/shard_map/ppermute | solution.py:280
  29.3 0.6 collective-permute-start.7
  29.9 0.4 collective-permute-done.8
  30.3 0.6 collective-permute-start.13
  30.9 1.6 %collective-permute-start.12 = (bf16[4,16,768]{2,1,0:T(8,128)(2,1)S(1)}, bf16[4,16,768]{2,1,0:T(8,128)(2,1)S(1)}, u32[]{:S(2)}, u32[]{:S(2)}) collective-permute-start(bf16[4,16,768]{2,1,0:T(8,128)(2,1)S(1)} %pad_maximum_fusion.1), channel_id=1, source_target_pairs={{0,128},{1,33},{2,130},{3,35},{4,132},{5,37},{6,134},{7,39},{8,136... | collective-permute-start | bytes 294920 | tf_op jit(solution)/shard_map/ppermute | solution.py:275
  32.5 0.8 %collective-permute-start.11 = (bf16[4,16,768]{2,1,0:T(8,128)(2,1)S(1)}, bf16[4,16,768]{2,1,0:T(8,128)(2,1)S(1)}, u32[]{:S(2)}, u32[]{:S(2)}) collective-permute-start(bf16[4,16,768]{2,1,0:T(8,128)(2,1)S(1)} %pad_maximum_fusion.1), channel_id=1, source_target_pairs={{0,64},{1,17},{2,66},{3,19},{4,68},{5,21},{6,70},{7,23},{8,72},{9,... | collective-permute-start | bytes 294920 | tf_op jit(solution)/shard_map/ppermute | solution.py:275
  33.3 0.8 %collective-permute-done.7.refs_3_ = bf16[18,16,128]{2,1,0:T(8,128)(2,1)S(1)} collective-permute-done((bf16[18,16,128]{2,1,0:T(8,128)(2,1)S(1)}, bf16[18,16,128]{2,1,0:T(8,128)(2,1)S(1)}, u32[]{:S(2)}, u32[]{:S(2)}) %collective-permute-start.7) | collective-permute-done | bytes 73760 | tf_op jit(solution)/shard_map/ppermute | solution.py:280
  34.0 0.7 route_kernel.1
  34.7 7.4 %all-to-all-start = ((bf16[8,3,16,128]{3,2,1,0:T(8,128)(2,1)}), bf16[8,3,16,128]{3,2,1,0:T(8,128)(2,1)S(1)}, u32[]{:S(2)}, u32[]{:S(2)}) async-start(bf16[8,3,16,128]{3,2,1,0:T(8,128)(2,1)} %route_kernel.1), calls=%async_computation | async-start | bytes 196608 | tf_op jit(solution)/shard_map/all_to_all | solution.py:306
  42.2 0.1 pad_maximum_fusion.known_ref
  42.3 3.0 %collective-permute-start.14 = (bf16[4,4,16,768]{3,2,1,0:T(8,128)(2,1)S(1)}, bf16[4,4,16,768]{3,2,1,0:T(8,128)(2,1)S(1)}, u32[]{:S(2)}, u32[]{:S(2)}) collective-permute-start(bf16[4,4,16,768]{3,2,1,0:T(8,128)(2,1)S(1)} %pad_maximum_fusion.known_ref), channel_id=1, source_target_pairs={{0,1},{1,0},{2,3},{3,2},{4,5},{5,4},{6,7},{7,6},{8,9},{9,8},{10,11... | collective-permute-start | bytes 1179656 | tf_op jit(solution)/shard_map/ppermute | solution.py:305
  45.3 4.6 %all-to-all-done = bf16[8,3,16,128]{3,2,1,0:T(8,128)(2,1)S(1)} async-done(((bf16[8,3,16,128]{3,2,1,0:T(8,128)(2,1)}), bf16[8,3,16,128]{3,2,1,0:T(8,128)(2,1)S(1)}, u32[]{:S(2)}, u32[]{:S(2)}) %all-to-all-start) | async-done | bytes 98336 | tf_op jit(solution)/shard_map/all_to_all | solution.py:306
  49.9 0.1 fusion.1
  50.0 0.8 %broadcast_in_dim.2 = bf16[32,16,384]{2,1,0:T(8,128)(2,1)} broadcast(bf16[16,384]{1,0:T(8,128)(2,1)S(1)} %pad_maximum_fusion.3), dimensions={1,2} | broadcast | bytes 405504 | tf_op jit(solution)/shard_map/broadcast_in_dim | solution.py:314
  50.8 9.5 %all-to-all-start.1 = ((bf16[32,16,384]{2,1,0:T(8,128)(2,1)}), bf16[32,16,384]{2,1,0:T(8,128)(2,1)S(1)}, u32[]{:S(2)}, u32[]{:S(2)}) async-start(bf16[32,16,384]{2,1,0:T(8,128)(2,1)} %broadcast_in_dim.2), calls=%async_computation.1 | async-start | bytes 786432 | tf_op jit(solution)/shard_map/all_to_all | solution.py:313
  60.3 0.1 pad_add_fusion.place_ref
  60.4 10.1 %all-to-all-done.1.window_ref = bf16[32,16,384]{2,1,0:T(8,128)(2,1)S(1)} async-done(((bf16[32,16,384]{2,1,0:T(8,128)(2,1)}), bf16[32,16,384]{2,1,0:T(8,128)(2,1)S(1)}, u32[]{:S(2)}, u32[]{:S(2)}) %all-to-all-start.1) | async-done | bytes 393248 | tf_op jit(solution)/shard_map/all_to_all | solution.py:313
  70.4 3.0 %iterate.1 = (bf16[1,16,256]{2,1,0:T(8,128)(2,1)}, f32[1,2,256]{2,1,0:T(2,128)}) custom-call(s32[3]{0:T(128)S(1)} %pad_add_fusion.place_ref, bf16[32,16,384]{2,1,0:T(8,128)(2,1)S(1)} %all-to-all-done.1.window_ref, bf16[4,4,16,768]{3,2,1,0:T(8,128)(2,1)S(1)} %pad_maximum_fusion.known_ref, bf16[4,4,16,768]{3,2,1,0:T(8,128)(2,1)S(1)} %collective-permute-done.14.known_other_ref, ...), custom_call_target="tpu_custom_call" | custom-call | tf_op jit(solution)/shard_map/iterate/pallas_call | solution.py:231
  (33 shorter events, 0.1 us)
Async XLA Ops:
  0.6 10.2 %copy-start.1 = (f32[8,128]{1,0:T(8,128)S(1)}, f32[8,128]{1,0:T(8,128)}, u32[]{:S(2)}) copy-start(f32[8,128]{1,0:T(8,128)} %eigen_ref.1) | copy-start | bytes 12292
  0.6 12.5 %copy-start.2 = (s32[8,1]{0,1:T(1,128)S(1)}, s32[8,1]{0,1:T(1,128)}, u32[]{:S(2)}) copy-start(s32[8,1]{0,1:T(1,128)} %param.11) | copy-start | bytes 100
  0.7 12.5 %copy-start.3 = (s32[8]{0:T(128)S(1)}, s32[8]{0:T(128)}, u32[]{:S(2)}) copy-start(s32[8]{0:T(128)} %offset_ref.1) | copy-start | bytes 100
  0.7 17.9 %copy-start.5 = (bf16[1,16,256]{2,1,0:T(8,128)(2,1)S(1)}, bf16[1,16,256]{2,1,0:T(8,128)(2,1)}, u32[]{:S(2)}) copy-start(bf16[1,16,256]{2,1,0:T(8,128)(2,1)} %param.14) | copy-start | bytes 24580
  0.7 17.9 %copy-start.4 = (bf16[1,512,16]{1,2,0:T(8,128)(2,1)S(1)}, bf16[1,512,16]{1,2,0:T(8,128)(2,1)}, u32[]{:S(2)}) copy-start(bf16[1,512,16]{1,2,0:T(8,128)(2,1)} %param.13) | copy-start | bytes 49156
  7.5 62.9 %copy-start = (bf16[1,2,256,256]{3,2,1,0:T(8,128)(2,1)S(1)}, bf16[1,2,256,256]{3,2,1,0:T(8,128)(2,1)}, u32[]{:S(2)}) copy-start(bf16[1,2,256,256]{3,2,1,0:T(8,128)(2,1)} %param.15) | copy-start | bytes 786436
  7.5 5.6 %collective-permute-start = (bf16[8,256,256]{2,1,0:T(8,128)(2,1)S(1)}, bf16[8,256,256]{2,1,0:T(8,128)(2,1)S(1)}, u32[]{:S(2)}, u32[]{:S(2)}) collective-permute-start(bf16[8,256,256]{2,1,0:T(8,128)(2,1)S(1)} %project.1.own_ref), channel_id=1, source_target_pairs={{0,1},{1,0},{2,3},{3,2},{4,5},{5,4},{6,7},{7,6},{8,9},{9,8},{10,11... | collective-permute-start | bytes 3145736 | tf_op jit(solution)/shard_map/ppermute | solution.py:293
  10.8 2.3 %collective-permute-start.1 = (f32[8,128]{1,0:T(8,128)S(1)}, f32[8,128]{1,0:T(8,128)S(1)}, u32[]{:S(2)}, u32[]{:S(2)}) collective-permute-start(f32[8,128]{1,0:T(8,128)S(1)} %copy-done.1), channel_id=1, source_target_pairs={{0,1},{1,0},{2,3},{3,2},{4,5},{5,4},{6,7},{7,6},{8,9},{9,8},{10,11... | collective-permute-start | bytes 12296 | tf_op jit(solution)/shard_map/ppermute | solution.py:291
  15.8 10.6 %collective-permute-start.2 = (bf16[4,18,16,128]{3,2,1,0:T(8,128)(2,1)S(1)}, bf16[4,18,16,128]{3,2,1,0:T(8,128)(2,1)S(1)}, u32[]{:S(2)}, u32[]{:S(2)}) collective-permute-start(bf16[4,18,16,128]{3,2,1,0:T(8,128)(2,1)S(1)} %get-tuple-element.14), channel_id=1, source_target_pairs={{0,16},{1,65},{2,18},{3,67},{4,20},{5,69},{6,22},{7,71},{8,24},{9,... | collective-permute-start | bytes 884744 | tf_op jit(solution)/shard_map/ppermute | solution.py:280
  15.9 10.5 %collective-permute-start.3 = (bf16[4,18,16,128]{3,2,1,0:T(8,128)(2,1)S(1)}, bf16[4,18,16,128]{3,2,1,0:T(8,128)(2,1)S(1)}, u32[]{:S(2)}, u32[]{:S(2)}) collective-permute-start(bf16[4,18,16,128]{3,2,1,0:T(8,128)(2,1)S(1)} %get-tuple-element.15), channel_id=1, source_target_pairs={{0,48},{1,193},{2,50},{3,195},{4,52},{5,197},{6,54},{7,199},{8,56}... | collective-permute-start | bytes 884744 | tf_op jit(solution)/shard_map/ppermute | solution.py:280
  18.6 7.8 %collective-permute-start.4 = (bf16[4,18,16,128]{3,2,1,0:T(8,128)(2,1)S(1)}, bf16[4,18,16,128]{3,2,1,0:T(8,128)(2,1)S(1)}, u32[]{:S(2)}, u32[]{:S(2)}) collective-permute-start(bf16[4,18,16,128]{3,2,1,0:T(8,128)(2,1)S(1)} %get-tuple-element.16), channel_id=1, source_target_pairs={{0,32},{1,129},{2,34},{3,131},{4,36},{5,133},{6,38},{7,135},{8,40}... | collective-permute-start | bytes 884744 | tf_op jit(solution)/shard_map/ppermute | solution.py:280
  18.6 10.7 %collective-permute-start.10 = (bf16[16,768]{1,0:T(8,128)(2,1)S(1)}, bf16[16,768]{1,0:T(8,128)(2,1)S(1)}, u32[]{:S(2)}, u32[]{:S(2)}) collective-permute-start(bf16[16,768]{1,0:T(8,128)(2,1)S(1)} %pad_maximum_fusion.2), channel_id=1, source_target_pairs={{0,48},{1,193},{2,50},{3,195},{4,52},{5,197},{6,54},{7,199},{8,56}... | collective-permute-start | bytes 73736 | tf_op jit(solution)/shard_map/ppermute | solution.py:275
  19.9 10.0 %collective-permute-start.9 = (bf16[16,768]{1,0:T(8,128)(2,1)S(1)}, bf16[16,768]{1,0:T(8,128)(2,1)S(1)}, u32[]{:S(2)}, u32[]{:S(2)}) collective-permute-start(bf16[16,768]{1,0:T(8,128)(2,1)S(1)} %pad_maximum_fusion.2), channel_id=1, source_target_pairs={{0,32},{1,129},{2,34},{3,131},{4,36},{5,133},{6,38},{7,135},{8,40}... | collective-permute-start | bytes 73736 | tf_op jit(solution)/shard_map/ppermute | solution.py:275
  26.4 3.9 %collective-permute-start.8 = (bf16[16,768]{1,0:T(8,128)(2,1)S(1)}, bf16[16,768]{1,0:T(8,128)(2,1)S(1)}, u32[]{:S(2)}, u32[]{:S(2)}) collective-permute-start(bf16[16,768]{1,0:T(8,128)(2,1)S(1)} %pad_maximum_fusion.2), channel_id=1, source_target_pairs={{0,16},{1,65},{2,18},{3,67},{4,20},{5,69},{6,22},{7,71},{8,24},{9,... | collective-permute-start | bytes 73736 | tf_op jit(solution)/shard_map/ppermute | solution.py:275
  26.6 5.9 %collective-permute-start.5 = (bf16[18,16,128]{2,1,0:T(8,128)(2,1)S(1)}, bf16[18,16,128]{2,1,0:T(8,128)(2,1)S(1)}, u32[]{:S(2)}, u32[]{:S(2)}) collective-permute-start(bf16[18,16,128]{2,1,0:T(8,128)(2,1)S(1)} %get-tuple-element.18), channel_id=1, source_target_pairs={{0,64},{1,17},{2,66},{3,19},{4,68},{5,21},{6,70},{7,23},{8,72},{9,... | collective-permute-start | bytes 221192 | tf_op jit(solution)/shard_map/ppermute | solution.py:280
  26.9 6.4 %collective-permute-start.6 = (bf16[18,16,128]{2,1,0:T(8,128)(2,1)S(1)}, bf16[18,16,128]{2,1,0:T(8,128)(2,1)S(1)}, u32[]{:S(2)}, u32[]{:S(2)}) collective-permute-start(bf16[18,16,128]{2,1,0:T(8,128)(2,1)S(1)} %get-tuple-element.19), channel_id=1, source_target_pairs={{0,192},{1,49},{2,194},{3,51},{4,196},{5,53},{6,198},{7,55},{8,200... | collective-permute-start | bytes 221192 | tf_op jit(solution)/shard_map/ppermute | solution.py:280
  29.3 4.7 %collective-permute-start.7 = (bf16[18,16,128]{2,1,0:T(8,128)(2,1)S(1)}, bf16[18,16,128]{2,1,0:T(8,128)(2,1)S(1)}, u32[]{:S(2)}, u32[]{:S(2)}) collective-permute-start(bf16[18,16,128]{2,1,0:T(8,128)(2,1)S(1)} %get-tuple-element.20), channel_id=1, source_target_pairs={{0,128},{1,33},{2,130},{3,35},{4,132},{5,37},{6,134},{7,39},{8,136... | collective-permute-start | bytes 221192 | tf_op jit(solution)/shard_map/ppermute | solution.py:280
  30.3 11.9 %collective-permute-start.13 = (bf16[4,16,768]{2,1,0:T(8,128)(2,1)S(1)}, bf16[4,16,768]{2,1,0:T(8,128)(2,1)S(1)}, u32[]{:S(2)}, u32[]{:S(2)}) collective-permute-start(bf16[4,16,768]{2,1,0:T(8,128)(2,1)S(1)} %pad_maximum_fusion.1), channel_id=1, source_target_pairs={{0,192},{1,49},{2,194},{3,51},{4,196},{5,53},{6,198},{7,55},{8,200... | collective-permute-start | bytes 294920 | tf_op jit(solution)/shard_map/ppermute | solution.py:275
  30.9 11.3 %collective-permute-start.12 = (bf16[4,16,768]{2,1,0:T(8,128)(2,1)S(1)}, bf16[4,16,768]{2,1,0:T(8,128)(2,1)S(1)}, u32[]{:S(2)}, u32[]{:S(2)}) collective-permute-start(bf16[4,16,768]{2,1,0:T(8,128)(2,1)S(1)} %pad_maximum_fusion.1), channel_id=1, source_target_pairs={{0,128},{1,33},{2,130},{3,35},{4,132},{5,37},{6,134},{7,39},{8,136... | collective-permute-start | bytes 294920 | tf_op jit(solution)/shard_map/ppermute | solution.py:275
  32.5 9.7 %collective-permute-start.11 = (bf16[4,16,768]{2,1,0:T(8,128)(2,1)S(1)}, bf16[4,16,768]{2,1,0:T(8,128)(2,1)S(1)}, u32[]{:S(2)}, u32[]{:S(2)}) collective-permute-start(bf16[4,16,768]{2,1,0:T(8,128)(2,1)S(1)} %pad_maximum_fusion.1), channel_id=1, source_target_pairs={{0,64},{1,17},{2,66},{3,19},{4,68},{5,21},{6,70},{7,23},{8,72},{9,... | collective-permute-start | bytes 294920 | tf_op jit(solution)/shard_map/ppermute | solution.py:275
  34.7 15.1 %all-to-all-start = ((bf16[8,3,16,128]{3,2,1,0:T(8,128)(2,1)}), bf16[8,3,16,128]{3,2,1,0:T(8,128)(2,1)S(1)}, u32[]{:S(2)}, u32[]{:S(2)}) async-start(bf16[8,3,16,128]{3,2,1,0:T(8,128)(2,1)} %route_kernel.1), calls=%async_computation | async-start | bytes 196608 | tf_op jit(solution)/shard_map/all_to_all | solution.py:306
  42.3 18.1 %collective-permute-start.14 = (bf16[4,4,16,768]{3,2,1,0:T(8,128)(2,1)S(1)}, bf16[4,4,16,768]{3,2,1,0:T(8,128)(2,1)S(1)}, u32[]{:S(2)}, u32[]{:S(2)}) collective-permute-start(bf16[4,4,16,768]{3,2,1,0:T(8,128)(2,1)S(1)} %pad_maximum_fusion.known_ref), channel_id=1, source_target_pairs={{0,1},{1,0},{2,3},{3,2},{4,5},{5,4},{6,7},{7,6},{8,9},{9,8},{10,11... | collective-permute-start | bytes 1179656 | tf_op jit(solution)/shard_map/ppermute | solution.py:305
  50.8 19.7 %all-to-all-start.1 = ((bf16[32,16,384]{2,1,0:T(8,128)(2,1)}), bf16[32,16,384]{2,1,0:T(8,128)(2,1)S(1)}, u32[]{:S(2)}, u32[]{:S(2)}) async-start(bf16[32,16,384]{2,1,0:T(8,128)(2,1)} %broadcast_in_dim.2), calls=%async_computation.1 | async-start | bytes 786432 | tf_op jit(solution)/shard_map/all_to_all | solution.py:313

commit v10 on v8

--- a/solution.py
+++ b/solution.py
@@ -20,6 +20,11 @@
 STRIP = 16
 ITERS = 2
 epsilon = 1e-06
+
+
+def position():
+    leaf = lax.axis_index("leaf").astype(jnp.int32)
+    return leaf >> 2, leaf & (SIDE - 1), lax.axis_index("mode").astype(jnp.int32)
 
 
 def place_of(d, e, place_ref):
@@ -146,11 +151,11 @@
 
 
 def iterate_kernel(
-    place_ref, own_ref, other_ref, known_ref, known_other_ref, turns_ref, out_ref, norms_ref, kt_ref, m_ref, high_ref, x_ref
+    own_ref, other_ref, known_ref, known_other_ref, turns_ref, out_hbm, norms_hbm, kt_ref, m_ref, high_ref, x_ref, out_ref, norms_ref, sems
 ):
-    core, device, sep = place_ref[0], place_ref[1], place_ref[2]
-    leaf = device >> 1
-    y, x = leaf >> 2, leaf & 3
+    y, x, core = position()
+    device = 2 * (y * SIDE + x) + core
+    sep = lax.axis_index("sep").astype(jnp.int32)
     lane = lax.broadcasted_iota(jnp.int32, (STRIP, 128), 1)
     halved = jnp.where(lane < 32, 0.5, 1.0)
     rest_weight = jnp.where(lane < 32, 0.5, 0.0)
@@ -194,24 +199,30 @@
         summed = summed + low * block.astype(jnp.float32)
         scale = jnp.sqrt(jnp.sum(summed * summed, 0, keepdims=True) / SEP_ROWS + epsilon)
         norms_ref[0, pl.ds(step, 1), :] = scale
-        normed = (summed / scale).astype(jnp.bfloat16)
+        normed = (summed * (1.0 / scale)).astype(jnp.bfloat16)
         if step < ITERS - 1:
             x_ref[...] = jnp.dot(
                 normed, turns_ref[step], preferred_element_type=jnp.float32
             ).astype(jnp.bfloat16)
         else:
+            norms_copy = pltpu.make_async_copy(norms_ref, norms_hbm, sems.at[0])
+            norms_copy.start()
             x_ref[...] = normed
             rows = x_ref[pl.ds(pl.multiple_of(16 * device, STRIP), STRIP), :]
             out_ref[0] = jnp.dot(
                 rows, turns_ref[step], preferred_element_type=jnp.float32
             ).astype(jnp.bfloat16)
-
-
-def iterate(place, *arrays):
+            out_copy = pltpu.make_async_copy(out_ref, out_hbm, sems.at[1])
+            out_copy.start()
+            norms_copy.wait()
+            out_copy.wait()
+
+
+def iterate(*arrays):
     return pl.pallas_call(
         iterate_kernel,
-        in_specs=[SMEM] + [VMEM] * len(arrays),
-        out_specs=[VMEM, VMEM],
+        in_specs=[VMEM] * len(arrays),
+        out_specs=[pl.BlockSpec(memory_space=pltpu.HBM)] * 2,
         out_shape=[
             jax.ShapeDtypeStruct((1, STRIP, COLS), jnp.bfloat16),
             jax.ShapeDtypeStruct((1, ITERS, COLS), jnp.float32),
@@ -221,10 +232,13 @@
             pltpu.VMEM((SEP_ROWS, SEP_ROWS), jnp.float32),
             pltpu.VMEM((SEP_ROWS, SEP_ROWS), jnp.bfloat16),
             pltpu.VMEM((SEP_ROWS, COLS), jnp.bfloat16),
+            pltpu.VMEM((1, STRIP, COLS), jnp.bfloat16),
+            pltpu.VMEM((1, ITERS, COLS), jnp.float32),
+            pltpu.SemaphoreType.DMA((2,)),
         ],
         compiler_params=pltpu.CompilerParams(vmem_limit_bytes=16 << 20),
         name="iterate",
-    )(place, *[in_vmem(array) for array in arrays])
+    )(*[in_vmem(array) for array in arrays])
 
 
 SWAP = [(0, 1), (1, 0)]
@@ -266,16 +280,13 @@
 def per_device(
     modes, coupling, eigenvalues, separator_of, row_offset, stiffness, start_block, rotations
 ):
-    core = lax.axis_index("mode").astype(jnp.int32)
-    device = lax.axis_index(("leaf", "mode")).astype(jnp.int32)
     other_eigen = lax.ppermute(eigenvalues, "mode", SWAP)
     own = jnp.einsum("ldw,ldm->lwm", coupling, modes, preferred_element_type=jnp.float32).astype(
         jnp.bfloat16
     )
     other = lax.ppermute(own, "mode", SWAP)
     sep = lax.axis_index("sep").astype(jnp.int32)
-    leaf = lax.axis_index("leaf").astype(jnp.int32)
-    y, x = leaf >> 2, leaf & 3
+    y, x, core = position()
     place = jnp.stack([core, jnp.where(core == 0, x, y), jnp.where(core == 0, y, x)])
     pieces = gram(separator_of[:, 0], row_offset, place, own, other, eigenvalues, other_eigen)
     piece = (TILES, STRIP, 128)
@@ -300,8 +311,7 @@
         tiled=True,
     )
     theirs = lax.ppermute(mine, "mode", SWAP)
-    place = jnp.stack([core, device, sep])
-    return tuple(iterate(place, mine, theirs, known, known_other, rotations[0]))
+    return tuple(iterate(mine, theirs, known, known_other, rotations[0]))
 
 
 def solution(mesh):

time: 69.9 us -> 69.8 us (level)
  starting transfers between devices: 31.8 us -> 34.2 us
  waiting for transfers between devices: 13.5 us -> 12.1 us
  blocking collectives: 11.8 us -> 11.1 us
    ppermute x6, starting transfers between devices: 6.09 us -> 7.41 us  [gather_stage(): got = [lax.ppermute(value, AXES, plane_steps(d, stage)) for d in ORDER]]
    ppermute x6, waiting for transfers between devices: 5.44 us -> 4.41 us  [scatter_stage(): got = [lax.ppermute(pieces[d], AXES, plane_steps(d, stage)) for d in ORDER]]
  transfers between devices with their start and end apart: 17 -> 17, of which waited for: 6 -> 4; matrix products, arithmetic and copies ran while one was open for 1% -> 0% of each run, Pallas kernels for 1% -> 1%
where the time goes in v10:
time: 69.8 us; the launch traced here: 69.6 us
  starting transfers between devices  34.2 us (49%)
  waiting for transfers between devices  12.1 us (17%)
  blocking collectives  11.1 us (16%)
  Pallas kernels  5.96 us (9%)
  matrix products  4.89 us (7%)
  between operations  0.97 us (1%)
    all_to_all x1, blocking collectives, per_device(): lax.all_to_all(jnp.broadcast_to(packed[None], (PLANE, *packed.shape)), 'l...  11.1 us
    all_to_all x1, starting transfers between devices, per_device(): got = lax.all_to_all(routed, 'sep', split_axis=0, concat_axis=0, tiled=True)  7.75 us
    ppermute x6, starting transfers between devices, gather_stage(): got = [lax.ppermute(value, AXES, plane_steps(d, stage)) for d in ORDER]  7.41 us
    ppermute x6, starting transfers between devices, scatter_stage(): got = [lax.ppermute(pieces[d], AXES, plane_steps(d, stage)) for d in ORDER]  6.35 us
    ppermute x1, starting transfers between devices, per_device(): theirs = lax.ppermute(mine, 'mode', SWAP)  6.23 us
    dot_general x1, matrix products, per_device(): jnp.einsum('ldw,ldm->lwm', coupling, modes, preferred_element_type=jnp.fl...  4.89 us
    all_to_all x1, waiting for transfers between devices, per_device(): got = lax.all_to_all(routed, 'sep', split_axis=0, concat_axis=0, tiled=True)  4.53 us
    ppermute x6, waiting for transfers between devices, scatter_stage(): got = [lax.ppermute(pieces[d], AXES, plane_steps(d, stage)) for d in ORDER]  4.41 us
  transfers between devices with their start and end apart: 17, of which 4 were waited for; matrix products, arithmetic and copies ran while one was open for 0% of the time, Pallas kernels for 1%

profile of v10, /device:TPU:1, one launch (start us, length us, event | category | flops | bytes accessed | tf_op | source)
XLA Modules:
  0.0 69.6 jit_solution(6320348309412256222)
XLA Ops:
  0.7 4.9 %convolution_convert_fusion.own_ref = bf16[8,256,256]{2,1,0:T(8,128)(2,1)S(1)} fusion(bf16[8,1024,256]{2,1,0:T(8,128)(2,1)} %param.9, bf16[8,1024,256]{2,1,0:T(8,128)(2,1)} %param.8), kind=kOutput, calls=%fused_computation | convolution fusion | flops 1074266112 | bytes 9437184 | tf_op jit(solution)/shard_map/ldw,ldm->lwm/dot_general | solution.py:284
  5.6 0.0 copy-start
  5.6 3.3 %collective-permute-start = (bf16[8,256,256]{2,1,0:T(8,128)(2,1)S(1)}, bf16[8,256,256]{2,1,0:T(8,128)(2,1)S(1)}, u32[]{:S(2)}, u32[]{:S(2)}) collective-permute-start(bf16[8,256,256]{2,1,0:T(8,128)(2,1)S(1)} %convolution_convert_fusion.own_ref), channel_id=1, source_target_pairs={{0,1},{1,0},{2,3},{3,2},{4,5},{5,4},{6,7},{7,6},{8,9},{9,8},{10,11... | collective-permute-start | bytes 3145736 | tf_op jit(solution)/shard_map/ppermute | solution.py:287
  8.9 0.1 collective-permute-start.1
  9.0 0.1 pad_add_fusion.place_ref
  9.1 2.1 %collective-permute-done.1.other_eigen_ref = f32[8,128]{1,0:T(8,128)S(1)} collective-permute-done((f32[8,128]{1,0:T(8,128)S(1)}, f32[8,128]{1,0:T(8,128)S(1)}, u32[]{:S(2)}, u32[]{:S(2)}) %collective-permute-start.1) | collective-permute-done | bytes 4128 | tf_op jit(solution)/shard_map/ppermute | solution.py:283
  11.2 2.7 %gram.1 = (bf16[4,18,16,128]{3,2,1,0:T(8,128)(2,1)S(1)}, bf16[4,18,16,128]{3,2,1,0:T(8,128)(2,1)S(1)}, bf16[4,18,16,128]{3,2,1,0:T(8,128)(2,1)S(1)}, bf16[4,18,16,128]{3,2,1,0:T(8,128)(2,1)S(1)}) custom-call(s32[8]{0:T(128)S(1)} %bitcast.30, s32[8]{0:T(128)S(1)} %copy-done.3, s32[3]{0:T(128)S(1)} %pad_add_fusion.place_ref, ...), custom_call_target="tpu_custom_call" | custom-call | tf_op jit(solution)/shard_map/gram/pallas_call | solution.py:106
  13.9 0.1 collective-permute-start.2
  14.0 2.7 %collective-permute-start.3 = (bf16[4,18,16,128]{3,2,1,0:T(8,128)(2,1)S(1)}, bf16[4,18,16,128]{3,2,1,0:T(8,128)(2,1)S(1)}, u32[]{:S(2)}, u32[]{:S(2)}) collective-permute-start(bf16[4,18,16,128]{3,2,1,0:T(8,128)(2,1)S(1)} %get-tuple-element.15), channel_id=1, source_target_pairs={{0,48},{1,193},{2,50},{3,195},{4,52},{5,197},{6,54},{7,199},{8,56}... | collective-permute-start | bytes 884744 | tf_op jit(solution)/shard_map/ppermute | solution.py:274
  16.6 0.0 collective-permute-start.4
  16.6 0.6 collective-permute-start.9
  17.3 2.5 %collective-permute-start.10 = (bf16[16,768]{1,0:T(8,128)(2,1)S(1)}, bf16[16,768]{1,0:T(8,128)(2,1)S(1)}, u32[]{:S(2)}, u32[]{:S(2)}) collective-permute-start(bf16[16,768]{1,0:T(8,128)(2,1)S(1)} %pad_maximum_fusion.2), channel_id=1, source_target_pairs={{0,32},{1,129},{2,34},{3,131},{4,36},{5,133},{6,38},{7,135},{8,40}... | collective-permute-start | bytes 73736 | tf_op jit(solution)/shard_map/ppermute | solution.py:269
  19.8 4.4 %collective-permute-done.2.refs_1_ = bf16[4,18,16,128]{3,2,1,0:T(8,128)(2,1)S(1)} collective-permute-done((bf16[4,18,16,128]{3,2,1,0:T(8,128)(2,1)S(1)}, bf16[4,18,16,128]{3,2,1,0:T(8,128)(2,1)S(1)}, u32[]{:S(2)}, u32[]{:S(2)}) %collective-permute-start.2) | collective-permute-done | bytes 294944 | tf_op jit(solution)/shard_map/ppermute | solution.py:274
  24.2 0.0 collective-permute-start.11
  24.2 0.0 collective-permute-done.3.refs_2_
  24.2 0.1 split_kernel.1
  24.3 0.6 collective-permute-start.5
  25.0 2.1 %collective-permute-start.6 = (bf16[18,16,128]{2,1,0:T(8,128)(2,1)S(1)}, bf16[18,16,128]{2,1,0:T(8,128)(2,1)S(1)}, u32[]{:S(2)}, u32[]{:S(2)}) collective-permute-start(bf16[18,16,128]{2,1,0:T(8,128)(2,1)S(1)} %get-tuple-element.19), channel_id=1, source_target_pairs={{0,192},{1,49},{2,194},{3,51},{4,196},{5,53},{6,198},{7,55},{8,200... | collective-permute-start | bytes 221192 | tf_op jit(solution)/shard_map/ppermute | solution.py:274
  27.1 0.9 %collective-permute-start.7 = (bf16[18,16,128]{2,1,0:T(8,128)(2,1)S(1)}, bf16[18,16,128]{2,1,0:T(8,128)(2,1)S(1)}, u32[]{:S(2)}, u32[]{:S(2)}) collective-permute-start(bf16[18,16,128]{2,1,0:T(8,128)(2,1)S(1)} %get-tuple-element.20), channel_id=1, source_target_pairs={{0,128},{1,33},{2,130},{3,35},{4,132},{5,37},{6,134},{7,39},{8,136... | collective-permute-start | bytes 221192 | tf_op jit(solution)/shard_map/ppermute | solution.py:274
  28.0 0.6 collective-permute-start.12
  28.6 1.8 %collective-permute-start.13 = (bf16[4,16,768]{2,1,0:T(8,128)(2,1)S(1)}, bf16[4,16,768]{2,1,0:T(8,128)(2,1)S(1)}, u32[]{:S(2)}, u32[]{:S(2)}) collective-permute-start(bf16[4,16,768]{2,1,0:T(8,128)(2,1)S(1)} %pad_maximum_fusion.1), channel_id=1, source_target_pairs={{0,128},{1,33},{2,130},{3,35},{4,132},{5,37},{6,134},{7,39},{8,136... | collective-permute-start | bytes 294920 | tf_op jit(solution)/shard_map/ppermute | solution.py:269
  30.5 1.8 %collective-permute-start.14 = (bf16[4,16,768]{2,1,0:T(8,128)(2,1)S(1)}, bf16[4,16,768]{2,1,0:T(8,128)(2,1)S(1)}, u32[]{:S(2)}, u32[]{:S(2)}) collective-permute-start(bf16[4,16,768]{2,1,0:T(8,128)(2,1)S(1)} %pad_maximum_fusion.1), channel_id=1, source_target_pairs={{0,192},{1,49},{2,194},{3,51},{4,196},{5,53},{6,198},{7,55},{8,200... | collective-permute-start | bytes 294920 | tf_op jit(solution)/shard_map/ppermute | solution.py:269
  32.3 0.7 route_kernel.1
  32.9 7.7 %all-to-all-start = ((bf16[8,3,16,128]{3,2,1,0:T(8,128)(2,1)}), bf16[8,3,16,128]{3,2,1,0:T(8,128)(2,1)S(1)}, u32[]{:S(2)}, u32[]{:S(2)}) async-start(bf16[8,3,16,128]{3,2,1,0:T(8,128)(2,1)} %route_kernel.1), calls=%async_computation | async-start | bytes 196608 | tf_op jit(solution)/shard_map/all_to_all | solution.py:299
  40.7 0.1 pad_maximum_fusion.known_ref
  40.8 3.0 %collective-permute-start.15 = (bf16[4,4,16,768]{3,2,1,0:T(8,128)(2,1)S(1)}, bf16[4,4,16,768]{3,2,1,0:T(8,128)(2,1)S(1)}, u32[]{:S(2)}, u32[]{:S(2)}) collective-permute-start(bf16[4,4,16,768]{3,2,1,0:T(8,128)(2,1)S(1)} %pad_maximum_fusion.known_ref), channel_id=1, source_target_pairs={{0,1},{1,0},{2,3},{3,2},{4,5},{5,4},{6,7},{7,6},{8,9},{9,8},{10,11... | collective-permute-start | bytes 1179656 | tf_op jit(solution)/shard_map/ppermute | solution.py:298
  43.8 4.5 %all-to-all-done = bf16[8,3,16,128]{3,2,1,0:T(8,128)(2,1)S(1)} async-done(((bf16[8,3,16,128]{3,2,1,0:T(8,128)(2,1)}), bf16[8,3,16,128]{3,2,1,0:T(8,128)(2,1)S(1)}, u32[]{:S(2)}, u32[]{:S(2)}) %all-to-all-start) | async-done | bytes 98336 | tf_op jit(solution)/shard_map/all_to_all | solution.py:299
  48.4 0.1 fusion.1
  48.6 11.1 %all_to_all.10.own_ref = bf16[16,16,384]{2,1,0:T(8,128)(2,1)S(1)} all-to-all(bf16[16,16,384]{2,1,0:T(8,128)(2,1)S(1)} %broadcast_in_dim.2), channel_id=1, replica_groups=mesh['leaf'=16,'sep'=8,'mode'=2] {'leaf'}, dimensions={0} | all-to-all | bytes 393216 | tf_op jit(solution)/shard_map/all_to_all | solution.py:306
  59.7 6.2 %collective-permute-start.8 = (bf16[16,16,384]{2,1,0:T(8,128)(2,1)S(1)}, bf16[16,16,384]{2,1,0:T(8,128)(2,1)S(1)}, u32[]{:S(2)}, u32[]{:S(2)}) collective-permute-start(bf16[16,16,384]{2,1,0:T(8,128)(2,1)S(1)} %all_to_all.10.own_ref), channel_id=1, source_target_pairs={{0,1},{1,0},{2,3},{3,2},{4,5},{5,4},{6,7},{7,6},{8,9},{9,8},{10,11... | collective-permute-start | bytes 589832 | tf_op jit(solution)/shard_map/ppermute | solution.py:313
  65.9 1.1 %collective-permute-done.8.other_ref = bf16[16,16,384]{2,1,0:T(8,128)(2,1)S(1)} collective-permute-done((bf16[16,16,384]{2,1,0:T(8,128)(2,1)S(1)}, bf16[16,16,384]{2,1,0:T(8,128)(2,1)S(1)}, u32[]{:S(2)}, u32[]{:S(2)}) %collective-permute-start.8) | collective-permute-done | bytes 196640 | tf_op jit(solution)/shard_map/ppermute | solution.py:313
  67.0 2.4 %iterate.1 = (bf16[1,16,256]{2,1,0:T(8,128)(2,1)}, f32[1,2,256]{2,1,0:T(2,128)}) custom-call(bf16[16,16,384]{2,1,0:T(8,128)(2,1)S(1)} %all_to_all.10.own_ref, bf16[16,16,384]{2,1,0:T(8,128)(2,1)S(1)} %collective-permute-done.8.other_ref, bf16[4,4,16,768]{3,2,1,0:T(8,128)(2,1)S(1)} %pad_maximum_fusion.known_ref, ...), custom_call_target="tpu_custom_call" | custom-call | tf_op jit(solution)/shard_map/iterate/pallas_call | solution.py:222
  (33 shorter events, 0.1 us)
Async XLA Ops:
  0.6 8.2 %copy-start.1 = (f32[8,128]{1,0:T(8,128)S(1)}, f32[8,128]{1,0:T(8,128)}, u32[]{:S(2)}) copy-start(f32[8,128]{1,0:T(8,128)} %eigen_ref.1) | copy-start | bytes 12292
  0.6 10.5 %copy-start.2 = (s32[8,1]{0,1:T(1,128)S(1)}, s32[8,1]{0,1:T(1,128)}, u32[]{:S(2)}) copy-start(s32[8,1]{0,1:T(1,128)} %param.11) | copy-start | bytes 100
  0.7 10.5 %copy-start.3 = (s32[8]{0:T(128)S(1)}, s32[8]{0:T(128)}, u32[]{:S(2)}) copy-start(s32[8]{0:T(128)} %offset_ref.1) | copy-start | bytes 100
  0.7 16.0 %copy-start.5 = (bf16[1,16,256]{2,1,0:T(8,128)(2,1)S(1)}, bf16[1,16,256]{2,1,0:T(8,128)(2,1)}, u32[]{:S(2)}) copy-start(bf16[1,16,256]{2,1,0:T(8,128)(2,1)} %param.14) | copy-start | bytes 24580
  0.7 16.0 %copy-start.4 = (bf16[1,512,16]{1,2,0:T(8,128)(2,1)S(1)}, bf16[1,512,16]{1,2,0:T(8,128)(2,1)}, u32[]{:S(2)}) copy-start(bf16[1,512,16]{1,2,0:T(8,128)(2,1)} %param.13) | copy-start | bytes 49156
  5.6 61.4 %copy-start = (bf16[1,2,256,256]{3,2,1,0:T(8,128)(2,1)S(1)}, bf16[1,2,256,256]{3,2,1,0:T(8,128)(2,1)}, u32[]{:S(2)}) copy-start(bf16[1,2,256,256]{3,2,1,0:T(8,128)(2,1)} %param.15) | copy-start | bytes 786436
  5.6 5.6 %collective-permute-start = (bf16[8,256,256]{2,1,0:T(8,128)(2,1)S(1)}, bf16[8,256,256]{2,1,0:T(8,128)(2,1)S(1)}, u32[]{:S(2)}, u32[]{:S(2)}) collective-permute-start(bf16[8,256,256]{2,1,0:T(8,128)(2,1)S(1)} %convolution_convert_fusion.own_ref), channel_id=1, source_target_pairs={{0,1},{1,0},{2,3},{3,2},{4,5},{5,4},{6,7},{7,6},{8,9},{9,8},{10,11... | collective-permute-start | bytes 3145736 | tf_op jit(solution)/shard_map/ppermute | solution.py:287
  8.9 2.3 %collective-permute-start.1 = (f32[8,128]{1,0:T(8,128)S(1)}, f32[8,128]{1,0:T(8,128)S(1)}, u32[]{:S(2)}, u32[]{:S(2)}) collective-permute-start(f32[8,128]{1,0:T(8,128)S(1)} %copy-done.1), channel_id=1, source_target_pairs={{0,1},{1,0},{2,3},{3,2},{4,5},{5,4},{6,7},{7,6},{8,9},{9,8},{10,11... | collective-permute-start | bytes 12296 | tf_op jit(solution)/shard_map/ppermute | solution.py:283
  13.9 10.3 %collective-permute-start.2 = (bf16[4,18,16,128]{3,2,1,0:T(8,128)(2,1)S(1)}, bf16[4,18,16,128]{3,2,1,0:T(8,128)(2,1)S(1)}, u32[]{:S(2)}, u32[]{:S(2)}) collective-permute-start(bf16[4,18,16,128]{3,2,1,0:T(8,128)(2,1)S(1)} %get-tuple-element.14), channel_id=1, source_target_pairs={{0,16},{1,65},{2,18},{3,67},{4,20},{5,69},{6,22},{7,71},{8,24},{9,... | collective-permute-start | bytes 884744 | tf_op jit(solution)/shard_map/ppermute | solution.py:274
  14.0 10.2 %collective-permute-start.3 = (bf16[4,18,16,128]{3,2,1,0:T(8,128)(2,1)S(1)}, bf16[4,18,16,128]{3,2,1,0:T(8,128)(2,1)S(1)}, u32[]{:S(2)}, u32[]{:S(2)}) collective-permute-start(bf16[4,18,16,128]{3,2,1,0:T(8,128)(2,1)S(1)} %get-tuple-element.15), channel_id=1, source_target_pairs={{0,48},{1,193},{2,50},{3,195},{4,52},{5,197},{6,54},{7,199},{8,56}... | collective-permute-start | bytes 884744 | tf_op jit(solution)/shard_map/ppermute | solution.py:274
  16.6 7.6 %collective-permute-start.4 = (bf16[4,18,16,128]{3,2,1,0:T(8,128)(2,1)S(1)}, bf16[4,18,16,128]{3,2,1,0:T(8,128)(2,1)S(1)}, u32[]{:S(2)}, u32[]{:S(2)}) collective-permute-start(bf16[4,18,16,128]{3,2,1,0:T(8,128)(2,1)S(1)} %get-tuple-element.16), channel_id=1, source_target_pairs={{0,32},{1,129},{2,34},{3,131},{4,36},{5,133},{6,38},{7,135},{8,40}... | collective-permute-start | bytes 884744 | tf_op jit(solution)/shard_map/ppermute | solution.py:274
  16.6 10.5 %collective-permute-start.9 = (bf16[16,768]{1,0:T(8,128)(2,1)S(1)}, bf16[16,768]{1,0:T(8,128)(2,1)S(1)}, u32[]{:S(2)}, u32[]{:S(2)}) collective-permute-start(bf16[16,768]{1,0:T(8,128)(2,1)S(1)} %pad_maximum_fusion.2), channel_id=1, source_target_pairs={{0,16},{1,65},{2,18},{3,67},{4,20},{5,69},{6,22},{7,71},{8,24},{9,... | collective-permute-start | bytes 73736 | tf_op jit(solution)/shard_map/ppermute | solution.py:269
  17.3 10.7 %collective-permute-start.10 = (bf16[16,768]{1,0:T(8,128)(2,1)S(1)}, bf16[16,768]{1,0:T(8,128)(2,1)S(1)}, u32[]{:S(2)}, u32[]{:S(2)}) collective-permute-start(bf16[16,768]{1,0:T(8,128)(2,1)S(1)} %pad_maximum_fusion.2), channel_id=1, source_target_pairs={{0,32},{1,129},{2,34},{3,131},{4,36},{5,133},{6,38},{7,135},{8,40}... | collective-permute-start | bytes 73736 | tf_op jit(solution)/shard_map/ppermute | solution.py:269
  24.2 3.8 %collective-permute-start.11 = (bf16[16,768]{1,0:T(8,128)(2,1)S(1)}, bf16[16,768]{1,0:T(8,128)(2,1)S(1)}, u32[]{:S(2)}, u32[]{:S(2)}) collective-permute-start(bf16[16,768]{1,0:T(8,128)(2,1)S(1)} %pad_maximum_fusion.2), channel_id=1, source_target_pairs={{0,48},{1,193},{2,50},{3,195},{4,52},{5,197},{6,54},{7,199},{8,56}... | collective-permute-start | bytes 73736 | tf_op jit(solution)/shard_map/ppermute | solution.py:269
  24.3 6.1 %collective-permute-start.5 = (bf16[18,16,128]{2,1,0:T(8,128)(2,1)S(1)}, bf16[18,16,128]{2,1,0:T(8,128)(2,1)S(1)}, u32[]{:S(2)}, u32[]{:S(2)}) collective-permute-start(bf16[18,16,128]{2,1,0:T(8,128)(2,1)S(1)} %get-tuple-element.18), channel_id=1, source_target_pairs={{0,64},{1,17},{2,66},{3,19},{4,68},{5,21},{6,70},{7,23},{8,72},{9,... | collective-permute-start | bytes 221192 | tf_op jit(solution)/shard_map/ppermute | solution.py:274
  25.0 7.3 %collective-permute-start.6 = (bf16[18,16,128]{2,1,0:T(8,128)(2,1)S(1)}, bf16[18,16,128]{2,1,0:T(8,128)(2,1)S(1)}, u32[]{:S(2)}, u32[]{:S(2)}) collective-permute-start(bf16[18,16,128]{2,1,0:T(8,128)(2,1)S(1)} %get-tuple-element.19), channel_id=1, source_target_pairs={{0,192},{1,49},{2,194},{3,51},{4,196},{5,53},{6,198},{7,55},{8,200... | collective-permute-start | bytes 221192 | tf_op jit(solution)/shard_map/ppermute | solution.py:274
  27.1 5.2 %collective-permute-start.7 = (bf16[18,16,128]{2,1,0:T(8,128)(2,1)S(1)}, bf16[18,16,128]{2,1,0:T(8,128)(2,1)S(1)}, u32[]{:S(2)}, u32[]{:S(2)}) collective-permute-start(bf16[18,16,128]{2,1,0:T(8,128)(2,1)S(1)} %get-tuple-element.20), channel_id=1, source_target_pairs={{0,128},{1,33},{2,130},{3,35},{4,132},{5,37},{6,134},{7,39},{8,136... | collective-permute-start | bytes 221192 | tf_op jit(solution)/shard_map/ppermute | solution.py:274
  28.0 12.7 %collective-permute-start.12 = (bf16[4,16,768]{2,1,0:T(8,128)(2,1)S(1)}, bf16[4,16,768]{2,1,0:T(8,128)(2,1)S(1)}, u32[]{:S(2)}, u32[]{:S(2)}) collective-permute-start(bf16[4,16,768]{2,1,0:T(8,128)(2,1)S(1)} %pad_maximum_fusion.1), channel_id=1, source_target_pairs={{0,64},{1,17},{2,66},{3,19},{4,68},{5,21},{6,70},{7,23},{8,72},{9,... | collective-permute-start | bytes 294920 | tf_op jit(solution)/shard_map/ppermute | solution.py:269
  28.6 12.1 %collective-permute-start.13 = (bf16[4,16,768]{2,1,0:T(8,128)(2,1)S(1)}, bf16[4,16,768]{2,1,0:T(8,128)(2,1)S(1)}, u32[]{:S(2)}, u32[]{:S(2)}) collective-permute-start(bf16[4,16,768]{2,1,0:T(8,128)(2,1)S(1)} %pad_maximum_fusion.1), channel_id=1, source_target_pairs={{0,128},{1,33},{2,130},{3,35},{4,132},{5,37},{6,134},{7,39},{8,136... | collective-permute-start | bytes 294920 | tf_op jit(solution)/shard_map/ppermute | solution.py:269
  30.5 10.3 %collective-permute-start.14 = (bf16[4,16,768]{2,1,0:T(8,128)(2,1)S(1)}, bf16[4,16,768]{2,1,0:T(8,128)(2,1)S(1)}, u32[]{:S(2)}, u32[]{:S(2)}) collective-permute-start(bf16[4,16,768]{2,1,0:T(8,128)(2,1)S(1)} %pad_maximum_fusion.1), channel_id=1, source_target_pairs={{0,192},{1,49},{2,194},{3,51},{4,196},{5,53},{6,198},{7,55},{8,200... | collective-permute-start | bytes 294920 | tf_op jit(solution)/shard_map/ppermute | solution.py:269
  32.9 15.4 %all-to-all-start = ((bf16[8,3,16,128]{3,2,1,0:T(8,128)(2,1)}), bf16[8,3,16,128]{3,2,1,0:T(8,128)(2,1)S(1)}, u32[]{:S(2)}, u32[]{:S(2)}) async-start(bf16[8,3,16,128]{3,2,1,0:T(8,128)(2,1)} %route_kernel.1), calls=%async_computation | async-start | bytes 196608 | tf_op jit(solution)/shard_map/all_to_all | solution.py:299
  40.8 25.1 %collective-permute-start.15 = (bf16[4,4,16,768]{3,2,1,0:T(8,128)(2,1)S(1)}, bf16[4,4,16,768]{3,2,1,0:T(8,128)(2,1)S(1)}, u32[]{:S(2)}, u32[]{:S(2)}) collective-permute-start(bf16[4,4,16,768]{3,2,1,0:T(8,128)(2,1)S(1)} %pad_maximum_fusion.known_ref), channel_id=1, source_target_pairs={{0,1},{1,0},{2,3},{3,2},{4,5},{5,4},{6,7},{7,6},{8,9},{9,8},{10,11... | collective-permute-start | bytes 1179656 | tf_op jit(solution)/shard_map/ppermute | solution.py:298
  59.7 7.3 %collective-permute-start.8 = (bf16[16,16,384]{2,1,0:T(8,128)(2,1)S(1)}, bf16[16,16,384]{2,1,0:T(8,128)(2,1)S(1)}, u32[]{:S(2)}, u32[]{:S(2)}) collective-permute-start(bf16[16,16,384]{2,1,0:T(8,128)(2,1)S(1)} %all_to_all.10.own_ref), channel_id=1, source_target_pairs={{0,1},{1,0},{2,3},{3,2},{4,5},{5,4},{6,7},{7,6},{8,9},{9,8},{10,11... | collective-permute-start | bytes 589832 | tf_op jit(solution)/shard_map/ppermute | solution.py:313

commit v11 on v10

--- a/solution.py
+++ b/solution.py
@@ -271,7 +271,7 @@
 
 
 def scatter_stage(pieces, stage):
-    got = [lax.ppermute(pieces[d], AXES, plane_steps(d, stage)) for d in ORDER]
+    got = [lax.ppermute(pieces[d], AXES, plane_steps(d, stage)) for d in (2, 1, 3)]
     return [pieces[0], *got]
 
 

time: 69.8 us -> 70.7 us (1.013)
  blocking collectives: 11.1 us -> 12.7 us
    ppermute x6, starting transfers between devices: 7.41 us -> 5 us  [gather_stage(): got = [lax.ppermute(value, AXES, plane_steps(d, stage)) for d in ORDER]]
    ppermute x6, starting transfers between devices: 6.35 us -> 8.11 us  [scatter_stage(): lax.ppermute(pieces[d], AXES, plane_steps(d, stage))]
    all_to_all x1, blocking collectives: 11.1 us -> 12.7 us  [per_device(): lax.all_to_all(jnp.broadcast_to(packed[None], (PLANE, *packed.shape)), 'l...]
  transfers between devices with their start and end apart: 17 -> 17, of which waited for: 4 -> 5; matrix products, arithmetic and copies ran while one was open for 0% -> 0% of each run, Pallas kernels for 1% -> 1%
where the time goes in v11:
time: 70.7 us; the launch traced here: 70.4 us
  starting transfers between devices  33.5 us (47%)
  blocking collectives  12.7 us (18%)
  waiting for transfers between devices  12.1 us (17%)
  Pallas kernels  5.96 us (8%)
  matrix products  4.89 us (7%)
  between operations  0.97 us (1%)
    all_to_all x1, blocking collectives, per_device(): lax.all_to_all(jnp.broadcast_to(packed[None], (PLANE, *packed.shape)), 'l...  12.7 us
    ppermute x6, starting transfers between devices, scatter_stage(): lax.ppermute(pieces[d], AXES, plane_steps(d, stage))  8.11 us
    all_to_all x1, starting transfers between devices, per_device(): got = lax.all_to_all(routed, 'sep', split_axis=0, concat_axis=0, tiled=True)  8.04 us
    ppermute x1, starting transfers between devices, per_device(): theirs = lax.ppermute(mine, 'mode', SWAP)  5.91 us
    ppermute x6, starting transfers between devices, gather_stage(): got = [lax.ppermute(value, AXES, plane_steps(d, stage)) for d in ORDER]  5 us
    dot_general x1, matrix products, per_device(): jnp.einsum('ldw,ldm->lwm', coupling, modes, preferred_element_type=jnp.fl...  4.89 us
    all_to_all x1, waiting for transfers between devices, per_device(): got = lax.all_to_all(routed, 'sep', split_axis=0, concat_axis=0, tiled=True)  4.55 us
    ppermute x6, waiting for transfers between devices, scatter_stage(): lax.ppermute(pieces[d], AXES, plane_steps(d, stage))  4.39 us
  transfers between devices with their start and end apart: 17, of which 5 were waited for; matrix products, arithmetic and copies ran while one was open for 0% of the time, Pallas kernels for 1%

profile of v11, /device:TPU:1, one launch (start us, length us, event | category | flops | bytes accessed | tf_op | source)
XLA Modules:
  0.0 70.4 jit_solution(1254565879249616323)
XLA Ops:
  0.7 4.9 %convolution_convert_fusion.own_ref = bf16[8,256,256]{2,1,0:T(8,128)(2,1)S(1)} fusion(bf16[8,1024,256]{2,1,0:T(8,128)(2,1)} %param.9, bf16[8,1024,256]{2,1,0:T(8,128)(2,1)} %param.8), kind=kOutput, calls=%fused_computation | convolution fusion | flops 1074266112 | bytes 9437184 | tf_op jit(solution)/shard_map/ldw,ldm->lwm/dot_general | solution.py:284
  5.6 0.0 copy-start
  5.6 3.3 %collective-permute-start = (bf16[8,256,256]{2,1,0:T(8,128)(2,1)S(1)}, bf16[8,256,256]{2,1,0:T(8,128)(2,1)S(1)}, u32[]{:S(2)}, u32[]{:S(2)}) collective-permute-start(bf16[8,256,256]{2,1,0:T(8,128)(2,1)S(1)} %convolution_convert_fusion.own_ref), channel_id=1, source_target_pairs={{0,1},{1,0},{2,3},{3,2},{4,5},{5,4},{6,7},{7,6},{8,9},{9,8},{10,11... | collective-permute-start | bytes 3145736 | tf_op jit(solution)/shard_map/ppermute | solution.py:287
  8.9 0.1 collective-permute-start.1
  9.0 0.1 pad_add_fusion.place_ref
  9.1 2.1 %collective-permute-done.1.other_eigen_ref = f32[8,128]{1,0:T(8,128)S(1)} collective-permute-done((f32[8,128]{1,0:T(8,128)S(1)}, f32[8,128]{1,0:T(8,128)S(1)}, u32[]{:S(2)}, u32[]{:S(2)}) %collective-permute-start.1) | collective-permute-done | bytes 4128 | tf_op jit(solution)/shard_map/ppermute | solution.py:283
  11.2 2.7 %gram.1 = (bf16[4,18,16,128]{3,2,1,0:T(8,128)(2,1)S(1)}, bf16[4,18,16,128]{3,2,1,0:T(8,128)(2,1)S(1)}, bf16[4,18,16,128]{3,2,1,0:T(8,128)(2,1)S(1)}, bf16[4,18,16,128]{3,2,1,0:T(8,128)(2,1)S(1)}) custom-call(s32[8]{0:T(128)S(1)} %bitcast.30, s32[8]{0:T(128)S(1)} %copy-done.3, s32[3]{0:T(128)S(1)} %pad_add_fusion.place_ref, ...), custom_call_target="tpu_custom_call" | custom-call | tf_op jit(solution)/shard_map/gram/pallas_call | solution.py:106
  13.9 1.3 %collective-permute-start.2 = (bf16[4,18,16,128]{3,2,1,0:T(8,128)(2,1)S(1)}, bf16[4,18,16,128]{3,2,1,0:T(8,128)(2,1)S(1)}, u32[]{:S(2)}, u32[]{:S(2)}) collective-permute-start(bf16[4,18,16,128]{3,2,1,0:T(8,128)(2,1)S(1)} %get-tuple-element.14), channel_id=1, source_target_pairs={{0,32},{1,129},{2,34},{3,131},{4,36},{5,133},{6,38},{7,135},{8,40}... | collective-permute-start | bytes 884744 | tf_op jit(solution)/shard_map/ppermute | solution.py:274
  15.2 0.4 collective-permute-start.3
  15.6 2.3 %collective-permute-start.4 = (bf16[4,18,16,128]{3,2,1,0:T(8,128)(2,1)S(1)}, bf16[4,18,16,128]{3,2,1,0:T(8,128)(2,1)S(1)}, u32[]{:S(2)}, u32[]{:S(2)}) collective-permute-start(bf16[4,18,16,128]{3,2,1,0:T(8,128)(2,1)S(1)} %get-tuple-element.16), channel_id=1, source_target_pairs={{0,48},{1,193},{2,50},{3,195},{4,52},{5,197},{6,54},{7,199},{8,56}... | collective-permute-start | bytes 884744 | tf_op jit(solution)/shard_map/ppermute | solution.py:274
  17.8 0.1 collective-permute-start.9
  17.9 1.2 %collective-permute-start.10 = (bf16[16,768]{1,0:T(8,128)(2,1)S(1)}, bf16[16,768]{1,0:T(8,128)(2,1)S(1)}, u32[]{:S(2)}, u32[]{:S(2)}) collective-permute-start(bf16[16,768]{1,0:T(8,128)(2,1)S(1)} %pad_maximum_fusion.2), channel_id=1, source_target_pairs={{0,32},{1,129},{2,34},{3,131},{4,36},{5,133},{6,38},{7,135},{8,40}... | collective-permute-start | bytes 73736 | tf_op jit(solution)/shard_map/ppermute | solution.py:269
  19.1 2.2 %collective-permute-done.2.refs_1_ = bf16[4,18,16,128]{3,2,1,0:T(8,128)(2,1)S(1)} collective-permute-done((bf16[4,18,16,128]{3,2,1,0:T(8,128)(2,1)S(1)}, bf16[4,18,16,128]{3,2,1,0:T(8,128)(2,1)S(1)}, u32[]{:S(2)}, u32[]{:S(2)}) %collective-permute-start.2) | collective-permute-done | bytes 294944 | tf_op jit(solution)/shard_map/ppermute | solution.py:274
  21.4 1.0 %collective-permute-start.11 = (bf16[16,768]{1,0:T(8,128)(2,1)S(1)}, bf16[16,768]{1,0:T(8,128)(2,1)S(1)}, u32[]{:S(2)}, u32[]{:S(2)}) collective-permute-start(bf16[16,768]{1,0:T(8,128)(2,1)S(1)} %pad_maximum_fusion.2), channel_id=1, source_target_pairs={{0,48},{1,193},{2,50},{3,195},{4,52},{5,197},{6,54},{7,199},{8,56}... | collective-permute-start | bytes 73736 | tf_op jit(solution)/shard_map/ppermute | solution.py:269
  22.3 2.1 %collective-permute-done.3.refs_2_ = bf16[4,18,16,128]{3,2,1,0:T(8,128)(2,1)S(1)} collective-permute-done((bf16[4,18,16,128]{3,2,1,0:T(8,128)(2,1)S(1)}, bf16[4,18,16,128]{3,2,1,0:T(8,128)(2,1)S(1)}, u32[]{:S(2)}, u32[]{:S(2)}) %collective-permute-start.3) | collective-permute-done | bytes 294944 | tf_op jit(solution)/shard_map/ppermute | solution.py:274
  24.5 0.1 split_kernel.1
  24.6 1.5 %collective-permute-start.5 = (bf16[18,16,128]{2,1,0:T(8,128)(2,1)S(1)}, bf16[18,16,128]{2,1,0:T(8,128)(2,1)S(1)}, u32[]{:S(2)}, u32[]{:S(2)}) collective-permute-start(bf16[18,16,128]{2,1,0:T(8,128)(2,1)S(1)} %get-tuple-element.18), channel_id=1, source_target_pairs={{0,128},{1,33},{2,130},{3,35},{4,132},{5,37},{6,134},{7,39},{8,136... | collective-permute-start | bytes 221192 | tf_op jit(solution)/shard_map/ppermute | solution.py:274
  26.1 0.3 collective-permute-start.6
  26.4 2.4 %collective-permute-start.7 = (bf16[18,16,128]{2,1,0:T(8,128)(2,1)S(1)}, bf16[18,16,128]{2,1,0:T(8,128)(2,1)S(1)}, u32[]{:S(2)}, u32[]{:S(2)}) collective-permute-start(bf16[18,16,128]{2,1,0:T(8,128)(2,1)S(1)} %get-tuple-element.20), channel_id=1, source_target_pairs={{0,192},{1,49},{2,194},{3,51},{4,196},{5,53},{6,198},{7,55},{8,200... | collective-permute-start | bytes 221192 | tf_op jit(solution)/shard_map/ppermute | solution.py:274
  28.8 0.1 collective-permute-start.12
  28.9 1.2 %collective-permute-start.13 = (bf16[4,16,768]{2,1,0:T(8,128)(2,1)S(1)}, bf16[4,16,768]{2,1,0:T(8,128)(2,1)S(1)}, u32[]{:S(2)}, u32[]{:S(2)}) collective-permute-start(bf16[4,16,768]{2,1,0:T(8,128)(2,1)S(1)} %pad_maximum_fusion.1), channel_id=1, source_target_pairs={{0,128},{1,33},{2,130},{3,35},{4,132},{5,37},{6,134},{7,39},{8,136... | collective-permute-start | bytes 294920 | tf_op jit(solution)/shard_map/ppermute | solution.py:269
  30.1 1.5 %collective-permute-start.14 = (bf16[4,16,768]{2,1,0:T(8,128)(2,1)S(1)}, bf16[4,16,768]{2,1,0:T(8,128)(2,1)S(1)}, u32[]{:S(2)}, u32[]{:S(2)}) collective-permute-start(bf16[4,16,768]{2,1,0:T(8,128)(2,1)S(1)} %pad_maximum_fusion.1), channel_id=1, source_target_pairs={{0,192},{1,49},{2,194},{3,51},{4,196},{5,53},{6,198},{7,55},{8,200... | collective-permute-start | bytes 294920 | tf_op jit(solution)/shard_map/ppermute | solution.py:269
  31.6 0.7 route_kernel.1
  32.3 8.0 %all-to-all-start = ((bf16[8,3,16,128]{3,2,1,0:T(8,128)(2,1)}), bf16[8,3,16,128]{3,2,1,0:T(8,128)(2,1)S(1)}, u32[]{:S(2)}, u32[]{:S(2)}) async-start(bf16[8,3,16,128]{3,2,1,0:T(8,128)(2,1)} %route_kernel.1), calls=%async_computation | async-start | bytes 196608 | tf_op jit(solution)/shard_map/all_to_all | solution.py:299
  40.3 0.1 pad_maximum_fusion.known_ref
  40.4 3.0 %collective-permute-start.15 = (bf16[4,4,16,768]{3,2,1,0:T(8,128)(2,1)S(1)}, bf16[4,4,16,768]{3,2,1,0:T(8,128)(2,1)S(1)}, u32[]{:S(2)}, u32[]{:S(2)}) collective-permute-start(bf16[4,4,16,768]{3,2,1,0:T(8,128)(2,1)S(1)} %pad_maximum_fusion.known_ref), channel_id=1, source_target_pairs={{0,1},{1,0},{2,3},{3,2},{4,5},{5,4},{6,7},{7,6},{8,9},{9,8},{10,11... | collective-permute-start | bytes 1179656 | tf_op jit(solution)/shard_map/ppermute | solution.py:298
  43.4 4.6 %all-to-all-done = bf16[8,3,16,128]{3,2,1,0:T(8,128)(2,1)S(1)} async-done(((bf16[8,3,16,128]{3,2,1,0:T(8,128)(2,1)}), bf16[8,3,16,128]{3,2,1,0:T(8,128)(2,1)S(1)}, u32[]{:S(2)}, u32[]{:S(2)}) %all-to-all-start) | async-done | bytes 98336 | tf_op jit(solution)/shard_map/all_to_all | solution.py:299
  48.1 0.1 fusion.1
  48.2 12.7 %all_to_all.10.own_ref = bf16[16,16,384]{2,1,0:T(8,128)(2,1)S(1)} all-to-all(bf16[16,16,384]{2,1,0:T(8,128)(2,1)S(1)} %broadcast_in_dim.2), channel_id=1, replica_groups=mesh['leaf'=16,'sep'=8,'mode'=2] {'leaf'}, dimensions={0} | all-to-all | bytes 393216 | tf_op jit(solution)/shard_map/all_to_all | solution.py:306
  60.9 5.9 %collective-permute-start.8 = (bf16[16,16,384]{2,1,0:T(8,128)(2,1)S(1)}, bf16[16,16,384]{2,1,0:T(8,128)(2,1)S(1)}, u32[]{:S(2)}, u32[]{:S(2)}) collective-permute-start(bf16[16,16,384]{2,1,0:T(8,128)(2,1)S(1)} %all_to_all.10.own_ref), channel_id=1, source_target_pairs={{0,1},{1,0},{2,3},{3,2},{4,5},{5,4},{6,7},{7,6},{8,9},{9,8},{10,11... | collective-permute-start | bytes 589832 | tf_op jit(solution)/shard_map/ppermute | solution.py:313
  66.8 1.1 %collective-permute-done.8.other_ref = bf16[16,16,384]{2,1,0:T(8,128)(2,1)S(1)} collective-permute-done((bf16[16,16,384]{2,1,0:T(8,128)(2,1)S(1)}, bf16[16,16,384]{2,1,0:T(8,128)(2,1)S(1)}, u32[]{:S(2)}, u32[]{:S(2)}) %collective-permute-start.8) | collective-permute-done | bytes 196640 | tf_op jit(solution)/shard_map/ppermute | solution.py:313
  67.8 2.4 %iterate.1 = (bf16[1,16,256]{2,1,0:T(8,128)(2,1)}, f32[1,2,256]{2,1,0:T(2,128)}) custom-call(bf16[16,16,384]{2,1,0:T(8,128)(2,1)S(1)} %all_to_all.10.own_ref, bf16[16,16,384]{2,1,0:T(8,128)(2,1)S(1)} %collective-permute-done.8.other_ref, bf16[4,4,16,768]{3,2,1,0:T(8,128)(2,1)S(1)} %pad_maximum_fusion.known_ref, ...), custom_call_target="tpu_custom_call" | custom-call | tf_op jit(solution)/shard_map/iterate/pallas_call | solution.py:222
  (33 shorter events, 0.1 us)
Async XLA Ops:
  0.6 8.2 %copy-start.1 = (f32[8,128]{1,0:T(8,128)S(1)}, f32[8,128]{1,0:T(8,128)}, u32[]{:S(2)}) copy-start(f32[8,128]{1,0:T(8,128)} %eigen_ref.1) | copy-start | bytes 12292
  0.6 10.5 %copy-start.2 = (s32[8,1]{0,1:T(1,128)S(1)}, s32[8,1]{0,1:T(1,128)}, u32[]{:S(2)}) copy-start(s32[8,1]{0,1:T(1,128)} %param.11) | copy-start | bytes 100
  0.7 10.5 %copy-start.3 = (s32[8]{0:T(128)S(1)}, s32[8]{0:T(128)}, u32[]{:S(2)}) copy-start(s32[8]{0:T(128)} %offset_ref.1) | copy-start | bytes 100
  0.7 17.2 %copy-start.5 = (bf16[1,16,256]{2,1,0:T(8,128)(2,1)S(1)}, bf16[1,16,256]{2,1,0:T(8,128)(2,1)}, u32[]{:S(2)}) copy-start(bf16[1,16,256]{2,1,0:T(8,128)(2,1)} %param.14) | copy-start | bytes 24580
  0.7 17.2 %copy-start.4 = (bf16[1,512,16]{1,2,0:T(8,128)(2,1)S(1)}, bf16[1,512,16]{1,2,0:T(8,128)(2,1)}, u32[]{:S(2)}) copy-start(bf16[1,512,16]{1,2,0:T(8,128)(2,1)} %param.13) | copy-start | bytes 49156
  5.6 62.3 %copy-start = (bf16[1,2,256,256]{3,2,1,0:T(8,128)(2,1)S(1)}, bf16[1,2,256,256]{3,2,1,0:T(8,128)(2,1)}, u32[]{:S(2)}) copy-start(bf16[1,2,256,256]{3,2,1,0:T(8,128)(2,1)} %param.15) | copy-start | bytes 786436
  5.6 5.6 %collective-permute-start = (bf16[8,256,256]{2,1,0:T(8,128)(2,1)S(1)}, bf16[8,256,256]{2,1,0:T(8,128)(2,1)S(1)}, u32[]{:S(2)}, u32[]{:S(2)}) collective-permute-start(bf16[8,256,256]{2,1,0:T(8,128)(2,1)S(1)} %convolution_convert_fusion.own_ref), channel_id=1, source_target_pairs={{0,1},{1,0},{2,3},{3,2},{4,5},{5,4},{6,7},{7,6},{8,9},{9,8},{10,11... | collective-permute-start | bytes 3145736 | tf_op jit(solution)/shard_map/ppermute | solution.py:287
  8.9 2.3 %collective-permute-start.1 = (f32[8,128]{1,0:T(8,128)S(1)}, f32[8,128]{1,0:T(8,128)S(1)}, u32[]{:S(2)}, u32[]{:S(2)}) collective-permute-start(f32[8,128]{1,0:T(8,128)S(1)} %copy-done.1), channel_id=1, source_target_pairs={{0,1},{1,0},{2,3},{3,2},{4,5},{5,4},{6,7},{7,6},{8,9},{9,8},{10,11... | collective-permute-start | bytes 12296 | tf_op jit(solution)/shard_map/ppermute | solution.py:283
  13.9 7.5 %collective-permute-start.2 = (bf16[4,18,16,128]{3,2,1,0:T(8,128)(2,1)S(1)}, bf16[4,18,16,128]{3,2,1,0:T(8,128)(2,1)S(1)}, u32[]{:S(2)}, u32[]{:S(2)}) collective-permute-start(bf16[4,18,16,128]{3,2,1,0:T(8,128)(2,1)S(1)} %get-tuple-element.14), channel_id=1, source_target_pairs={{0,32},{1,129},{2,34},{3,131},{4,36},{5,133},{6,38},{7,135},{8,40}... | collective-permute-start | bytes 884744 | tf_op jit(solution)/shard_map/ppermute | solution.py:274
  15.2 9.3 %collective-permute-start.3 = (bf16[4,18,16,128]{3,2,1,0:T(8,128)(2,1)S(1)}, bf16[4,18,16,128]{3,2,1,0:T(8,128)(2,1)S(1)}, u32[]{:S(2)}, u32[]{:S(2)}) collective-permute-start(bf16[4,18,16,128]{3,2,1,0:T(8,128)(2,1)S(1)} %get-tuple-element.15), channel_id=1, source_target_pairs={{0,16},{1,65},{2,18},{3,67},{4,20},{5,69},{6,22},{7,71},{8,24},{9,... | collective-permute-start | bytes 884744 | tf_op jit(solution)/shard_map/ppermute | solution.py:274
  15.6 8.9 %collective-permute-start.4 = (bf16[4,18,16,128]{3,2,1,0:T(8,128)(2,1)S(1)}, bf16[4,18,16,128]{3,2,1,0:T(8,128)(2,1)S(1)}, u32[]{:S(2)}, u32[]{:S(2)}) collective-permute-start(bf16[4,18,16,128]{3,2,1,0:T(8,128)(2,1)S(1)} %get-tuple-element.16), channel_id=1, source_target_pairs={{0,48},{1,193},{2,50},{3,195},{4,52},{5,197},{6,54},{7,199},{8,56}... | collective-permute-start | bytes 884744 | tf_op jit(solution)/shard_map/ppermute | solution.py:274
  17.8 8.6 %collective-permute-start.9 = (bf16[16,768]{1,0:T(8,128)(2,1)S(1)}, bf16[16,768]{1,0:T(8,128)(2,1)S(1)}, u32[]{:S(2)}, u32[]{:S(2)}) collective-permute-start(bf16[16,768]{1,0:T(8,128)(2,1)S(1)} %pad_maximum_fusion.2), channel_id=1, source_target_pairs={{0,16},{1,65},{2,18},{3,67},{4,20},{5,69},{6,22},{7,71},{8,24},{9,... | collective-permute-start | bytes 73736 | tf_op jit(solution)/shard_map/ppermute | solution.py:269
  17.9 10.8 %collective-permute-start.10 = (bf16[16,768]{1,0:T(8,128)(2,1)S(1)}, bf16[16,768]{1,0:T(8,128)(2,1)S(1)}, u32[]{:S(2)}, u32[]{:S(2)}) collective-permute-start(bf16[16,768]{1,0:T(8,128)(2,1)S(1)} %pad_maximum_fusion.2), channel_id=1, source_target_pairs={{0,32},{1,129},{2,34},{3,131},{4,36},{5,133},{6,38},{7,135},{8,40}... | collective-permute-start | bytes 73736 | tf_op jit(solution)/shard_map/ppermute | solution.py:269
  21.4 7.4 %collective-permute-start.11 = (bf16[16,768]{1,0:T(8,128)(2,1)S(1)}, bf16[16,768]{1,0:T(8,128)(2,1)S(1)}, u32[]{:S(2)}, u32[]{:S(2)}) collective-permute-start(bf16[16,768]{1,0:T(8,128)(2,1)S(1)} %pad_maximum_fusion.2), channel_id=1, source_target_pairs={{0,48},{1,193},{2,50},{3,195},{4,52},{5,197},{6,54},{7,199},{8,56}... | collective-permute-start | bytes 73736 | tf_op jit(solution)/shard_map/ppermute | solution.py:269
  24.6 5.5 %collective-permute-start.5 = (bf16[18,16,128]{2,1,0:T(8,128)(2,1)S(1)}, bf16[18,16,128]{2,1,0:T(8,128)(2,1)S(1)}, u32[]{:S(2)}, u32[]{:S(2)}) collective-permute-start(bf16[18,16,128]{2,1,0:T(8,128)(2,1)S(1)} %get-tuple-element.18), channel_id=1, source_target_pairs={{0,128},{1,33},{2,130},{3,35},{4,132},{5,37},{6,134},{7,39},{8,136... | collective-permute-start | bytes 221192 | tf_op jit(solution)/shard_map/ppermute | solution.py:274
  26.1 5.5 %collective-permute-start.6 = (bf16[18,16,128]{2,1,0:T(8,128)(2,1)S(1)}, bf16[18,16,128]{2,1,0:T(8,128)(2,1)S(1)}, u32[]{:S(2)}, u32[]{:S(2)}) collective-permute-start(bf16[18,16,128]{2,1,0:T(8,128)(2,1)S(1)} %get-tuple-element.19), channel_id=1, source_target_pairs={{0,64},{1,17},{2,66},{3,19},{4,68},{5,21},{6,70},{7,23},{8,72},{9,... | collective-permute-start | bytes 221192 | tf_op jit(solution)/shard_map/ppermute | solution.py:274
  26.4 5.2 %collective-permute-start.7 = (bf16[18,16,128]{2,1,0:T(8,128)(2,1)S(1)}, bf16[18,16,128]{2,1,0:T(8,128)(2,1)S(1)}, u32[]{:S(2)}, u32[]{:S(2)}) collective-permute-start(bf16[18,16,128]{2,1,0:T(8,128)(2,1)S(1)} %get-tuple-element.20), channel_id=1, source_target_pairs={{0,192},{1,49},{2,194},{3,51},{4,196},{5,53},{6,198},{7,55},{8,200... | collective-permute-start | bytes 221192 | tf_op jit(solution)/shard_map/ppermute | solution.py:274
  28.8 11.5 %collective-permute-start.12 = (bf16[4,16,768]{2,1,0:T(8,128)(2,1)S(1)}, bf16[4,16,768]{2,1,0:T(8,128)(2,1)S(1)}, u32[]{:S(2)}, u32[]{:S(2)}) collective-permute-start(bf16[4,16,768]{2,1,0:T(8,128)(2,1)S(1)} %pad_maximum_fusion.1), channel_id=1, source_target_pairs={{0,64},{1,17},{2,66},{3,19},{4,68},{5,21},{6,70},{7,23},{8,72},{9,... | collective-permute-start | bytes 294920 | tf_op jit(solution)/shard_map/ppermute | solution.py:269
  28.9 11.4 %collective-permute-start.13 = (bf16[4,16,768]{2,1,0:T(8,128)(2,1)S(1)}, bf16[4,16,768]{2,1,0:T(8,128)(2,1)S(1)}, u32[]{:S(2)}, u32[]{:S(2)}) collective-permute-start(bf16[4,16,768]{2,1,0:T(8,128)(2,1)S(1)} %pad_maximum_fusion.1), channel_id=1, source_target_pairs={{0,128},{1,33},{2,130},{3,35},{4,132},{5,37},{6,134},{7,39},{8,136... | collective-permute-start | bytes 294920 | tf_op jit(solution)/shard_map/ppermute | solution.py:269
  30.1 10.2 %collective-permute-start.14 = (bf16[4,16,768]{2,1,0:T(8,128)(2,1)S(1)}, bf16[4,16,768]{2,1,0:T(8,128)(2,1)S(1)}, u32[]{:S(2)}, u32[]{:S(2)}) collective-permute-start(bf16[4,16,768]{2,1,0:T(8,128)(2,1)S(1)} %pad_maximum_fusion.1), channel_id=1, source_target_pairs={{0,192},{1,49},{2,194},{3,51},{4,196},{5,53},{6,198},{7,55},{8,200... | collective-permute-start | bytes 294920 | tf_op jit(solution)/shard_map/ppermute | solution.py:269
  32.3 15.7 %all-to-all-start = ((bf16[8,3,16,128]{3,2,1,0:T(8,128)(2,1)}), bf16[8,3,16,128]{3,2,1,0:T(8,128)(2,1)S(1)}, u32[]{:S(2)}, u32[]{:S(2)}) async-start(bf16[8,3,16,128]{3,2,1,0:T(8,128)(2,1)} %route_kernel.1), calls=%async_computation | async-start | bytes 196608 | tf_op jit(solution)/shard_map/all_to_all | solution.py:299
  40.4 26.4 %collective-permute-start.15 = (bf16[4,4,16,768]{3,2,1,0:T(8,128)(2,1)S(1)}, bf16[4,4,16,768]{3,2,1,0:T(8,128)(2,1)S(1)}, u32[]{:S(2)}, u32[]{:S(2)}) collective-permute-start(bf16[4,4,16,768]{3,2,1,0:T(8,128)(2,1)S(1)} %pad_maximum_fusion.known_ref), channel_id=1, source_target_pairs={{0,1},{1,0},{2,3},{3,2},{4,5},{5,4},{6,7},{7,6},{8,9},{9,8},{10,11... | collective-permute-start | bytes 1179656 | tf_op jit(solution)/shard_map/ppermute | solution.py:298
  60.9 7.0 %collective-permute-start.8 = (bf16[16,16,384]{2,1,0:T(8,128)(2,1)S(1)}, bf16[16,16,384]{2,1,0:T(8,128)(2,1)S(1)}, u32[]{:S(2)}, u32[]{:S(2)}) collective-permute-start(bf16[16,16,384]{2,1,0:T(8,128)(2,1)S(1)} %all_to_all.10.own_ref), channel_id=1, source_target_pairs={{0,1},{1,0},{2,3},{3,2},{4,5},{5,4},{6,7},{7,6},{8,9},{9,8},{10,11... | collective-permute-start | bytes 589832 | tf_op jit(solution)/shard_map/ppermute | solution.py:313
